TPU v7x, 32 devices: a whole 2x2x4 slice. The times are simulated.
32 devices in a mesh: rep: 4 (over z), fsdp: 8 (over y, x, core).
Axes of the slice: x: 2, y: 2, z: 4, core: 2. Of those that a mesh axis runs over, the one named last changes fastest.
Arguments:
- activations: bfloat16 [4, 16384, 4096], P('rep', 'fsdp'), may hold values from -6 to 6
- cotangent: bfloat16 [4, 16384, 1024], P('rep', 'fsdp'), may hold values from -0.046875 to 0.046875
- momentum: float32 [4, 4096, 1024], P('rep', 'fsdp'), may hold values from -6 to 6
Outputs:
- momentum_next: float32 [4, 4096, 1024], P('rep', 'fsdp')
- update: float32 [4096, 1024], P('fsdp')
All inputs are finite; a program needn't handle non-finite values.
Results may differ from a plain program's by a relative error of at most 0.0021.
Values sent between devices are 32-bit elements; how exact they have to be, the bound alone decides.
No kernel may reach another device: no remote copies, remote signals or barrier semaphores. Data moves between devices by JAX's collectives and lax.ppermute only.
A program may use at most 128 MiB of HBM per device.

v0:
```python
import jax
import jax.numpy as jnp
from jax import lax
from jax.sharding import PartitionSpec as P

CH = 64
BAND = 16


momentum_decay = 0.9


def basis_rows(size, keep):
    freq = jnp.arange(keep, dtype=jnp.float32)[:, None]
    point = jnp.arange(size, dtype=jnp.float32)[None, :]
    waves = jnp.cos(jnp.pi * (2.0 * point + 1.0) * freq / (2.0 * size))
    scales = jnp.where(freq == 0.0, jnp.sqrt(1.0 / size), jnp.sqrt(2.0 / size))
    return waves * scales


def bands_of(field, basis):
    rows, width = field.shape
    blocks = field.reshape(rows // CH, CH, width // CH, CH)
    return jnp.einsum("kn,anbm,lm->akbl", basis, blocks, basis, precision=lax.Precision.HIGHEST)


def term_maker(normed, part):
    return lax.dot_general(
        normed, part, (((0,), (0,)), ((), ())), preferred_element_type=jnp.float32
    )


def settle(grad, field, basis):
    accumulated = momentum_decay * field + grad
    bands = bands_of(accumulated, basis)
    count, _, wide, _ = bands.shape
    blocks = jnp.einsum("kn,akbl,lm->anbm", basis, bands, basis, precision=lax.Precision.HIGHEST)
    return (accumulated - blocks.reshape(count * CH, wide * CH), bands)


def body(activations, cotangent, momentum):
    values = activations[0].astype(jnp.float32)
    stat = jnp.mean(values * values, axis=-1, keepdims=True)
    normed = (values * lax.rsqrt(stat + 1e-05)).astype(jnp.bfloat16)
    targets = cotangent[0]
    field = momentum[0]
    basis = basis_rows(CH, BAND)
    grad = lax.psum_scatter(term_maker(normed, targets), "fsdp", scatter_dimension=0, tiled=True)
    cleared, bands = settle(grad, field, basis)
    count, _, wide, _ = bands.shape
    summed = lax.psum(bands, "rep")
    blocks = jnp.einsum("kn,akbl,lm->anbm", basis, summed, basis, precision=lax.Precision.HIGHEST)
    update = blocks.reshape(count * CH, wide * CH)
    groups = lax.axis_size("rep")
    return (cleared[None], update / groups)


def solution(mesh):
    return jax.shard_map(
        body,
        mesh=mesh,
        in_specs=(P("rep", "fsdp", None), P("rep", "fsdp", None), P("rep", "fsdp", None)),
        out_specs=(P("rep", "fsdp", None), P("fsdp", None)),
        check_vma=False,
    )
```

profile of v0, /device:TPU:0, one launch (start us, length us, event | category | flops | bytes accessed | tf_op | source)
XLA Modules:
  0.0 262.0 jit_solution(10249392141727543123)
XLA Ops:
  7.2 0.0 reduce-scatter.2.cloned.1.call-start
  7.2 0.0 copy-start
  7.2 7.6 %fusion = f32[2048]{0:T(1024)S(1)} fusion(bf16[1,2048,4096]{2,1,0:T(8,128)(2,1)} %param.3), kind=kLoop, calls=%fused_computation.2 | loop fusion | flops 25163776 | bytes 16785408 | tf_op jit(solution)/shard_map/reduce_sum | solution.py:43
  14.8 3.1 %copy-done = bf16[1,2048,4096]{2,1,0:T(8,128)(2,1)S(1)} copy-done((bf16[1,2048,4096]{2,1,0:T(8,128)(2,1)S(1)}, bf16[1,2048,4096]{2,1,0:T(8,128)(2,1)}, u32[]{:S(2)}) %copy-start) | copy-done | bytes 16777240
  17.9 23.4 %fusion.3 = f32[4096,1024]{1,0:T(8,128)} fusion(bf16[1,2048,4096]{2,1,0:T(8,128)(2,1)S(1)} %copy-done, f32[2048]{0:T(1024)S(1)} %add_rsqrt_fusion, bf16[1,2048,1024]{2,1,0:T(8,128)(2,1)} %param.4), kind=kOutput, calls=%fused_computation.5 | convolution fusion | flops 17205035008 | bytes 37756928 | tf_op jit(solution)/shard_map/dot_general | solution.py:28
  41.3 0.0 reduce-scatter.2.cloned.1.call-update
  41.3 119.0 %reduce-scatter.2.cloned.1.call-done = f32[512,1024]{1,0:T(8,128)} async-done(((f32[4096,1024]{1,0:T(8,128)}), f32[512,1024]{1,0:T(8,128)}) %reduce-scatter.2.cloned.1.call-update) | async-done | bytes 2097168 | tf_op jit(solution)/shard_map/reduce_scatter | solution.py:48
  160.3 2.7 %bitcast_add_fusion = f32[512,1024]{1,0:T(8,128)S(1)} fusion(f32[512,1024]{1,0:T(8,128)} %reduce-scatter.2.cloned.1.call-done, f32[1,512,1024]{2,1,0:T(8,128)} %param.5), kind=kLoop, calls=%fused_computation.12 | loop fusion | flops 1048576 | bytes 6291456 | tf_op jit(solution)/shard_map/add | solution.py:34
  163.0 2.5 reshape.49
  165.5 5.6 %fusion.7 = f32[8,16,64,16]{2,3,1,0:T(8,128)S(1)} fusion(f32[8,64,16,64]{3,2,1,0:T(8,128)} %reshape.49, f32[16]{0:T(128)S(1)} %compare_select_fusion, f32[64]{0:T(128)S(1)} %add_multiply_fusion), kind=kOutput, calls=%fused_computation.8 | convolution fusion | flops 100666368 | bytes 2621760 | tf_op jit(solution)/shard_map/kn,anbm,lm->akbl/dot_general | solution.py:24
  171.1 1.0 convolution_bitcast_fusion.1
  172.1 0.0 copy-start.1
  172.1 2.8 %fusion.13 = f32[8,16,16,64]{3,2,1,0:T(8,128)} fusion(f32[8,16,16,16]{3,1,2,0:T(8,128)S(1)} %convolution_bitcast_fusion.1, f32[16]{0:T(128)S(1)} %compare_select_fusion, f32[64]{0:T(128)S(1)} %add_multiply_fusion), kind=kOutput, calls=%fused_computation.19 | convolution fusion | flops 25168896 | bytes 655680 | tf_op jit(solution)/shard_map/kn,akbl,lm->anbm/dot_general | solution.py:37
  174.9 0.0 all-reduce.2.cloned.1.call-start
  174.9 9.3 %convolution_bitcast_fusion = f32[8,64,16,64]{3,1,2,0:T(8,128)} fusion(f32[8,16,16,64]{3,2,1,0:T(8,128)} %fusion.13, f32[16]{0:T(128)S(1)} %compare_select_fusion, f32[64]{0:T(128)S(1)} %add_multiply_fusion), kind=kOutput, calls=%fused_computation.11 | convolution fusion | flops 100666368 | bytes 2621760 | tf_op jit(solution)/shard_map/kn,akbl,lm->anbm/dot_general | solution.py:37
  184.2 0.0 copy-done.1
  184.2 0.0 all-reduce.2.cloned.1.call-update
  184.2 6.5 %copy.6 = f32[8,64,16,64]{3,2,1,0:T(8,128)} copy(f32[8,64,16,64]{3,1,2,0:T(8,128)} %convolution_bitcast_fusion) | data formatting | bytes 4194304 | tf_op jit(solution)/shard_map/kn,akbl,lm->anbm/transpose | solution.py:37
  190.8 4.8 %reshape.50 = f32[512,1024]{1,0:T(8,128)} reshape(f32[8,64,16,64]{3,2,1,0:T(8,128)} %copy.6) | data formatting | bytes 4194304 | tf_op jit(solution)/shard_map/reshape | solution.py:38
  195.6 3.3 %subtract_bitcast_fusion = f32[1,512,1024]{2,1,0:T(8,128)} fusion(f32[512,1024]{1,0:T(8,128)S(1)} %bitcast_add_fusion, f32[512,1024]{1,0:T(8,128)} %reshape.50), kind=kLoop, calls=%fused_computation.13 | loop fusion | flops 524288 | bytes 6291456 | tf_op jit(solution)/shard_map/broadcast_in_dim | solution.py:55
  198.9 37.4 %all-reduce.2.cloned.1.call-done = f32[8,16,16,16]{3,1,2,0:T(8,128)} async-done(((f32[8,16,16,16]{3,1,2,0:T(8,128)}), f32[8,16,16,16]{3,1,2,0:T(8,128)}) %all-reduce.2.cloned.1.call-update) | async-done | bytes 131088 | tf_op jit(solution)/shard_map/psum | solution.py:51
  236.3 3.0 %fusion.10 = f32[8,16,16,64]{3,2,1,0:T(8,128)S(1)} fusion(f32[8,16,16,16]{3,1,2,0:T(8,128)} %all-reduce.2.cloned.1.call-done, f32[16]{0:T(128)S(1)} %compare_select_fusion, f32[64]{0:T(128)S(1)} %add_multiply_fusion), kind=kOutput, calls=%fused_computation.16 | convolution fusion | flops 25168896 | bytes 655680 | tf_op jit(solution)/shard_map/kn,akbl,lm->anbm/dot_general | solution.py:52
  239.3 6.7 %multiply_bitcast_fusion = f32[8,64,16,64]{3,1,2,0:T(8,128)S(1)} fusion(f32[8,16,16,64]{3,2,1,0:T(8,128)S(1)} %fusion.10, f32[16]{0:T(128)S(1)} %compare_select_fusion, f32[64]{0:T(128)S(1)} %add_multiply_fusion), kind=kOutput, calls=%fused_computation.10 | convolution fusion | flops 101190656 | bytes 2621760 | tf_op jit(solution)/shard_map/kn,akbl,lm->anbm/dot_general | solution.py:52
  246.1 4.3 %copy.7 = f32[8,64,16,64]{3,2,1,0:T(8,128)} copy(f32[8,64,16,64]{3,1,2,0:T(8,128)S(1)} %multiply_bitcast_fusion) | data formatting | bytes 4194304 | tf_op jit(solution)/shard_map/div | solution.py:55
  250.4 4.8 %div.39 = f32[512,1024]{1,0:T(8,128)} reshape(f32[8,64,16,64]{3,2,1,0:T(8,128)} %copy.7) | data formatting | bytes 4194304 | tf_op jit(solution)/shard_map/div | solution.py:55
  (3 shorter events, 0.0 us)
Async XLA Ops:
  7.2 153.2 %reduce-scatter.2.cloned.1.call-start = ((), (), s32[]{:S(2)}) async-start(), calls=%async_computation.1 | async-start | bytes 18874368 | tf_op jit(solution)/shard_map/reduce_scatter | solution.py:48
  7.2 10.7 %copy-start = (bf16[1,2048,4096]{2,1,0:T(8,128)(2,1)S(1)}, bf16[1,2048,4096]{2,1,0:T(8,128)(2,1)}, u32[]{:S(2)}) copy-start(bf16[1,2048,4096]{2,1,0:T(8,128)(2,1)} %param.3) | copy-start | bytes 50331652
  172.1 12.1 %copy-start.1 = (f32[8,16,16,16]{3,1,2,0:T(8,128)}, f32[8,16,16,16]{3,1,2,0:T(8,128)S(1)}, u32[]{:S(2)}) copy-start(f32[8,16,16,16]{3,1,2,0:T(8,128)S(1)} %convolution_bitcast_fusion.1) | copy-start | bytes 393220
  174.9 61.4 %all-reduce.2.cloned.1.call-start = ((), (), s32[]{:S(2)}) async-start(), calls=%async_computation.2 | async-start | bytes 2097152 | tf_op jit(solution)/shard_map/psum | solution.py:51
Sparse Core Ops, SparseCore 0:
  41.4 118.8 reduce-scatter.1
  184.4 51.8 all-reduce.1
where the time goes:
time: 262 us
  waiting for transfers between devices  156 us (60%)
  matrix products  51.8 us (20%)
  local copies, waits for them, and re-layouts  26.1 us (10%)
  between operations  14.1 us (5%)
  other arithmetic  13.6 us (5%)
    reduce_scatter x1, waiting for transfers between devices, body(): lax.psum_scatter(term_maker(normed, targets), 'fsdp', scatter_dimension=0...  119 us
    psum x1, waiting for transfers between devices, body(): summed = lax.psum(bands, 'rep')  37.4 us
    dot_general x1, matrix products, term_maker(): lax.dot_general(normed, part, (((0,), (0,)), ((), ())), preferred_element...  23.4 us
    dot_general x2, matrix products, settle(): jnp.einsum('kn,akbl,lm->anbm', basis, bands, basis, precision=lax.Precisi...  12.1 us
    dot_general x2, matrix products, body(): jnp.einsum('kn,akbl,lm->anbm', basis, summed, basis, precision=lax.Precis...  9.76 us
    div x2, local copies, waits for them, and re-layouts, body(): return (cleared[None], update / groups)  9.14 us
    reduce_sum x1, other arithmetic, body(): stat = jnp.mean(values * values, axis=-1, keepdims=True)  7.6 us
    dot_general x2, matrix products, bands_of(): jnp.einsum('kn,anbm,lm->akbl', basis, blocks, basis, precision=lax.Precis...  6.6 us
  transfers between devices with their start and end apart: 2, of which 2 were waited for; matrix products, arithmetic and copies ran while one was open for 6% of the time, Pallas kernels for 0%

commit v1 on v0

v1 whole, which is shorter than its diff:
```python
import jax
import jax.numpy as jnp
import numpy as np
from jax import lax
from jax.experimental import pallas as pl
from jax.experimental.pallas import tpu as pltpu
from jax.sharding import PartitionSpec as P

CH = 64
BAND = 16
EPS = 1e-05
LATE = (5,)
ROWS = 128
SPAN = 256

momentum_decay = 0.9


def basis_rows(size, keep):
    freq = np.arange(keep, dtype=np.float64)[:, None]
    point = np.arange(size, dtype=np.float64)[None, :]
    waves = np.cos(np.pi * (2.0 * point + 1.0) * freq / (2.0 * size))
    scales = np.where(freq == 0.0, np.sqrt(1.0 / size), np.sqrt(2.0 / size))
    return (waves * scales).astype(np.float32)


def halves(value):
    high = value.astype(jnp.bfloat16)
    return high, (value - high.astype(jnp.float32)).astype(jnp.bfloat16)


def times_const(value, const):
    high, low = halves(value)
    return jnp.dot(
        jnp.concatenate([high, low, high], axis=1), const, preferred_element_type=jnp.float32
    )


def const_times(const, value):
    high, low = halves(value)
    return jnp.dot(
        const, jnp.concatenate([high, low, high], axis=0), preferred_element_type=jnp.float32
    )


def constants():
    small = basis_rows(CH, BAND)
    left = np.kron(np.eye(ROWS // CH, dtype=np.float32), small)
    right = np.kron(np.eye(SPAN // CH, dtype=np.float32), small.T)

    def split(m, axis):
        high, low = halves(jnp.asarray(m))
        parts = [high, high, low]
        return jnp.concatenate(parts, axis=axis)

    return {
        "bands_left": split(left, 1),
        "bands_right": split(right, 0),
        "expand_left": split(left.T, 1),
        "expand_right": split(right.T, 0),
    }


def bands_of(fields, left, right):
    tall = times_const(jnp.concatenate(fields, axis=0), right)
    wide = jnp.concatenate([tall[k * ROWS : (k + 1) * ROWS] for k in range(len(fields))], axis=1)
    return const_times(left, wide)


def expand(bands, left, right):
    low = ROWS * BAND // CH
    part = SPAN * BAND // CH
    spans = bands.shape[1] // part
    count = bands.shape[0]
    tall = times_const(
        jnp.concatenate([bands[:, s * part : (s + 1) * part] for s in range(spans)], axis=0), right
    )
    wide = jnp.concatenate([tall[s * count : (s + 1) * count] for s in range(spans)], axis=1)
    return [const_times(left, wide[k : k + low]) for k in range(0, count, low)]


def cost(flops, nbytes):
    return pl.CostEstimate(flops=int(flops), bytes_accessed=int(nbytes), transcendentals=0)


ANY = pl.BlockSpec(memory_space=pl.ANY)
VMEM = pl.BlockSpec(memory_space=pltpu.VMEM)
SMEM = pl.BlockSpec(memory_space=pltpu.SMEM)
F32 = jnp.float32


def on_chip(kernel, ins, tokens, outs, scratch=(), owners=None, flops=0, aliases=None, grant=12):
    lead = [] if owners is None else [owners]
    count = len(lead) + len(ins)

    def run(*refs):
        kernel(*refs[:count], *refs[count + len(tokens) :])

    arrays = [pltpu.with_memory_space_constraint(a, pltpu.VMEM) for a in [*ins, *tokens]]
    return pl.pallas_call(
        run,
        out_shape=tuple(pltpu.VMEM(shape, F32) for shape in outs),
        in_specs=[SMEM] * len(lead) + [VMEM] * len(arrays),
        out_specs=(VMEM,) * len(outs),
        scratch_shapes=list(scratch),
        input_output_aliases={len(lead) + i: o for i, o in (aliases or {}).items()},
        compiler_params=pltpu.CompilerParams(vmem_limit_bytes=grant << 20),
        cost_estimate=cost(flops, 0),
    )(*lead, *arrays)


def fill(xt_ref, x_ref, scale_ref, starts, r):
    scale = scale_ref[...]
    for j, at in enumerate(starts):
        piece = x_ref[:, pl.ds(pl.multiple_of(at, 128), r)].astype(F32) * scale
        xt_ref[j * r : (j + 1) * r, :] = piece.astype(jnp.bfloat16).T


def columns(side, cols, q, w):
    return slice(side * cols // 2 + q, side * cols // 2 + q + w)


def first_call(x, c, owners, n, rows, chunk):
    off, q, w = chunk
    r = ROWS
    tokens, width = x.shape
    cols = c.shape[1]
    half = n // 2
    tile = 128
    group = 64
    tiles = tokens // tile
    parts = [columns(side, cols, q, w) for side in range(2)]
    others = [
        slice(lo, hi)
        for side in range(2)
        for lo, hi in ((side * cols // 2, parts[side].start), (parts[side].stop, (side + 1) * cols // 2))
        if lo < hi
    ]

    def kernel(own, x_hbm, c_hbm, x_ref, c_ref, s_ref, p_ref, xt_ref, x_sem, c_sem):
        def piece(i):
            at = pl.ds(pl.multiple_of(i * tile, tile), tile)
            return pltpu.make_async_copy(x_hbm.at[at, :], x_ref.at[at, :], x_sem.at[i])

        def begin(i, _):
            piece(i).start()
            return 0

        def scale(i, _):
            piece(i).wait()
            for g in range(0, tile, group):
                at = pl.ds(pl.multiple_of(i * tile + g, group), group)
                total = jnp.zeros((group, 128), F32)
                for s in range(0, width, 128):
                    v = x_ref[at, s : s + 128].astype(F32)
                    total = total + v * v
                stat = jnp.sum(total, axis=1, keepdims=True) / width
                s_ref[at, :] = jnp.broadcast_to(lax.rsqrt(stat + EPS), (group, 128))
            return 0

        lax.fori_loop(0, tiles, begin, 0)
        rest = [
            pltpu.make_async_copy(c_hbm.at[:, at], c_ref.at[:, at], c_sem.at[k])
            for k, at in enumerate(parts + others)
        ]
        for copy in rest:
            copy.start()
        lax.fori_loop(0, tiles, scale, 0)
        fill(xt_ref, x_ref, s_ref, [own[2 * j + 1] * rows + off for j in range(half)], r)
        for side in range(2):
            rest[side].wait()
            p_ref[:, :, side * w : (side + 1) * w] = jnp.dot(
                xt_ref[...], c_ref[:, parts[side]], preferred_element_type=F32
            ).reshape(half, r, w)
        for copy in rest[2:]:
            copy.wait()

    return pl.pallas_call(
        kernel,
        out_shape=(
            pltpu.VMEM(x.shape, x.dtype),
            pltpu.VMEM(c.shape, c.dtype),
            pltpu.VMEM((tokens, 128), F32),
            pltpu.VMEM((half, r, 2 * w), F32),
        ),
        in_specs=[SMEM, ANY, ANY],
        out_specs=(VMEM,) * 4,
        scratch_shapes=[
            pltpu.VMEM((half * r, tokens), jnp.bfloat16),
            pltpu.SemaphoreType.DMA((tiles,)),
            pltpu.SemaphoreType.DMA((2 + len(others),)),
        ],
        compiler_params=pltpu.CompilerParams(vmem_limit_bytes=12 << 20),
        cost_estimate=cost(4 * tokens * half * r * w, 2 * tokens * (width + cols)),
        name="first",
    )(owners, *[pltpu.with_memory_space_constraint(a, pltpu.HBM) for a in (x, c)])


def product_call(x, scale, c, owners, n, rows, chunk, parity, tokens):
    off, q, w = chunk
    r = ROWS
    cols = c.shape[1]
    half = n // 2

    def kernel(own, x_ref, s_ref, c_ref, out_ref, xt_ref):
        fill(xt_ref, x_ref, s_ref, [own[2 * j + parity] * rows + off for j in range(half)], r)
        for side in range(2):
            out_ref[:, :, side * w : (side + 1) * w] = jnp.dot(
                xt_ref[...], c_ref[:, columns(side, cols, q, w)], preferred_element_type=F32
            ).reshape(half, r, w)

    (out,) = on_chip(
        kernel, [x, scale, c], tokens, [(half, r, 2 * w)],
        [pltpu.VMEM((half * r, x.shape[0]), jnp.bfloat16)], owners, 4 * x.shape[0] * half * r * w,
    )
    return out


def part_call(even, got, sends, keeps, tokens):
    r, w = even.shape[1], even.shape[2] // 2

    def kernel(even_ref, got_ref, *outs):
        for side in range(2):
            at = slice(side * w, (side + 1) * w)
            for out, masks in ((outs[2 * side], sends[side]), (outs[2 * side + 1], keeps[side])):
                for k, m in enumerate(masks):
                    out[k] = even_ref[m // 2, :, at] + got_ref[m // 2, :, at]

    shapes = [(len(m), r, w) for side in range(2) for m in (sends[side], keeps[side])]
    return on_chip(kernel, [even, got], tokens, shapes)


def add_up(terms, refs):
    total = None
    for array, at in terms:
        value = refs[array][at]
        total = value if total is None else total + value
    return total


def gather(groups):
    arrays, places = [], {}

    def place(array):
        if id(array) not in places:
            places[id(array)] = len(arrays)
            arrays.append(array)
        return places[id(array)]

    plan = [[[(place(a), at) for a, at in terms] for terms in group] for group in groups]
    return arrays, plan


def stage_call(sends, r, wide, tokens):
    arrays, plan = gather(sends)

    def kernel(*refs):
        for out, group in zip(refs[len(arrays) :], plan):
            for j, terms in enumerate(group):
                out[j] = add_up(terms, refs)

    return on_chip(kernel, arrays, tokens, [(len(g), r, wide) for g in plan])


def last_call(sends, keeps, momentum, consts, chunks, rows, wide, before, tokens):
    arrays, plan = gather([sends, keeps])
    terms = len(arrays)
    r = ROWS
    off, _, w = chunks[0]
    narrow = wide * BAND // CH
    low = r * BAND // CH
    high = rows * BAND // CH
    arrays = arrays + [momentum, consts["bands_left"], consts["bands_right"]]
    aliases = {}
    for k, array in enumerate(before or []):
        aliases[len(arrays)] = 2 + k
        arrays.append(array)
    count = len(arrays)
    subs = len(chunks)

    def kernel(*refs):
        out_refs = refs[count : count + 2]
        l_ref, ba_ref, bb_ref, bl_ref = refs[count + 2 :]
        m_ref, left_ref, right_ref = refs[terms : terms + 3]
        sums = [add_up(t, refs) for group in plan for t in group]
        for side in range(2):
            for k, (_, q, _) in enumerate(chunks):
                out_refs[side][k] = sums[side * subs + k]
                at = columns(side, 2 * wide, q, w)
                mine = sums[(2 + side) * subs + k] + momentum_decay * m_ref[0, off : off + r, at]
                sums[(2 + side) * subs + k] = mine
                l_ref[off : off + r, at] = mine
        fields = [total[:, s : s + SPAN] for total in sums for s in range(0, w, SPAN)]
        bands = bands_of(fields, left_ref[...], right_ref[...])
        at = slice(off * BAND // CH, off * BAND // CH + low)
        ba_ref[at, :] = bands[:, :narrow]
        bb_ref[at, :] = bands[:, narrow : 2 * narrow]
        bl_ref[at, :] = bands[:, 2 * narrow :]

    shapes = [
        (subs, r, w), (subs, r, w), (rows, 2 * wide),
        (high, narrow), (high, narrow), (high, 2 * narrow),
    ]
    return on_chip(kernel, arrays, tokens, shapes, flops=24 * r * wide * 128, aliases=aliases)


def join_call(own, a, b):
    narrow = a.shape[1]

    def kernel(own_ref, a_ref, b_ref, out_ref):
        out_ref[:, :narrow] = own_ref[:, :narrow] + a_ref[...]
        out_ref[:, narrow:] = own_ref[:, narrow:] + b_ref[...]

    return on_chip(kernel, [own, a, b], [], [own.shape])[0]


def tree(terms):
    while len(terms) > 1:
        terms = [terms[k] + terms[k + 1] for k in range(0, len(terms), 2)]
    return terms[0]


def outward(kernel, ins, tokens, shape, parts, part, flops, before=None):
    olds = [] if before is None else [before]

    def run(*refs):
        lead = refs[: len(ins)]
        out_hbm, buf, sem = refs[len(ins) + len(tokens) + len(olds) :]

        def send(k, index):
            pltpu.make_async_copy(buf.at[k], out_hbm.at[index], sem.at[k]).start()

        def wait(k, index):
            pltpu.make_async_copy(buf.at[k], out_hbm.at[index], sem.at[k]).wait()

        indices = kernel(buf, send, *lead)
        for k, index in enumerate(indices):
            wait(k, index)

    arrays = [pltpu.with_memory_space_constraint(a, pltpu.VMEM) for a in [*ins, *tokens]]
    return pl.pallas_call(
        run,
        out_shape=jax.ShapeDtypeStruct(shape, F32),
        in_specs=[VMEM] * len(arrays) + [ANY] * len(olds),
        out_specs=ANY,
        scratch_shapes=[pltpu.VMEM((parts,) + part, F32), pltpu.SemaphoreType.DMA((parts,))],
        input_output_aliases={len(arrays): 0} if olds else {},
        compiler_params=pltpu.CompilerParams(vmem_limit_bytes=12 << 20),
        cost_estimate=cost(flops, 4 * parts * part[0] * part[1]),
    )(*arrays, *olds)


def update_call(bands, consts, rows, cols, tokens):
    count = len(bands)
    parts = rows // ROWS

    def kernel(buf, send, *refs):
        total = tree([ref[...] for ref in refs[:count]]) / count
        pieces = expand(total, refs[count][...], refs[count + 1][...])
        indices = [pl.ds(k * ROWS, ROWS) for k in range(parts)]
        for k, piece in enumerate(pieces):
            buf[k] = piece
            send(k, indices[k])
        return indices

    return outward(
        kernel, [*bands, consts["expand_left"], consts["expand_right"]], tokens,
        (rows, cols), parts, (ROWS, cols), 6 * rows * cols * 128,
    )


def finish_call(own, a, b, bands, consts, chunks, before, tokens):
    rows, cols = own.shape
    low = ROWS * BAND // CH
    off, _, w = chunks[0]

    def kernel(buf, send, own_ref, a_ref, b_ref, g_ref, left_ref, right_ref):
        picked = g_ref[off * BAND // CH : off * BAND // CH + low, :]
        (taken,) = expand(picked, left_ref[...], right_ref[...])
        for side, ref in enumerate((a_ref, b_ref)):
            for k, (_, q, _) in enumerate(chunks):
                at = columns(side, cols, q, w)
                buf[0, :, at] = own_ref[off : off + ROWS, at] + ref[k] - taken[:, at]
        index = (0, pl.ds(off, ROWS))
        send(0, index)
        return [index]

    return outward(
        kernel, [own, a, b, bands, consts["expand_left"], consts["expand_right"]], tokens,
        (1, rows, cols), 1, (ROWS, cols), 6 * ROWS * cols * 128, before,
    )


def chunks_of(rows, wide):
    offs = list(range(0, rows, ROWS))
    groups = []
    for k, off in enumerate(offs):
        w = wide // 2 if k < 2 else wide
        groups.append([(off, q, w) for q in range(0, wide, w)])
    return groups


def fast_body(n, groups, activations, cotangent, momentum):
    x, c = activations[0], cotangent[0]
    width = x.shape[1]
    cols = c.shape[1]
    rows = width // n
    wide = cols // 2
    consts = constants()
    owners = lax.axis_index("fsdp").astype(jnp.int32) ^ jnp.arange(n, dtype=jnp.int32)
    bits = [1 << b for b in range(1, n.bit_length() - 1)]
    orders = (bits, bits[::-1])
    evens = range(0, n, 2)
    sends = [[m for m in evens if m & order[0]] for order in orders]
    keeps = [[m for m in evens if not m & order[0]] for order in orders]

    def swap(value, bit, axis="fsdp", size=n):
        return lax.ppermute(value, axis, [(i, i ^ bit) for i in range(size)])

    row_groups = chunks_of(rows, wide)
    chunks = [chunk for group in row_groups for chunk in group]
    x, c, scale, odd = first_call(x, c, owners, n, rows, chunks[0])
    token = odd
    got = swap(odd, 1)
    state = []
    for k, chunk in enumerate(chunks):
        even = product_call(x, scale, c, owners, n, rows, chunk, 0, [token])
        token = even
        here = got
        if k + 1 < len(chunks) and k + 1 not in LATE:
            odd = product_call(x, scale, c, owners, n, rows, chunks[k + 1], 1, [token])
            token = odd
            got = swap(odd, 1)
        outs = part_call(even, here, sends, keeps, [token])
        token = outs[1]
        if k + 1 < len(chunks) and k + 1 in LATE:
            odd = product_call(x, scale, c, owners, n, rows, chunks[k + 1], 1, [token])
            token = odd
            got = swap(odd, 1)
        terms = []
        for side in range(2):
            back = swap(outs[2 * side], orders[side][0])
            terms.append({m: [(outs[2 * side + 1], j), (back, j)] for j, m in enumerate(keeps[side])})
        for stage in range(1, len(bits) - 1):
            now = [orders[side][stage] for side in range(2)]
            out = stage_call(
                [[terms[side][m] for m in sorted(terms[side]) if m & now[side]] for side in range(2)],
                ROWS, chunk[2], [],
            )
            for side in range(2):
                back = swap(out[side], now[side])
                keep = [m for m in sorted(terms[side]) if not m & now[side]]
                terms[side] = {m: terms[side][m] + [(back, j)] for j, m in enumerate(keep)}
        state.append(terms)

    ends = [order[-1] for order in orders]
    before = None
    bulk = []
    at = 0
    for group in row_groups:
        held = state[at : at + len(group)]
        at += len(group)
        a, b, *before = last_call(
            [terms[side][ends[side]] for side in range(2) for terms in held],
            [terms[side][0] for side in range(2) for terms in held],
            momentum, consts, group, rows, wide, before, [token],
        )
        token = a
        bulk.append((swap(a, ends[0]), swap(b, ends[1])))
    band_a = swap(before[1], ends[0])
    band_b = swap(before[2], ends[1])
    mine = join_call(before[3], band_a, band_b)
    every = [mine] + [swap(mine, k, "rep", groups) for k in range(1, groups)]
    nexts = None
    token = mine
    final = len(row_groups) - 1
    for g, group in enumerate(row_groups):
        if g == final:
            update = update_call(every, consts, rows, cols, [token])
        nexts = finish_call(before[0], *bulk[g], mine, consts, group, nexts, [])
    return nexts, update


def plain_body(n, groups, activations, cotangent, momentum):
    values = activations[0].astype(jnp.float32)
    stat = jnp.mean(values * values, axis=-1, keepdims=True)
    normed = (values * lax.rsqrt(stat + EPS)).astype(jnp.bfloat16)
    part = lax.dot_general(
        normed, cotangent[0], (((0,), (0,)), ((), ())), preferred_element_type=jnp.float32
    )
    basis = jnp.asarray(basis_rows(CH, BAND))
    grad = lax.psum_scatter(part, "fsdp", scatter_dimension=0, tiled=True)
    accumulated = momentum_decay * momentum[0] + grad
    rows, width = accumulated.shape
    blocks = accumulated.reshape(rows // CH, CH, width // CH, CH)
    high = lax.Precision.HIGHEST
    bands = jnp.einsum("kn,anbm,lm->akbl", basis, blocks, basis, precision=high)
    own = jnp.einsum("kn,akbl,lm->anbm", basis, bands, basis, precision=high)
    summed = lax.psum(bands, "rep")
    every = jnp.einsum("kn,akbl,lm->anbm", basis, summed, basis, precision=high)
    return ((accumulated - own.reshape(rows, width))[None], every.reshape(rows, width) / groups)


def power(k):
    return k & (k - 1) == 0


def solution(mesh):
    n, groups = mesh.shape["fsdp"], mesh.shape["rep"]
    fits = power(n) and n >= 4 and power(groups)

    def body(activations, cotangent, momentum):
        rows, cols = momentum.shape[1:]
        good = fits and rows % ROWS == 0 and cols % (4 * SPAN) == 0 and activations.shape[1] % 256 == 0
        return (fast_body if good else plain_body)(n, groups, activations, cotangent, momentum)

    return jax.shard_map(
        body,
        mesh=mesh,
        in_specs=(P("rep", "fsdp", None), P("rep", "fsdp", None), P("rep", "fsdp", None)),
        out_specs=(P("rep", "fsdp", None), P("fsdp", None)),
        check_vma=False,
    )
```

time: 262 us -> 128 us (0.49)
  waiting for transfers between devices: 156 us -> 44.4 us
  matrix products: 51.8 us -> 0 us
  Pallas kernels: 0 us -> 47 us
  starting transfers between devices: 0.04 us -> 35.9 us
  local copies, waits for them, and re-layouts: 26.1 us -> 0.03 us
  other arithmetic: 13.6 us -> 0.01 us
  between operations: 14.1 us -> 1.03 us
    reduce_scatter x1 -> x0, waiting for transfers between devices: 119 us -> none  [body(): lax.psum_scatter(term_maker(normed, targets), 'fsdp', scatter_dimension=0...]
    dot_general x7 -> x0, matrix products: 51.8 us -> none  [the longest x1 23.4 us: term_maker(): lax.dot_general(normed, part, (((0,), (0,)), ((), ())), preferred_element...]
    pallas_call x0 -> x28, Pallas kernels: none -> 47 us  [the longest x22 29.9 us: on_chip(): pl.pallas_call(run, out_shape=tuple((pltpu.VMEM(shape, F32) for shape in...]
    ppermute x0 -> x31, waiting for transfers between devices: none -> 44.4 us  [swap(): return lax.ppermute(value, axis, [(i, i ^ bit) for i in range(size)])]
    psum x1 -> x0, waiting for transfers between devices: 37.4 us -> none  [body(): summed = lax.psum(bands, 'rep')]
    ppermute x0 -> x31, starting transfers between devices: none -> 35.9 us  [swap(): return lax.ppermute(value, axis, [(i, i ^ bit) for i in range(size)])]
    div x2 -> x0, local copies, waits for them, and re-layouts: 9.14 us -> none  [body(): return (cleared[None], update / groups)]
    reduce_sum x1 -> x0, other arithmetic: 7.6 us -> none  [body(): stat = jnp.mean(values * values, axis=-1, keepdims=True)]
  transfers between devices with their start and end apart: 2 -> 31, of which waited for: 2 -> 8; matrix products, arithmetic and copies ran while one was open for 6% -> 0% of each run, Pallas kernels for 0% -> 21%
where the time goes in v1:
time: 128 us
  Pallas kernels  47 us (37%)
  waiting for transfers between devices  44.4 us (35%)
  starting transfers between devices  35.9 us (28%)
    ppermute x31, waiting for transfers between devices, swap(): return lax.ppermute(value, axis, [(i, i ^ bit) for i in range(size)])  44.4 us
    ppermute x31, starting transfers between devices, swap(): return lax.ppermute(value, axis, [(i, i ^ bit) for i in range(size)])  35.9 us
    pallas_call x22, Pallas kernels, on_chip(): pl.pallas_call(run, out_shape=tuple((pltpu.VMEM(shape, F32) for shape in...  29.9 us
    pallas_call x1, Pallas kernels, first_call(): pl.pallas_call(kernel, out_shape=(pltpu.VMEM(x.shape, x.dtype), pltpu.VME...  10.1 us
    pallas_call x5, Pallas kernels, outward(): pl.pallas_call(run, out_shape=jax.ShapeDtypeStruct(shape, F32), in_specs=...  6.95 us
  transfers between devices with their start and end apart: 31, of which 8 were waited for; matrix products, arithmetic and copies ran while one was open for 0% of the time, Pallas kernels for 21%

profile of v1, /device:TPU:0, one launch (start us, length us, event | category | flops | bytes accessed | tf_op | source)
XLA Modules:
  0.0 128.3 jit_solution(2201320825691219936)
XLA Ops:
  0.6 10.1 %first.1 = (bf16[2048,4096]{1,0:T(8,128)(2,1)S(1)}, bf16[2048,1024]{1,0:T(8,128)(2,1)S(1)}, f32[2048,128]{1,0:T(8,128)S(1)}, f32[4,128,512]{2,1,0:T(8,128)S(1)}) custom-call(s32[8]{0:T(128)S(1)} %iota_xor_fusion.own.refs_0_, bf16[2048,4096]{1,0:T(8,128)(2,1)} %bitcast.2, bf16[2048,1024]{1,0:T(8,128)(2,1)} %bitcast.3), custom_call_target="tpu_custom_call" | custom-call | flops 1073741824 | bytes 20971520 | tf_op jit(solution)/shard_map/first/pallas_call | solution.py:178
  10.8 0.6 collective-permute-start
  11.3 1.9 %shard_map.86.refs_4_.refs_0_ = f32[4,128,512]{2,1,0:T(8,128)S(1)} custom-call(s32[8]{0:T(128)S(1)} %iota_xor_fusion.own.refs_0_, bf16[2048,4096]{1,0:T(8,128)(2,1)S(1)} %get-tuple-element.54.refs_1_, f32[2048,128]{1,0:T(8,128)S(1)} %get-tuple-element.55.refs_2_, bf16[2048,1024]{1,0:T(8,128)(2,1)S(1)} %get-tuple-element.56.refs_3_, ...), custom_call_target="tpu_custom_call" | custom-call | flops 1073741824 | tf_op jit(solution)/shard_map/pallas_call | solution.py:100
  13.2 1.9 %shard_map.87.refs_2_ = f32[4,128,512]{2,1,0:T(8,128)S(1)} custom-call(s32[8]{0:T(128)S(1)} %iota_xor_fusion.own.refs_0_, bf16[2048,4096]{1,0:T(8,128)(2,1)S(1)} %get-tuple-element.54.refs_1_, f32[2048,128]{1,0:T(8,128)S(1)} %get-tuple-element.55.refs_2_, bf16[2048,1024]{1,0:T(8,128)(2,1)S(1)} %get-tuple-element.56.refs_3_, ...), custom_call_target="tpu_custom_call" | custom-call | flops 1073741824 | tf_op jit(solution)/shard_map/pallas_call | solution.py:100
  15.1 0.1 collective-permute-start.1
  15.2 0.1 shard_map.88
  15.4 1.9 %shard_map.89.refs_4_.refs_0_ = f32[4,128,512]{2,1,0:T(8,128)S(1)} custom-call(s32[8]{0:T(128)S(1)} %iota_xor_fusion.own.refs_0_, bf16[2048,4096]{1,0:T(8,128)(2,1)S(1)} %get-tuple-element.54.refs_1_, f32[2048,128]{1,0:T(8,128)S(1)} %get-tuple-element.55.refs_2_, bf16[2048,1024]{1,0:T(8,128)(2,1)S(1)} %get-tuple-element.56.refs_3_, ...), custom_call_target="tpu_custom_call" | custom-call | flops 1073741824 | tf_op jit(solution)/shard_map/pallas_call | solution.py:100
  17.3 1.9 %shard_map.90.refs_2_ = f32[4,128,512]{2,1,0:T(8,128)S(1)} custom-call(s32[8]{0:T(128)S(1)} %iota_xor_fusion.own.refs_0_, bf16[2048,4096]{1,0:T(8,128)(2,1)S(1)} %get-tuple-element.54.refs_1_, f32[2048,128]{1,0:T(8,128)S(1)} %get-tuple-element.55.refs_2_, bf16[2048,1024]{1,0:T(8,128)(2,1)S(1)} %get-tuple-element.56.refs_3_, ...), custom_call_target="tpu_custom_call" | custom-call | flops 1073741824 | tf_op jit(solution)/shard_map/pallas_call | solution.py:100
  19.2 0.6 collective-permute-start.2
  19.8 0.1 shard_map.91
  19.9 1.9 %shard_map.92.refs_4_.refs_0_ = f32[4,128,512]{2,1,0:T(8,128)S(1)} custom-call(s32[8]{0:T(128)S(1)} %iota_xor_fusion.own.refs_0_, bf16[2048,4096]{1,0:T(8,128)(2,1)S(1)} %get-tuple-element.54.refs_1_, f32[2048,128]{1,0:T(8,128)S(1)} %get-tuple-element.55.refs_2_, bf16[2048,1024]{1,0:T(8,128)(2,1)S(1)} %get-tuple-element.56.refs_3_, ...), custom_call_target="tpu_custom_call" | custom-call | flops 1073741824 | tf_op jit(solution)/shard_map/pallas_call | solution.py:100
  21.8 1.9 %shard_map.93.refs_2_ = f32[4,128,512]{2,1,0:T(8,128)S(1)} custom-call(s32[8]{0:T(128)S(1)} %iota_xor_fusion.own.refs_0_, bf16[2048,4096]{1,0:T(8,128)(2,1)S(1)} %get-tuple-element.54.refs_1_, f32[2048,128]{1,0:T(8,128)S(1)} %get-tuple-element.55.refs_2_, bf16[2048,1024]{1,0:T(8,128)(2,1)S(1)} %get-tuple-element.56.refs_3_, ...), custom_call_target="tpu_custom_call" | custom-call | flops 1073741824 | tf_op jit(solution)/shard_map/pallas_call | solution.py:100
  23.7 0.1 shard_map.94
  23.9 1.9 %shard_map.95.refs_4_.refs_0_ = f32[4,128,512]{2,1,0:T(8,128)S(1)} custom-call(s32[8]{0:T(128)S(1)} %iota_xor_fusion.own.refs_0_, bf16[2048,4096]{1,0:T(8,128)(2,1)S(1)} %get-tuple-element.54.refs_1_, f32[2048,128]{1,0:T(8,128)S(1)} %get-tuple-element.55.refs_2_, bf16[2048,1024]{1,0:T(8,128)(2,1)S(1)} %get-tuple-element.56.refs_3_, ...), custom_call_target="tpu_custom_call" | custom-call | flops 1073741824 | tf_op jit(solution)/shard_map/pallas_call | solution.py:100
  25.8 3.1 %shard_map.96.refs_2_ = f32[4,128,1024]{2,1,0:T(8,128)S(1)} custom-call(s32[8]{0:T(128)S(1)} %iota_xor_fusion.own.refs_0_, bf16[2048,4096]{1,0:T(8,128)(2,1)S(1)} %get-tuple-element.54.refs_1_, f32[2048,128]{1,0:T(8,128)S(1)} %get-tuple-element.55.refs_2_, bf16[2048,1024]{1,0:T(8,128)(2,1)S(1)} %get-tuple-element.56.refs_3_, ...), custom_call_target="tpu_custom_call" | custom-call | flops 2147483648 | tf_op jit(solution)/shard_map/pallas_call | solution.py:100
  28.9 0.1 collective-permute-start.4
  29.1 0.4 collective-permute-start.3
  29.5 5.1 %collective-permute-done.3.refs_1_ = f32[4,128,512]{2,1,0:T(8,128)S(1)} collective-permute-done((f32[4,128,512]{2,1,0:T(8,128)S(1)}, f32[4,128,512]{2,1,0:T(8,128)S(1)}, u32[]{:S(2)}, u32[]{:S(2)}) %collective-permute-start.3) | collective-permute-done | bytes 1048608 | tf_op jit(solution)/shard_map/ppermute | solution.py:418
  34.7 0.1 shard_map.97
  34.8 3.0 %shard_map.98.refs_0_.refs_2_ = f32[4,128,1024]{2,1,0:T(8,128)S(1)} custom-call(s32[8]{0:T(128)S(1)} %iota_xor_fusion.own.refs_0_, bf16[2048,4096]{1,0:T(8,128)(2,1)S(1)} %get-tuple-element.54.refs_1_, f32[2048,128]{1,0:T(8,128)S(1)} %get-tuple-element.55.refs_2_, bf16[2048,1024]{1,0:T(8,128)(2,1)S(1)} %get-tuple-element.56.refs_3_, ...), custom_call_target="tpu_custom_call" | custom-call | flops 2147483648 | tf_op jit(solution)/shard_map/pallas_call | solution.py:100
  37.8 0.2 shard_map.99
  38.0 2.9 %shard_map.100.refs_4_ = f32[4,128,1024]{2,1,0:T(8,128)S(1)} custom-call(s32[8]{0:T(128)S(1)} %iota_xor_fusion.own.refs_0_, bf16[2048,4096]{1,0:T(8,128)(2,1)S(1)} %get-tuple-element.54.refs_1_, f32[2048,128]{1,0:T(8,128)S(1)} %get-tuple-element.55.refs_2_, bf16[2048,1024]{1,0:T(8,128)(2,1)S(1)} %get-tuple-element.56.refs_3_, ...), custom_call_target="tpu_custom_call" | custom-call | flops 2147483648 | tf_op jit(solution)/shard_map/pallas_call | solution.py:100
  40.9 0.2 collective-permute-start.5
  41.1 2.9 %collective-permute-start.14 = (f32[2,128,256]{2,1,0:T(8,128)S(1)}, f32[2,128,256]{2,1,0:T(8,128)S(1)}, u32[]{:S(2)}, u32[]{:S(2)}) collective-permute-start(f32[2,128,256]{2,1,0:T(8,128)S(1)} %get-tuple-element.76), channel_id=1, source_target_pairs={{0,2},{1,3},{2,0},{3,1},{4,6},{5,7},{6,4},{7,5},{8,10},{9,11},{10,... | collective-permute-start | bytes 786440 | tf_op jit(solution)/shard_map/ppermute | solution.py:418
  44.0 1.5 %collective-permute-start.16 = (f32[2,128,256]{2,1,0:T(8,128)S(1)}, f32[2,128,256]{2,1,0:T(8,128)S(1)}, u32[]{:S(2)}, u32[]{:S(2)}) collective-permute-start(f32[2,128,256]{2,1,0:T(8,128)S(1)} %get-tuple-element.79), channel_id=1, source_target_pairs={{0,4},{1,5},{2,6},{3,7},{4,0},{5,1},{6,2},{7,3},{8,12},{9,13},{10,... | collective-permute-start | bytes 786440 | tf_op jit(solution)/shard_map/ppermute | solution.py:418
  45.5 0.5 collective-permute-start.15
  46.1 5.1 %collective-permute-done.14.refs_1_ = f32[2,128,256]{2,1,0:T(8,128)S(1)} collective-permute-done((f32[2,128,256]{2,1,0:T(8,128)S(1)}, f32[2,128,256]{2,1,0:T(8,128)S(1)}, u32[]{:S(2)}, u32[]{:S(2)}) %collective-permute-start.14) | collective-permute-done | bytes 262176 | tf_op jit(solution)/shard_map/ppermute | solution.py:418
  51.2 2.0 %collective-permute-start.10 = (f32[2,128,256]{2,1,0:T(8,128)S(1)}, f32[2,128,256]{2,1,0:T(8,128)S(1)}, u32[]{:S(2)}, u32[]{:S(2)}) collective-permute-start(f32[2,128,256]{2,1,0:T(8,128)S(1)} %get-tuple-element.70), channel_id=1, source_target_pairs={{0,2},{1,3},{2,0},{3,1},{4,6},{5,7},{6,4},{7,5},{8,10},{9,11},{10,... | collective-permute-start | bytes 786440 | tf_op jit(solution)/shard_map/ppermute | solution.py:418
  53.2 3.6 %collective-permute-done.15.refs_3_ = f32[2,128,256]{2,1,0:T(8,128)S(1)} collective-permute-done((f32[2,128,256]{2,1,0:T(8,128)S(1)}, f32[2,128,256]{2,1,0:T(8,128)S(1)}, u32[]{:S(2)}, u32[]{:S(2)}) %collective-permute-start.15) | collective-permute-done | bytes 262176 | tf_op jit(solution)/shard_map/ppermute | solution.py:418
  56.8 2.0 %collective-permute-start.9 = (f32[2,128,512]{2,1,0:T(8,128)S(1)}, f32[2,128,512]{2,1,0:T(8,128)S(1)}, u32[]{:S(2)}, u32[]{:S(2)}) collective-permute-start(f32[2,128,512]{2,1,0:T(8,128)S(1)} %get-tuple-element.69), channel_id=1, source_target_pairs={{0,4},{1,5},{2,6},{3,7},{4,0},{5,1},{6,2},{7,3},{8,12},{9,13},{10,... | collective-permute-start | bytes 1572872 | tf_op jit(solution)/shard_map/ppermute | solution.py:418
  58.9 0.4 collective-permute-start.12
  59.2 3.2 %collective-permute-done.10.refs_1_ = f32[2,128,256]{2,1,0:T(8,128)S(1)} collective-permute-done((f32[2,128,256]{2,1,0:T(8,128)S(1)}, f32[2,128,256]{2,1,0:T(8,128)S(1)}, u32[]{:S(2)}, u32[]{:S(2)}) %collective-permute-start.10) | collective-permute-done | bytes 262176 | tf_op jit(solution)/shard_map/ppermute | solution.py:418
  62.4 2.0 %collective-permute-start.11 = (f32[2,128,256]{2,1,0:T(8,128)S(1)}, f32[2,128,256]{2,1,0:T(8,128)S(1)}, u32[]{:S(2)}, u32[]{:S(2)}) collective-permute-start(f32[2,128,256]{2,1,0:T(8,128)S(1)} %get-tuple-element.71), channel_id=1, source_target_pairs={{0,2},{1,3},{2,0},{3,1},{4,6},{5,7},{6,4},{7,5},{8,10},{9,11},{10,... | collective-permute-start | bytes 786440 | tf_op jit(solution)/shard_map/ppermute | solution.py:418
  64.4 1.5 %collective-permute-start.13 = (f32[2,128,256]{2,1,0:T(8,128)S(1)}, f32[2,128,256]{2,1,0:T(8,128)S(1)}, u32[]{:S(2)}, u32[]{:S(2)}) collective-permute-start(f32[2,128,256]{2,1,0:T(8,128)S(1)} %get-tuple-element.75), channel_id=1, source_target_pairs={{0,4},{1,5},{2,6},{3,7},{4,0},{5,1},{6,2},{7,3},{8,12},{9,13},{10,... | collective-permute-start | bytes 786440 | tf_op jit(solution)/shard_map/ppermute | solution.py:418
  66.0 3.0 %shard_map.101.refs_0_.refs_2_ = f32[4,128,1024]{2,1,0:T(8,128)S(1)} custom-call(s32[8]{0:T(128)S(1)} %iota_xor_fusion.own.refs_0_, bf16[2048,4096]{1,0:T(8,128)(2,1)S(1)} %get-tuple-element.54.refs_1_, f32[2048,128]{1,0:T(8,128)S(1)} %get-tuple-element.55.refs_2_, bf16[2048,1024]{1,0:T(8,128)(2,1)S(1)} %get-tuple-element.56.refs_3_, ...), custom_call_target="tpu_custom_call" | custom-call | flops 2147483648 | tf_op jit(solution)/shard_map/pallas_call | solution.py:100
  69.0 0.3 shard_map.102
  69.3 7.9 %collective-permute-done.12.refs_5_ = f32[2,128,256]{2,1,0:T(8,128)S(1)} collective-permute-done((f32[2,128,256]{2,1,0:T(8,128)S(1)}, f32[2,128,256]{2,1,0:T(8,128)S(1)}, u32[]{:S(2)}, u32[]{:S(2)}) %collective-permute-start.12) | collective-permute-done | bytes 262176 | tf_op jit(solution)/shard_map/ppermute | solution.py:418
  77.2 2.0 %collective-permute-start.6 = (f32[2,128,512]{2,1,0:T(8,128)S(1)}, f32[2,128,512]{2,1,0:T(8,128)S(1)}, u32[]{:S(2)}, u32[]{:S(2)}) collective-permute-start(f32[2,128,512]{2,1,0:T(8,128)S(1)} %get-tuple-element.64), channel_id=1, source_target_pairs={{0,2},{1,3},{2,0},{3,1},{4,6},{5,7},{6,4},{7,5},{8,10},{9,11},{10,... | collective-permute-start | bytes 1572872 | tf_op jit(solution)/shard_map/ppermute | solution.py:418
  79.2 0.0 collective-permute-done.11.refs_3_
  79.3 2.0 %collective-permute-start.7 = (f32[2,128,512]{2,1,0:T(8,128)S(1)}, f32[2,128,512]{2,1,0:T(8,128)S(1)}, u32[]{:S(2)}, u32[]{:S(2)}) collective-permute-start(f32[2,128,512]{2,1,0:T(8,128)S(1)} %get-tuple-element.66), channel_id=1, source_target_pairs={{0,4},{1,5},{2,6},{3,7},{4,0},{5,1},{6,2},{7,3},{8,12},{9,13},{10,... | collective-permute-start | bytes 1572872 | tf_op jit(solution)/shard_map/ppermute | solution.py:418
  81.3 0.9 shard_map.103
  82.2 0.9 shard_map.104
  83.1 0.9 shard_map.105
  84.0 1.5 %collective-permute-start.23 = (f32[1,128,512]{2,1,0:T(8,128)S(1)}, f32[1,128,512]{2,1,0:T(8,128)S(1)}, u32[]{:S(2)}, u32[]{:S(2)}) collective-permute-start(f32[1,128,512]{2,1,0:T(8,128)S(1)} %get-tuple-element.103), channel_id=1, source_target_pairs={{0,2},{1,3},{2,0},{3,1},{4,6},{5,7},{6,4},{7,5},{8,10},{9,11},{10,... | collective-permute-start | bytes 786440 | tf_op jit(solution)/shard_map/ppermute | solution.py:418
  85.5 0.5 collective-permute-start.22
  86.0 0.2 collective-permute-start.25
  86.2 11.5 %collective-permute-done.23.refs_2_ = f32[1,128,512]{2,1,0:T(8,128)S(1)} collective-permute-done((f32[1,128,512]{2,1,0:T(8,128)S(1)}, f32[1,128,512]{2,1,0:T(8,128)S(1)}, u32[]{:S(2)}, u32[]{:S(2)}) %collective-permute-start.23) | collective-permute-done | bytes 262176 | tf_op jit(solution)/shard_map/ppermute | solution.py:418
  97.7 2.0 %collective-permute-start.24 = (f32[2,128,256]{2,1,0:T(8,128)S(1)}, f32[2,128,256]{2,1,0:T(8,128)S(1)}, u32[]{:S(2)}, u32[]{:S(2)}) collective-permute-start(f32[2,128,256]{2,1,0:T(8,128)S(1)} %get-tuple-element.91.refs_11_), channel_id=1, source_target_pairs={{0,4},{1,5},{2,6},{3,7},{4,0},{5,1},{6,2},{7,3},{8,12},{9,13},{10,... | collective-permute-start | bytes 786440 | tf_op jit(solution)/shard_map/ppermute | solution.py:418
  99.7 1.5 %collective-permute-start.27 = (f32[2,128,256]{2,1,0:T(8,128)S(1)}, f32[2,128,256]{2,1,0:T(8,128)S(1)}, u32[]{:S(2)}, u32[]{:S(2)}) collective-permute-start(f32[2,128,256]{2,1,0:T(8,128)S(1)} %get-tuple-element.105), channel_id=1, source_target_pairs={{0,2},{1,3},{2,0},{3,1},{4,6},{5,7},{6,4},{7,5},{8,10},{9,11},{10,... | collective-permute-start | bytes 786440 | tf_op jit(solution)/shard_map/ppermute | solution.py:418
  101.2 0.5 collective-permute-start.26
  101.7 0.9 shard_map.106
  102.6 1.5 %collective-permute-start.20 = (f32[128,128]{1,0:T(8,128)S(1)}, f32[128,128]{1,0:T(8,128)S(1)}, u32[]{:S(2)}, u32[]{:S(2)}) collective-permute-start(f32[128,128]{1,0:T(8,128)S(1)} %get-tuple-element.101), channel_id=1, source_target_pairs={{0,4},{1,5},{2,6},{3,7},{4,0},{5,1},{6,2},{7,3},{8,12},{9,13},{10,... | collective-permute-start | bytes 196616 | tf_op jit(solution)/shard_map/ppermute | solution.py:418
  104.1 1.2 collective-permute-start.21
  105.3 5.9 %collective-permute-done.20.refs_1_ = f32[128,128]{1,0:T(8,128)S(1)} collective-permute-done((f32[128,128]{1,0:T(8,128)S(1)}, f32[128,128]{1,0:T(8,128)S(1)}, u32[]{:S(2)}, u32[]{:S(2)}) %collective-permute-start.20) | collective-permute-done | bytes 65568 | tf_op jit(solution)/shard_map/ppermute | solution.py:418
  111.1 2.0 %collective-permute-start.18 = (f32[1,128,512]{2,1,0:T(8,128)S(1)}, f32[1,128,512]{2,1,0:T(8,128)S(1)}, u32[]{:S(2)}, u32[]{:S(2)}) collective-permute-start(f32[1,128,512]{2,1,0:T(8,128)S(1)} %get-tuple-element.98), channel_id=1, source_target_pairs={{0,4},{1,5},{2,6},{3,7},{4,0},{5,1},{6,2},{7,3},{8,12},{9,13},{10,... | collective-permute-start | bytes 786440 | tf_op jit(solution)/shard_map/ppermute | solution.py:418
  113.2 1.5 %collective-permute-start.19 = (f32[1,128,512]{2,1,0:T(8,128)S(1)}, f32[1,128,512]{2,1,0:T(8,128)S(1)}, u32[]{:S(2)}, u32[]{:S(2)}) collective-permute-start(f32[1,128,512]{2,1,0:T(8,128)S(1)} %get-tuple-element.99), channel_id=1, source_target_pairs={{0,2},{1,3},{2,0},{3,1},{4,6},{5,7},{6,4},{7,5},{8,10},{9,11},{10,... | collective-permute-start | bytes 786440 | tf_op jit(solution)/shard_map/ppermute | solution.py:418
  114.7 3.7 %collective-permute-start.30 = (f32[128,256]{1,0:T(8,128)S(1)}, f32[128,256]{1,0:T(8,128)S(1)}, u32[]{:S(2)}, u32[]{:S(2)}) collective-permute-start(f32[128,256]{1,0:T(8,128)S(1)} %shard_map.107.refs_3_.refs_0_.refs_6_), channel_id=1, source_target_pairs={{0,24},{8,16},{16,8},{24,0},{1,25},{9,17},{17,9},{25,1},{2,26},{10... | collective-permute-start | bytes 393224 | tf_op jit(solution)/shard_map/ppermute | solution.py:418
  118.4 0.8 collective-permute-start.28
  119.2 1.3 shard_map.108.refs_6_
  120.4 1.3 shard_map.109.refs_6_
  121.7 1.3 shard_map.110.refs_6_
  123.0 1.9 %collective-permute-done.29.refs_2_ = f32[128,256]{1,0:T(8,128)S(1)} collective-permute-done((f32[128,256]{1,0:T(8,128)S(1)}, f32[128,256]{1,0:T(8,128)S(1)}, u32[]{:S(2)}, u32[]{:S(2)}) %collective-permute-start.29) | collective-permute-done | bytes 131104 | tf_op jit(solution)/shard_map/ppermute | solution.py:418
  125.0 1.9 %shard_map.112 = f32[512,1024]{1,0:T(8,128)} custom-call(f32[128,256]{1,0:T(8,128)S(1)} %shard_map.107.refs_3_.refs_0_.refs_6_, f32[128,256]{1,0:T(8,128)S(1)} %collective-permute-done.28.refs_1_, f32[128,256]{1,0:T(8,128)S(1)} %collective-permute-done.29.refs_2_, f32[128,256]{1,0:T(8,128)S(1)} %collective-permute-done.30.refs_3_, ...), custom_call_target="tpu_custom_call" | custom-call | flops 402653184 | bytes 2097152 | tf_op jit(solution)/shard_map/pallas_call | solution.py:341
  126.9 1.3 shard_map.111
  (37 shorter events, 0.1 us)
Async XLA Ops:
  10.8 4.5 %collective-permute-start = (f32[4,128,512]{2,1,0:T(8,128)S(1)}, f32[4,128,512]{2,1,0:T(8,128)S(1)}, u32[]{:S(2)}, u32[]{:S(2)}) collective-permute-start(f32[4,128,512]{2,1,0:T(8,128)S(1)} %get-tuple-element.57.refs_4_), channel_id=1, source_target_pairs={{0,1},{1,0},{2,3},{3,2},{4,5},{5,4},{6,7},{7,6},{8,9},{9,8},{10,11... | collective-permute-start | bytes 3145736 | tf_op jit(solution)/shard_map/ppermute | solution.py:418
  15.1 4.6 %collective-permute-start.1 = (f32[4,128,512]{2,1,0:T(8,128)S(1)}, f32[4,128,512]{2,1,0:T(8,128)S(1)}, u32[]{:S(2)}, u32[]{:S(2)}) collective-permute-start(f32[4,128,512]{2,1,0:T(8,128)S(1)} %shard_map.87.refs_2_), channel_id=1, source_target_pairs={{0,1},{1,0},{2,3},{3,2},{4,5},{5,4},{6,7},{7,6},{8,9},{9,8},{10,11... | collective-permute-start | bytes 3145736 | tf_op jit(solution)/shard_map/ppermute | solution.py:418
  19.2 4.5 %collective-permute-start.2 = (f32[4,128,512]{2,1,0:T(8,128)S(1)}, f32[4,128,512]{2,1,0:T(8,128)S(1)}, u32[]{:S(2)}, u32[]{:S(2)}) collective-permute-start(f32[4,128,512]{2,1,0:T(8,128)S(1)} %shard_map.90.refs_2_), channel_id=1, source_target_pairs={{0,1},{1,0},{2,3},{3,2},{4,5},{5,4},{6,7},{7,6},{8,9},{9,8},{10,11... | collective-permute-start | bytes 3145736 | tf_op jit(solution)/shard_map/ppermute | solution.py:418
  28.9 8.9 %collective-permute-start.4 = (f32[4,128,1024]{2,1,0:T(8,128)S(1)}, f32[4,128,1024]{2,1,0:T(8,128)S(1)}, u32[]{:S(2)}, u32[]{:S(2)}) collective-permute-start(f32[4,128,1024]{2,1,0:T(8,128)S(1)} %shard_map.96.refs_2_), channel_id=1, source_target_pairs={{0,1},{1,0},{2,3},{3,2},{4,5},{5,4},{6,7},{7,6},{8,9},{9,8},{10,11... | collective-permute-start | bytes 6291464 | tf_op jit(solution)/shard_map/ppermute | solution.py:418
  29.1 5.6 %collective-permute-start.3 = (f32[4,128,512]{2,1,0:T(8,128)S(1)}, f32[4,128,512]{2,1,0:T(8,128)S(1)}, u32[]{:S(2)}, u32[]{:S(2)}) collective-permute-start(f32[4,128,512]{2,1,0:T(8,128)S(1)} %shard_map.93.refs_2_), channel_id=1, source_target_pairs={{0,1},{1,0},{2,3},{3,2},{4,5},{5,4},{6,7},{7,6},{8,9},{9,8},{10,11... | collective-permute-start | bytes 3145736 | tf_op jit(solution)/shard_map/ppermute | solution.py:418
  40.9 23.5 %collective-permute-start.5 = (f32[4,128,1024]{2,1,0:T(8,128)S(1)}, f32[4,128,1024]{2,1,0:T(8,128)S(1)}, u32[]{:S(2)}, u32[]{:S(2)}) collective-permute-start(f32[4,128,1024]{2,1,0:T(8,128)S(1)} %shard_map.100.refs_4_), channel_id=1, source_target_pairs={{0,1},{1,0},{2,3},{3,2},{4,5},{5,4},{6,7},{7,6},{8,9},{9,8},{10,11... | collective-permute-start | bytes 6291464 | tf_op jit(solution)/shard_map/ppermute | solution.py:418
  41.1 10.0 %collective-permute-start.14 = (f32[2,128,256]{2,1,0:T(8,128)S(1)}, f32[2,128,256]{2,1,0:T(8,128)S(1)}, u32[]{:S(2)}, u32[]{:S(2)}) collective-permute-start(f32[2,128,256]{2,1,0:T(8,128)S(1)} %get-tuple-element.76), channel_id=1, source_target_pairs={{0,2},{1,3},{2,0},{3,1},{4,6},{5,7},{6,4},{7,5},{8,10},{9,11},{10,... | collective-permute-start | bytes 786440 | tf_op jit(solution)/shard_map/ppermute | solution.py:418
  44.0 9.2 %collective-permute-start.16 = (f32[2,128,256]{2,1,0:T(8,128)S(1)}, f32[2,128,256]{2,1,0:T(8,128)S(1)}, u32[]{:S(2)}, u32[]{:S(2)}) collective-permute-start(f32[2,128,256]{2,1,0:T(8,128)S(1)} %get-tuple-element.79), channel_id=1, source_target_pairs={{0,4},{1,5},{2,6},{3,7},{4,0},{5,1},{6,2},{7,3},{8,12},{9,13},{10,... | collective-permute-start | bytes 786440 | tf_op jit(solution)/shard_map/ppermute | solution.py:418
  45.5 11.3 %collective-permute-start.15 = (f32[2,128,256]{2,1,0:T(8,128)S(1)}, f32[2,128,256]{2,1,0:T(8,128)S(1)}, u32[]{:S(2)}, u32[]{:S(2)}) collective-permute-start(f32[2,128,256]{2,1,0:T(8,128)S(1)} %get-tuple-element.77), channel_id=1, source_target_pairs={{0,2},{1,3},{2,0},{3,1},{4,6},{5,7},{6,4},{7,5},{8,10},{9,11},{10,... | collective-permute-start | bytes 786440 | tf_op jit(solution)/shard_map/ppermute | solution.py:418
  46.1 12.8 %collective-permute-start.17 = (f32[2,128,256]{2,1,0:T(8,128)S(1)}, f32[2,128,256]{2,1,0:T(8,128)S(1)}, u32[]{:S(2)}, u32[]{:S(2)}) collective-permute-start(f32[2,128,256]{2,1,0:T(8,128)S(1)} %get-tuple-element.81), channel_id=1, source_target_pairs={{0,4},{1,5},{2,6},{3,7},{4,0},{5,1},{6,2},{7,3},{8,12},{9,13},{10,... | collective-permute-start | bytes 786440 | tf_op jit(solution)/shard_map/ppermute | solution.py:418
  51.2 11.2 %collective-permute-start.10 = (f32[2,128,256]{2,1,0:T(8,128)S(1)}, f32[2,128,256]{2,1,0:T(8,128)S(1)}, u32[]{:S(2)}, u32[]{:S(2)}) collective-permute-start(f32[2,128,256]{2,1,0:T(8,128)S(1)} %get-tuple-element.70), channel_id=1, source_target_pairs={{0,2},{1,3},{2,0},{3,1},{4,6},{5,7},{6,4},{7,5},{8,10},{9,11},{10,... | collective-permute-start | bytes 786440 | tf_op jit(solution)/shard_map/ppermute | solution.py:418
  53.2 29.9 %collective-permute-start.8 = (f32[2,128,512]{2,1,0:T(8,128)S(1)}, f32[2,128,512]{2,1,0:T(8,128)S(1)}, u32[]{:S(2)}, u32[]{:S(2)}) collective-permute-start(f32[2,128,512]{2,1,0:T(8,128)S(1)} %get-tuple-element.67), channel_id=1, source_target_pairs={{0,2},{1,3},{2,0},{3,1},{4,6},{5,7},{6,4},{7,5},{8,10},{9,11},{10,... | collective-permute-start | bytes 1572872 | tf_op jit(solution)/shard_map/ppermute | solution.py:418
  56.8 26.3 %collective-permute-start.9 = (f32[2,128,512]{2,1,0:T(8,128)S(1)}, f32[2,128,512]{2,1,0:T(8,128)S(1)}, u32[]{:S(2)}, u32[]{:S(2)}) collective-permute-start(f32[2,128,512]{2,1,0:T(8,128)S(1)} %get-tuple-element.69), channel_id=1, source_target_pairs={{0,4},{1,5},{2,6},{3,7},{4,0},{5,1},{6,2},{7,3},{8,12},{9,13},{10,... | collective-permute-start | bytes 1572872 | tf_op jit(solution)/shard_map/ppermute | solution.py:418
  58.9 18.4 %collective-permute-start.12 = (f32[2,128,256]{2,1,0:T(8,128)S(1)}, f32[2,128,256]{2,1,0:T(8,128)S(1)}, u32[]{:S(2)}, u32[]{:S(2)}) collective-permute-start(f32[2,128,256]{2,1,0:T(8,128)S(1)} %get-tuple-element.73), channel_id=1, source_target_pairs={{0,4},{1,5},{2,6},{3,7},{4,0},{5,1},{6,2},{7,3},{8,12},{9,13},{10,... | collective-permute-start | bytes 786440 | tf_op jit(solution)/shard_map/ppermute | solution.py:418
  62.4 16.9 %collective-permute-start.11 = (f32[2,128,256]{2,1,0:T(8,128)S(1)}, f32[2,128,256]{2,1,0:T(8,128)S(1)}, u32[]{:S(2)}, u32[]{:S(2)}) collective-permute-start(f32[2,128,256]{2,1,0:T(8,128)S(1)} %get-tuple-element.71), channel_id=1, source_target_pairs={{0,2},{1,3},{2,0},{3,1},{4,6},{5,7},{6,4},{7,5},{8,10},{9,11},{10,... | collective-permute-start | bytes 786440 | tf_op jit(solution)/shard_map/ppermute | solution.py:418
  64.4 17.8 %collective-permute-start.13 = (f32[2,128,256]{2,1,0:T(8,128)S(1)}, f32[2,128,256]{2,1,0:T(8,128)S(1)}, u32[]{:S(2)}, u32[]{:S(2)}) collective-permute-start(f32[2,128,256]{2,1,0:T(8,128)S(1)} %get-tuple-element.75), channel_id=1, source_target_pairs={{0,4},{1,5},{2,6},{3,7},{4,0},{5,1},{6,2},{7,3},{8,12},{9,13},{10,... | collective-permute-start | bytes 786440 | tf_op jit(solution)/shard_map/ppermute | solution.py:418
  68.9 12.4 %copy-start = (f32[1,512,1024]{2,1,0:T(8,128)S(1)}, f32[1,512,1024]{2,1,0:T(8,128)}, u32[]{:S(2)}) copy-start(f32[1,512,1024]{2,1,0:T(8,128)} %refs_4_.3) | copy-start | bytes 6291460
  69.0 12.4 %copy-start.1 = (bf16[768,64]{1,0:T(8,128)(2,1)S(1)}, bf16[768,64]{1,0:T(8,128)(2,1)}, u32[]{:S(2)}) copy-start(bf16[768,64]{1,0:T(8,128)(2,1)} %constant.28.refs_10_.refs_6_) | copy-start | bytes 294916
  69.0 12.4 %copy-start.4 = (bf16[32,384]{1,0:T(8,128)(2,1)S(1)}, bf16[32,384]{1,0:T(8,128)(2,1)}, u32[]{:S(2)}) copy-start(bf16[32,384]{1,0:T(8,128)(2,1)} %constant.23.refs_9_.refs_5_) | copy-start | bytes 73732
  77.2 22.4 %collective-permute-start.6 = (f32[2,128,512]{2,1,0:T(8,128)S(1)}, f32[2,128,512]{2,1,0:T(8,128)S(1)}, u32[]{:S(2)}, u32[]{:S(2)}) collective-permute-start(f32[2,128,512]{2,1,0:T(8,128)S(1)} %get-tuple-element.64), channel_id=1, source_target_pairs={{0,2},{1,3},{2,0},{3,1},{4,6},{5,7},{6,4},{7,5},{8,10},{9,11},{10,... | collective-permute-start | bytes 1572872 | tf_op jit(solution)/shard_map/ppermute | solution.py:418
  79.3 21.9 %collective-permute-start.7 = (f32[2,128,512]{2,1,0:T(8,128)S(1)}, f32[2,128,512]{2,1,0:T(8,128)S(1)}, u32[]{:S(2)}, u32[]{:S(2)}) collective-permute-start(f32[2,128,512]{2,1,0:T(8,128)S(1)} %get-tuple-element.66), channel_id=1, source_target_pairs={{0,4},{1,5},{2,6},{3,7},{4,0},{5,1},{6,2},{7,3},{8,12},{9,13},{10,... | collective-permute-start | bytes 1572872 | tf_op jit(solution)/shard_map/ppermute | solution.py:418
  84.0 13.7 %collective-permute-start.23 = (f32[1,128,512]{2,1,0:T(8,128)S(1)}, f32[1,128,512]{2,1,0:T(8,128)S(1)}, u32[]{:S(2)}, u32[]{:S(2)}) collective-permute-start(f32[1,128,512]{2,1,0:T(8,128)S(1)} %get-tuple-element.103), channel_id=1, source_target_pairs={{0,2},{1,3},{2,0},{3,1},{4,6},{5,7},{6,4},{7,5},{8,10},{9,11},{10,... | collective-permute-start | bytes 786440 | tf_op jit(solution)/shard_map/ppermute | solution.py:418
  85.5 17.1 %collective-permute-start.22 = (f32[1,128,512]{2,1,0:T(8,128)S(1)}, f32[1,128,512]{2,1,0:T(8,128)S(1)}, u32[]{:S(2)}, u32[]{:S(2)}) collective-permute-start(f32[1,128,512]{2,1,0:T(8,128)S(1)} %get-tuple-element.96.refs_11_), channel_id=1, source_target_pairs={{0,4},{1,5},{2,6},{3,7},{4,0},{5,1},{6,2},{7,3},{8,12},{9,13},{10,... | collective-permute-start | bytes 786440 | tf_op jit(solution)/shard_map/ppermute | solution.py:418
  86.0 18.1 %collective-permute-start.25 = (f32[2,128,256]{2,1,0:T(8,128)S(1)}, f32[2,128,256]{2,1,0:T(8,128)S(1)}, u32[]{:S(2)}, u32[]{:S(2)}) collective-permute-start(f32[2,128,256]{2,1,0:T(8,128)S(1)} %get-tuple-element.104), channel_id=1, source_target_pairs={{0,2},{1,3},{2,0},{3,1},{4,6},{5,7},{6,4},{7,5},{8,10},{9,11},{10,... | collective-permute-start | bytes 786440 | tf_op jit(solution)/shard_map/ppermute | solution.py:418
  97.7 17.0 %collective-permute-start.24 = (f32[2,128,256]{2,1,0:T(8,128)S(1)}, f32[2,128,256]{2,1,0:T(8,128)S(1)}, u32[]{:S(2)}, u32[]{:S(2)}) collective-permute-start(f32[2,128,256]{2,1,0:T(8,128)S(1)} %get-tuple-element.91.refs_11_), channel_id=1, source_target_pairs={{0,4},{1,5},{2,6},{3,7},{4,0},{5,1},{6,2},{7,3},{8,12},{9,13},{10,... | collective-permute-start | bytes 786440 | tf_op jit(solution)/shard_map/ppermute | solution.py:418
  99.7 18.7 %collective-permute-start.27 = (f32[2,128,256]{2,1,0:T(8,128)S(1)}, f32[2,128,256]{2,1,0:T(8,128)S(1)}, u32[]{:S(2)}, u32[]{:S(2)}) collective-permute-start(f32[2,128,256]{2,1,0:T(8,128)S(1)} %get-tuple-element.105), channel_id=1, source_target_pairs={{0,2},{1,3},{2,0},{3,1},{4,6},{5,7},{6,4},{7,5},{8,10},{9,11},{10,... | collective-permute-start | bytes 786440 | tf_op jit(solution)/shard_map/ppermute | solution.py:418
  101.2 17.2 %collective-permute-start.26 = (f32[2,128,256]{2,1,0:T(8,128)S(1)}, f32[2,128,256]{2,1,0:T(8,128)S(1)}, u32[]{:S(2)}, u32[]{:S(2)}) collective-permute-start(f32[2,128,256]{2,1,0:T(8,128)S(1)} %get-tuple-element.86.refs_15_), channel_id=1, source_target_pairs={{0,4},{1,5},{2,6},{3,7},{4,0},{5,1},{6,2},{7,3},{8,12},{9,13},{10,... | collective-permute-start | bytes 786440 | tf_op jit(solution)/shard_map/ppermute | solution.py:418
  101.7 17.5 %copy-start.2 = (bf16[192,256]{1,0:T(8,128)(2,1)S(1)}, bf16[192,256]{1,0:T(8,128)(2,1)}, u32[]{:S(2)}) copy-start(bf16[192,256]{1,0:T(8,128)(2,1)} %constant.38.refs_5_) | copy-start | bytes 294916
  101.7 17.5 %copy-start.3 = (bf16[128,96]{1,0:T(8,128)(2,1)S(1)}, bf16[128,96]{1,0:T(8,128)(2,1)}, u32[]{:S(2)}) copy-start(bf16[128,96]{1,0:T(8,128)(2,1)} %constant.33.refs_4_) | copy-start | bytes 73732
  102.6 8.6 %collective-permute-start.20 = (f32[128,128]{1,0:T(8,128)S(1)}, f32[128,128]{1,0:T(8,128)S(1)}, u32[]{:S(2)}, u32[]{:S(2)}) collective-permute-start(f32[128,128]{1,0:T(8,128)S(1)} %get-tuple-element.101), channel_id=1, source_target_pairs={{0,4},{1,5},{2,6},{3,7},{4,0},{5,1},{6,2},{7,3},{8,12},{9,13},{10,... | collective-permute-start | bytes 196616 | tf_op jit(solution)/shard_map/ppermute | solution.py:418
  104.1 9.1 %collective-permute-start.21 = (f32[128,128]{1,0:T(8,128)S(1)}, f32[128,128]{1,0:T(8,128)S(1)}, u32[]{:S(2)}, u32[]{:S(2)}) collective-permute-start(f32[128,128]{1,0:T(8,128)S(1)} %get-tuple-element.102), channel_id=1, source_target_pairs={{0,2},{1,3},{2,0},{3,1},{4,6},{5,7},{6,4},{7,5},{8,10},{9,11},{10,... | collective-permute-start | bytes 196616 | tf_op jit(solution)/shard_map/ppermute | solution.py:418
  111.1 15.7 %collective-permute-start.18 = (f32[1,128,512]{2,1,0:T(8,128)S(1)}, f32[1,128,512]{2,1,0:T(8,128)S(1)}, u32[]{:S(2)}, u32[]{:S(2)}) collective-permute-start(f32[1,128,512]{2,1,0:T(8,128)S(1)} %get-tuple-element.98), channel_id=1, source_target_pairs={{0,4},{1,5},{2,6},{3,7},{4,0},{5,1},{6,2},{7,3},{8,12},{9,13},{10,... | collective-permute-start | bytes 786440 | tf_op jit(solution)/shard_map/ppermute | solution.py:418
  113.2 13.7 %collective-permute-start.19 = (f32[1,128,512]{2,1,0:T(8,128)S(1)}, f32[1,128,512]{2,1,0:T(8,128)S(1)}, u32[]{:S(2)}, u32[]{:S(2)}) collective-permute-start(f32[1,128,512]{2,1,0:T(8,128)S(1)} %get-tuple-element.99), channel_id=1, source_target_pairs={{0,2},{1,3},{2,0},{3,1},{4,6},{5,7},{6,4},{7,5},{8,10},{9,11},{10,... | collective-permute-start | bytes 786440 | tf_op jit(solution)/shard_map/ppermute | solution.py:418
  114.7 8.3 %collective-permute-start.30 = (f32[128,256]{1,0:T(8,128)S(1)}, f32[128,256]{1,0:T(8,128)S(1)}, u32[]{:S(2)}, u32[]{:S(2)}) collective-permute-start(f32[128,256]{1,0:T(8,128)S(1)} %shard_map.107.refs_3_.refs_0_.refs_6_), channel_id=1, source_target_pairs={{0,24},{8,16},{16,8},{24,0},{1,25},{9,17},{17,9},{25,1},{2,26},{10... | collective-permute-start | bytes 393224 | tf_op jit(solution)/shard_map/ppermute | solution.py:418
  118.4 6.6 %collective-permute-start.29 = (f32[128,256]{1,0:T(8,128)S(1)}, f32[128,256]{1,0:T(8,128)S(1)}, u32[]{:S(2)}, u32[]{:S(2)}) collective-permute-start(f32[128,256]{1,0:T(8,128)S(1)} %shard_map.107.refs_3_.refs_0_.refs_6_), channel_id=1, source_target_pairs={{0,16},{8,24},{16,0},{24,8},{1,17},{9,25},{17,1},{25,9},{2,18},{10... | collective-permute-start | bytes 393224 | tf_op jit(solution)/shard_map/ppermute | solution.py:418
  118.4 6.6 %collective-permute-start.28 = (f32[128,256]{1,0:T(8,128)S(1)}, f32[128,256]{1,0:T(8,128)S(1)}, u32[]{:S(2)}, u32[]{:S(2)}) collective-permute-start(f32[128,256]{1,0:T(8,128)S(1)} %shard_map.107.refs_3_.refs_0_.refs_6_), channel_id=1, source_target_pairs={{0,8},{8,0},{16,24},{24,16},{1,9},{9,1},{17,25},{25,17},{2,10},{10... | collective-permute-start | bytes 393224 | tf_op jit(solution)/shard_map/ppermute | solution.py:418

commit v2 on v1

--- a/solution.py
+++ b/solution.py
@@ -9,7 +9,7 @@
 CH = 64
 BAND = 16
 EPS = 1e-05
-LATE = (5,)
+LATE = (1, 5)
 ROWS = 128
 SPAN = 256
 
@@ -89,24 +89,28 @@
 F32 = jnp.float32
 
 
-def on_chip(kernel, ins, tokens, outs, scratch=(), owners=None, flops=0, aliases=None, grant=12):
+def on_chip(kernel, ins, tokens, outs, scratch=(), owners=None, flops=0, aliases=None, far=(), grant=12):
     lead = [] if owners is None else [owners]
-    count = len(lead) + len(ins)
+    count = len(lead) + len(ins) + len(far)
+
+    outs = [out if isinstance(out[0], tuple) else (out, F32) for out in outs]
 
     def run(*refs):
         kernel(*refs[:count], *refs[count + len(tokens) :])
 
-    arrays = [pltpu.with_memory_space_constraint(a, pltpu.VMEM) for a in [*ins, *tokens]]
+    near = [pltpu.with_memory_space_constraint(a, pltpu.VMEM) for a in ins]
+    past = [pltpu.with_memory_space_constraint(a, pltpu.VMEM) for a in tokens]
+    far = [pltpu.with_memory_space_constraint(a, pltpu.HBM) for a in far]
     return pl.pallas_call(
         run,
-        out_shape=tuple(pltpu.VMEM(shape, F32) for shape in outs),
-        in_specs=[SMEM] * len(lead) + [VMEM] * len(arrays),
+        out_shape=tuple(pltpu.VMEM(shape, kind) for shape, kind in outs),
+        in_specs=[SMEM] * len(lead) + [VMEM] * len(near) + [ANY] * len(far) + [VMEM] * len(past),
         out_specs=(VMEM,) * len(outs),
         scratch_shapes=list(scratch),
         input_output_aliases={len(lead) + i: o for i, o in (aliases or {}).items()},
         compiler_params=pltpu.CompilerParams(vmem_limit_bytes=grant << 20),
         cost_estimate=cost(flops, 0),
-    )(*lead, *arrays)
+    )(*lead, *near, *far, *past)
 
 
 def fill(xt_ref, x_ref, scale_ref, starts, r):
@@ -126,9 +130,126 @@
     tokens, width = x.shape
     cols = c.shape[1]
     half = n // 2
-    tile = 128
+    tile = 256
     group = 64
-    tiles = tokens // tile
+    steps = tokens // tile
+    parts = [columns(side, cols, q, w) for side in range(2)]
+
+    def kernel(own, x_hbm, c_hbm, x_ref, c_ref, s_ref, p_ref, xt_ref, x_sem, c_sem):
+        def rows_at(i):
+            return pl.ds(pl.multiple_of(i * tile, tile), tile)
+
+        def piece(i):
+            at = rows_at(i)
+            return pltpu.make_async_copy(x_hbm.at[at, :], x_ref.at[at, :], x_sem.at[i])
+
+        def begin(i, _):
+            piece(i).start()
+            return 0
+
+        def scales(i):
+            out = []
+            for g in range(0, tile, group):
+                at = pl.ds(pl.multiple_of(i * tile + g, group), group)
+                total = jnp.zeros((group, 128), F32)
+                for s in range(0, width, 128):
+                    v = x_ref[at, s : s + 128].astype(F32)
+                    total = total + v * v
+                stat = jnp.sum(total, axis=1, keepdims=True) / width
+                out.append(jnp.broadcast_to(lax.rsqrt(stat + EPS), (group, 128)))
+            return jnp.concatenate(out, axis=0)
+
+        def turn(i, now):
+            at = rows_at(i)
+            for j in range(half):
+                lanes = pl.ds(pl.multiple_of(own[2 * j + 1] * rows + off, 128), r)
+                value = (x_ref[at, lanes].astype(F32) * now).astype(jnp.bfloat16)
+                xt_ref[j * r : (j + 1) * r, at] = value.T
+
+        def both(i, _):
+            piece(i + 1).wait()
+            now = s_ref[rows_at(i), :]
+            later = scales(i + 1)
+            turn(i, now)
+            s_ref[rows_at(i + 1), :] = later
+            return 0
+
+        near = [
+            pltpu.make_async_copy(c_hbm.at[:, at], c_ref.at[:, at], c_sem.at[side])
+            for side, at in enumerate(parts)
+        ]
+        for copy in near:
+            copy.start()
+        lax.fori_loop(0, steps, begin, 0)
+        piece(0).wait()
+        s_ref[rows_at(0), :] = scales(0)
+        lax.fori_loop(0, steps - 2, both, 0)
+        for copy in near:
+            copy.wait()
+        cut = (steps - 2) * tile
+        for side in range(2):
+            p_ref[:, :, side * w : (side + 1) * w] = jnp.dot(
+                xt_ref[:, :cut], c_ref[:cut, parts[side]], preferred_element_type=F32
+            ).reshape(half, r, w)
+        both(steps - 2, 0)
+        turn(steps - 1, s_ref[rows_at(steps - 1), :])
+        for side in range(2):
+            p_ref[:, :, side * w : (side + 1) * w] += jnp.dot(
+                xt_ref[:, cut:], c_ref[cut:, parts[side]], preferred_element_type=F32
+            ).reshape(half, r, w)
+
+    return pl.pallas_call(
+        kernel,
+        out_shape=(
+            pltpu.VMEM(x.shape, x.dtype),
+            pltpu.VMEM(c.shape, c.dtype),
+            pltpu.VMEM((tokens, 128), F32),
+            pltpu.VMEM((half, r, 2 * w), F32),
+            pltpu.VMEM((half * r, tokens), jnp.bfloat16),
+        ),
+        in_specs=[SMEM, ANY, ANY],
+        out_specs=(VMEM,) * 5,
+        scratch_shapes=[
+            pltpu.SemaphoreType.DMA((steps,)),
+            pltpu.SemaphoreType.DMA((2,)),
+        ],
+        compiler_params=pltpu.CompilerParams(vmem_limit_bytes=12 << 20),
+        cost_estimate=cost(4 * tokens * half * r * w, 2 * tokens * (width + cols)),
+        name="first",
+    )(owners, *[pltpu.with_memory_space_constraint(a, pltpu.HBM) for a in (x, c)])
+
+
+def product_call(x, scale, c, owners, n, rows, chunk, parity, xt, tokens):
+    off, q, w = chunk
+    r = ROWS
+    cols = c.shape[1]
+    half = n // 2
+
+    def multiply(xt_ref, c_ref, out_ref):
+        for side in range(2):
+            out_ref[:, :, side * w : (side + 1) * w] = jnp.dot(
+                xt_ref[...], c_ref[:, columns(side, cols, q, w)], preferred_element_type=F32
+            ).reshape(half, r, w)
+
+    def kernel(own, x_ref, s_ref, c_ref, out_ref, xt_ref):
+        fill(xt_ref, x_ref, s_ref, [own[2 * j + parity] * rows + off for j in range(half)], r)
+        multiply(xt_ref, c_ref, out_ref)
+
+    shape = (half, r, 2 * w)
+    flops = 4 * x.shape[0] * half * r * w
+    if xt is not None:
+        (out,) = on_chip(multiply, [xt, c], tokens, [shape], flops=flops)
+        return out, xt
+    return on_chip(
+        kernel, [x, scale, c], tokens,
+        [shape, ((half * r, x.shape[0]), jnp.bfloat16)], owners=owners, flops=flops,
+    )
+
+
+def second_call(x, scale, c, c_hbm, owners, n, rows, chunk, tokens):
+    off, q, w = chunk
+    cols = c.shape[1]
+    half = n // 2
     parts = [columns(side, cols, q, w) for side in range(2)]
     others = [
         slice(lo, hi)
@@ -137,83 +258,27 @@
         if lo < hi
     ]
 
-    def kernel(own, x_hbm, c_hbm, x_ref, c_ref, s_ref, p_ref, xt_ref, x_sem, c_sem):
-        def piece(i):
-            at = pl.ds(pl.multiple_of(i * tile, tile), tile)
-            return pltpu.make_async_copy(x_hbm.at[at, :], x_ref.at[at, :], x_sem.at[i])
-
-        def begin(i, _):
-            piece(i).start()
-            return 0
-
-        def scale(i, _):
-            piece(i).wait()
-            for g in range(0, tile, group):
-                at = pl.ds(pl.multiple_of(i * tile + g, group), group)
-                total = jnp.zeros((group, 128), F32)
-                for s in range(0, width, 128):
-                    v = x_ref[at, s : s + 128].astype(F32)
-                    total = total + v * v
-                stat = jnp.sum(total, axis=1, keepdims=True) / width
-                s_ref[at, :] = jnp.broadcast_to(lax.rsqrt(stat + EPS), (group, 128))
-            return 0
-
-        lax.fori_loop(0, tiles, begin, 0)
+    def kernel(own, x_ref, s_ref, old_ref, from_ref, out_ref, c_ref, xt_ref, sem):
         rest = [
-            pltpu.make_async_copy(c_hbm.at[:, at], c_ref.at[:, at], c_sem.at[k])
-            for k, at in enumerate(parts + others)
+            pltpu.make_async_copy(from_ref.at[:, at], c_ref.at[:, at], sem.at[k])
+            for k, at in enumerate(others)
         ]
         for copy in rest:
             copy.start()
-        lax.fori_loop(0, tiles, scale, 0)
-        fill(xt_ref, x_ref, s_ref, [own[2 * j + 1] * rows + off for j in range(half)], r)
-        for side in range(2):
-            rest[side].wait()
-            p_ref[:, :, side * w : (side + 1) * w] = jnp.dot(
-                xt_ref[...], c_ref[:, parts[side]], preferred_element_type=F32
-            ).reshape(half, r, w)
-        for copy in rest[2:]:
-            copy.wait()
-
-    return pl.pallas_call(
-        kernel,
-        out_shape=(
-            pltpu.VMEM(x.shape, x.dtype),
-            pltpu.VMEM(c.shape, c.dtype),
-            pltpu.VMEM((tokens, 128), F32),
-            pltpu.VMEM((half, r, 2 * w), F32),
-        ),
-        in_specs=[SMEM, ANY, ANY],
-        out_specs=(VMEM,) * 4,
-        scratch_shapes=[
-            pltpu.VMEM((half * r, tokens), jnp.bfloat16),
-            pltpu.SemaphoreType.DMA((tiles,)),
-            pltpu.SemaphoreType.DMA((2 + len(others),)),
-        ],
-        compiler_params=pltpu.CompilerParams(vmem_limit_bytes=12 << 20),
-        cost_estimate=cost(4 * tokens * half * r * w, 2 * tokens * (width + cols)),
-        name="first",
-    )(owners, *[pltpu.with_memory_space_constraint(a, pltpu.HBM) for a in (x, c)])
-
-
-def product_call(x, scale, c, owners, n, rows, chunk, parity, tokens):
-    off, q, w = chunk
-    r = ROWS
-    cols = c.shape[1]
-    half = n // 2
-
-    def kernel(own, x_ref, s_ref, c_ref, out_ref, xt_ref):
-        fill(xt_ref, x_ref, s_ref, [own[2 * j + parity] * rows + off for j in range(half)], r)
+        fill(xt_ref, x_ref, s_ref, [own[2 * j] * rows + off for j in range(half)], ROWS)
         for side in range(2):
             out_ref[:, :, side * w : (side + 1) * w] = jnp.dot(
-                xt_ref[...], c_ref[:, columns(side, cols, q, w)], preferred_element_type=F32
-            ).reshape(half, r, w)
-
-    (out,) = on_chip(
-        kernel, [x, scale, c], tokens, [(half, r, 2 * w)],
-        [pltpu.VMEM((half * r, x.shape[0]), jnp.bfloat16)], owners, 4 * x.shape[0] * half * r * w,
-    )
-    return out
+                xt_ref[...], c_ref[:, parts[side]], preferred_element_type=F32
+            ).reshape(half, ROWS, w)
+        for copy in rest:
+            copy.wait()
+
+    return on_chip(
+        kernel, [x, scale, c], tokens,
+        [(half, ROWS, 2 * w), (c.shape, c.dtype), ((half * ROWS, x.shape[0]), x.dtype)],
+        [pltpu.SemaphoreType.DMA((max(len(others), 1),))], owners, 4 * c.shape[0] * half * ROWS * w,
+        aliases={2: 1}, far=[c_hbm],
+    )
 
 
 def part_call(even, got, sends, keeps, tokens):
@@ -369,26 +434,37 @@
     )
 
 
-def finish_call(own, a, b, bands, consts, chunks, before, tokens):
+def settle_call(own, bands, consts, tokens):
+    def kernel(own_ref, g_ref, left_ref, right_ref, out_ref):
+        for k, taken in enumerate(expand(g_ref[...], left_ref[...], right_ref[...])):
+            at = slice(k * ROWS, (k + 1) * ROWS)
+            out_ref[at, :] = own_ref[at, :] - taken
+
+    return on_chip(
+        kernel, [own, bands, consts["expand_left"], consts["expand_right"]], tokens,
+        [own.shape], flops=6 * own.size * 128, aliases={0: 0},
+    )[0]
+
+
+def finish_call(own, a, b, chunks, before, tokens):
     rows, cols = own.shape
-    low = ROWS * BAND // CH
     off, _, w = chunks[0]
-
-    def kernel(buf, send, own_ref, a_ref, b_ref, g_ref, left_ref, right_ref):
-        picked = g_ref[off * BAND // CH : off * BAND // CH + low, :]
-        (taken,) = expand(picked, left_ref[...], right_ref[...])
-        for side, ref in enumerate((a_ref, b_ref)):
-            for k, (_, q, _) in enumerate(chunks):
-                at = columns(side, cols, q, w)
-                buf[0, :, at] = own_ref[off : off + ROWS, at] + ref[k] - taken[:, at]
-        index = (0, pl.ds(off, ROWS))
-        send(0, index)
-        return [index]
-
-    return outward(
-        kernel, [own, a, b, bands, consts["expand_left"], consts["expand_right"]], tokens,
-        (1, rows, cols), 1, (ROWS, cols), 6 * ROWS * cols * 128, before,
-    )
+    parts = 2
+    step = ROWS // parts
+
+    def kernel(buf, send, own_ref, a_ref, b_ref):
+        indices = []
+        for part in range(parts):
+            lo = part * step
+            for side, ref in enumerate((a_ref, b_ref)):
+                for k, (_, q, _) in enumerate(chunks):
+                    at = columns(side, cols, q, w)
+                    buf[part, :, at] = own_ref[off + lo : off + lo + step, at] + ref[k, lo : lo + step]
+            indices.append((0, pl.ds(off + lo, step)))
+            send(part, indices[part])
+        return indices
+
+    return outward(kernel, [own, a, b], tokens, (1, rows, cols), parts, (step, cols), 0, before)
 
 
 def chunks_of(rows, wide):
@@ -419,22 +495,37 @@
 
     row_groups = chunks_of(rows, wide)
     chunks = [chunk for group in row_groups for chunk in group]
-    x, c, scale, odd = first_call(x, c, owners, n, rows, chunks[0])
+    c_hbm = c
+    x, c, scale, odd, xt = first_call(x, c, owners, n, rows, chunks[0])
     token = odd
+    kept = {(1, chunks[0][0]): xt}
+
+    def product(k, parity):
+        at = parity, chunks[k][0]
+        out, kept[at] = product_call(
+            x, scale, c, owners, n, rows, chunks[k], parity, kept.get(at), [token]
+        )
+        return out
+
     got = swap(odd, 1)
     state = []
     for k, chunk in enumerate(chunks):
-        even = product_call(x, scale, c, owners, n, rows, chunk, 0, [token])
+        if k == 0:
+            even, c, kept[0, chunk[0]] = second_call(
+                x, scale, c, c_hbm, owners, n, rows, chunk, [token]
+            )
+        else:
+            even = product(k, 0)
         token = even
         here = got
         if k + 1 < len(chunks) and k + 1 not in LATE:
-            odd = product_call(x, scale, c, owners, n, rows, chunks[k + 1], 1, [token])
+            odd = product(k + 1, 1)
             token = odd
             got = swap(odd, 1)
         outs = part_call(even, here, sends, keeps, [token])
         token = outs[1]
         if k + 1 < len(chunks) and k + 1 in LATE:
-            odd = product_call(x, scale, c, owners, n, rows, chunks[k + 1], 1, [token])
+            odd = product(k + 1, 1)
             token = odd
             got = swap(odd, 1)
         terms = []
@@ -471,13 +562,13 @@
     band_b = swap(before[2], ends[1])
     mine = join_call(before[3], band_a, band_b)
     every = [mine] + [swap(mine, k, "rep", groups) for k in range(1, groups)]
+    settled = settle_call(before[0], mine, consts, [])
     nexts = None
-    token = mine
     final = len(row_groups) - 1
     for g, group in enumerate(row_groups):
         if g == final:
-            update = update_call(every, consts, rows, cols, [token])
-        nexts = finish_call(before[0], *bulk[g], mine, consts, group, nexts, [])
+            update = update_call(every, consts, rows, cols, [settled])
+        nexts = finish_call(settled, *bulk[g], group, nexts, [])
     return nexts, update
 
 
@@ -511,7 +602,7 @@
 
     def body(activations, cotangent, momentum):
         rows, cols = momentum.shape[1:]
-        good = fits and rows % ROWS == 0 and cols % (4 * SPAN) == 0 and activations.shape[1] % 256 == 0
+        good = fits and rows % ROWS == 0 and cols % (4 * SPAN) == 0 and activations.shape[1] % 512 == 0
         return (fast_body if good else plain_body)(n, groups, activations, cotangent, momentum)
 
     return jax.shard_map(

time: 128 us -> 125 us (0.977)
  Pallas kernels: 47 us -> 43 us
    pallas_call x5, Pallas kernels: 6.95 us -> 5.27 us  [outward(): pl.pallas_call(run, out_shape=jax.ShapeDtypeStruct(shape, F32), in_specs=...]
    pallas_call x22 -> x23, Pallas kernels: 29.9 us -> 28.9 us  [on_chip(): pl.pallas_call(run, out_shape=tuple((pltpu.VMEM(shape, kind) for shape, k...]
  transfers between devices with their start and end apart: 31 -> 31, of which waited for: 8 -> 9; matrix products, arithmetic and copies ran while one was open for 0% -> 0% of each run, Pallas kernels for 21% -> 19%
where the time goes in v2:
time: 125 us
  waiting for transfers between devices  44.1 us (35%)
  Pallas kernels  43 us (34%)
  starting transfers between devices  36.4 us (29%)
    ppermute x31, waiting for transfers between devices, swap(): return lax.ppermute(value, axis, [(i, i ^ bit) for i in range(size)])  44.1 us
    ppermute x31, starting transfers between devices, swap(): return lax.ppermute(value, axis, [(i, i ^ bit) for i in range(size)])  36.4 us
    pallas_call x23, Pallas kernels, on_chip(): pl.pallas_call(run, out_shape=tuple((pltpu.VMEM(shape, kind) for shape, k...  28.9 us
    pallas_call x1, Pallas kernels, first_call(): pl.pallas_call(kernel, out_shape=(pltpu.VMEM(x.shape, x.dtype), pltpu.VME...  8.91 us
    pallas_call x5, Pallas kernels, outward(): pl.pallas_call(run, out_shape=jax.ShapeDtypeStruct(shape, F32), in_specs=...  5.27 us
  transfers between devices with their start and end apart: 31, of which 9 were waited for; matrix products, arithmetic and copies ran while one was open for 0% of the time, Pallas kernels for 19%

profile of v2, /device:TPU:0, one launch (start us, length us, event | category | flops | bytes accessed | tf_op | source)
XLA Modules:
  0.0 124.6 jit_solution(16293757133497231596)
XLA Ops:
  0.6 8.9 %first.1 = (bf16[2048,4096]{1,0:T(8,128)(2,1)S(1)}, bf16[2048,1024]{1,0:T(8,128)(2,1)S(1)}, f32[2048,128]{1,0:T(8,128)S(1)}, f32[4,128,512]{2,1,0:T(8,128)S(1)}, bf16[512,2048]{1,0:T(8,128)(2,1)S(1)}) custom-call(s32[8]{0:T(128)S(1)} %iota_xor_fusion.own.refs_0_, bf16[2048,4096]{1,0:T(8,128)(2,1)} %bitcast.2, bf16[2048,1024]{1,0:T(8,128)(2,1)} %bitcast.3), custom_call_target="tpu_custom_call" | custom-call | flops 1073741824 | bytes 20971520 | tf_op jit(solution)/shard_map/first/pallas_call | solution.py:201
  9.6 0.6 collective-permute-start
  10.1 2.1 %shard_map.86 = (f32[4,128,512]{2,1,0:T(8,128)S(1)}, bf16[2048,1024]{1,0:T(8,128)(2,1)S(1)}, bf16[512,2048]{1,0:T(8,128)(2,1)S(1)}) custom-call(s32[8]{0:T(128)S(1)} %iota_xor_fusion.own.refs_0_, bf16[2048,4096]{1,0:T(8,128)(2,1)S(1)} %get-tuple-element.66.refs_1_, f32[2048,128]{1,0:T(8,128)S(1)} %get-tuple-element.67.refs_2_, ...), custom_call_target="tpu_custom_call", output_to_operand_aliasing={{1}: (3, {})} | custom-call | flops 1073741824 | tf_op jit(solution)/shard_map/pallas_call | solution.py:104
  12.3 0.1 collective-permute-done.refs_1_
  12.4 0.1 shard_map.87
  12.5 1.2 shard_map.88.refs_2_
  13.8 0.4 collective-permute-start.1
  14.2 1.3 %shard_map.89.refs_4_.refs_0_ = f32[4,128,512]{2,1,0:T(8,128)S(1)} custom-call(bf16[512,2048]{1,0:T(8,128)(2,1)S(1)} %get-tuple-element.71.refs_0_, bf16[2048,1024]{1,0:T(8,128)(2,1)S(1)} %get-tuple-element.70.refs_1_.refs_3_, f32[4,128,512]{2,1,0:T(8,128)S(1)} %shard_map.88.refs_2_), custom_call_target="tpu_custom_call" | custom-call | flops 1073741824 | tf_op jit(solution)/shard_map/pallas_call | solution.py:104
  15.5 1.9 %shard_map.90 = (f32[4,128,512]{2,1,0:T(8,128)S(1)}, bf16[512,2048]{1,0:T(8,128)(2,1)S(1)}) custom-call(s32[8]{0:T(128)S(1)} %iota_xor_fusion.own.refs_0_, bf16[2048,4096]{1,0:T(8,128)(2,1)S(1)} %get-tuple-element.66.refs_1_, f32[2048,128]{1,0:T(8,128)S(1)} %get-tuple-element.67.refs_2_, bf16[2048,1024]{1,0:T(8,128)(2,1)S(1)} %get-tuple-element.70.refs_1_.refs_3_, ...), custom_call_target="tpu_custom_call" | custom-call | flops 1073741824 | tf_op jit(solution)/shard_map/pallas_call | solution.py:104
  17.4 0.2 collective-permute-start.2
  17.6 0.1 shard_map.91
  17.8 1.9 %shard_map.92 = (f32[4,128,512]{2,1,0:T(8,128)S(1)}, bf16[512,2048]{1,0:T(8,128)(2,1)S(1)}) custom-call(s32[8]{0:T(128)S(1)} %iota_xor_fusion.own.refs_0_, bf16[2048,4096]{1,0:T(8,128)(2,1)S(1)} %get-tuple-element.66.refs_1_, f32[2048,128]{1,0:T(8,128)S(1)} %get-tuple-element.67.refs_2_, bf16[2048,1024]{1,0:T(8,128)(2,1)S(1)} %get-tuple-element.70.refs_1_.refs_3_, ...), custom_call_target="tpu_custom_call" | custom-call | flops 1073741824 | tf_op jit(solution)/shard_map/pallas_call | solution.py:104
  19.7 1.2 shard_map.93.refs_2_
  21.0 0.1 shard_map.94
  21.1 1.3 %shard_map.95.refs_4_.refs_0_ = f32[4,128,512]{2,1,0:T(8,128)S(1)} custom-call(bf16[512,2048]{1,0:T(8,128)(2,1)S(1)} %get-tuple-element.77.refs_0_, bf16[2048,1024]{1,0:T(8,128)(2,1)S(1)} %get-tuple-element.70.refs_1_.refs_3_, f32[2,128,256]{2,1,0:T(8,128)S(1)} %get-tuple-element.80.refs_2_.refs_0_), custom_call_target="tpu_custom_call" | custom-call | flops 1073741824 | tf_op jit(solution)/shard_map/pallas_call | solution.py:104
  22.4 3.0 %shard_map.96 = (f32[4,128,1024]{2,1,0:T(8,128)S(1)}, bf16[512,2048]{1,0:T(8,128)(2,1)}) custom-call(s32[8]{0:T(128)S(1)} %iota_xor_fusion.own.refs_0_, bf16[2048,4096]{1,0:T(8,128)(2,1)S(1)} %get-tuple-element.66.refs_1_, f32[2048,128]{1,0:T(8,128)S(1)} %get-tuple-element.67.refs_2_, bf16[2048,1024]{1,0:T(8,128)(2,1)S(1)} %get-tuple-element.70.refs_1_.refs_3_, ...), custom_call_target="tpu_custom_call" | custom-call | flops 2147483648 | tf_op jit(solution)/shard_map/pallas_call | solution.py:104
  25.4 0.4 collective-permute-start.4
  25.9 5.2 %collective-permute-done.3.refs_1_ = f32[4,128,512]{2,1,0:T(8,128)S(1)} collective-permute-done((f32[4,128,512]{2,1,0:T(8,128)S(1)}, f32[4,128,512]{2,1,0:T(8,128)S(1)}, u32[]{:S(2)}, u32[]{:S(2)}) %collective-permute-start.3) | collective-permute-done | bytes 1048608 | tf_op jit(solution)/shard_map/ppermute | solution.py:494
  31.1 0.1 shard_map.97
  31.3 3.0 %shard_map.98 = (f32[4,128,1024]{2,1,0:T(8,128)S(1)}, bf16[512,2048]{1,0:T(8,128)(2,1)}) custom-call(s32[8]{0:T(128)S(1)} %iota_xor_fusion.own.refs_0_, bf16[2048,4096]{1,0:T(8,128)(2,1)S(1)} %get-tuple-element.66.refs_1_, f32[2048,128]{1,0:T(8,128)S(1)} %get-tuple-element.67.refs_2_, bf16[2048,1024]{1,0:T(8,128)(2,1)S(1)} %get-tuple-element.70.refs_1_.refs_3_, ...), custom_call_target="tpu_custom_call" | custom-call | flops 2147483648 | tf_op jit(solution)/shard_map/pallas_call | solution.py:104
  34.3 0.5 shard_map.99
  34.8 3.0 %shard_map.100 = (f32[4,128,1024]{2,1,0:T(8,128)S(1)}, bf16[512,2048]{1,0:T(8,128)(2,1)}) custom-call(s32[8]{0:T(128)S(1)} %iota_xor_fusion.own.refs_0_, bf16[2048,4096]{1,0:T(8,128)(2,1)S(1)} %get-tuple-element.66.refs_1_, f32[2048,128]{1,0:T(8,128)S(1)} %get-tuple-element.67.refs_2_, bf16[2048,1024]{1,0:T(8,128)(2,1)S(1)} %get-tuple-element.70.refs_1_.refs_3_, ...), custom_call_target="tpu_custom_call" | custom-call | flops 2147483648 | tf_op jit(solution)/shard_map/pallas_call | solution.py:104
  37.8 0.4 collective-permute-start.5
  38.2 2.6 %collective-permute-start.14 = (f32[2,128,256]{2,1,0:T(8,128)S(1)}, f32[2,128,256]{2,1,0:T(8,128)S(1)}, u32[]{:S(2)}, u32[]{:S(2)}) collective-permute-start(f32[2,128,256]{2,1,0:T(8,128)S(1)} %get-tuple-element.100), channel_id=1, source_target_pairs={{0,2},{1,3},{2,0},{3,1},{4,6},{5,7},{6,4},{7,5},{8,10},{9,11},{10,... | collective-permute-start | bytes 786440 | tf_op jit(solution)/shard_map/ppermute | solution.py:494
  40.8 1.5 %collective-permute-start.16 = (f32[2,128,256]{2,1,0:T(8,128)S(1)}, f32[2,128,256]{2,1,0:T(8,128)S(1)}, u32[]{:S(2)}, u32[]{:S(2)}) collective-permute-start(f32[2,128,256]{2,1,0:T(8,128)S(1)} %get-tuple-element.103), channel_id=1, source_target_pairs={{0,4},{1,5},{2,6},{3,7},{4,0},{5,1},{6,2},{7,3},{8,12},{9,13},{10,... | collective-permute-start | bytes 786440 | tf_op jit(solution)/shard_map/ppermute | solution.py:494
  42.3 0.5 collective-permute-start.15
  42.8 5.1 %collective-permute-done.14.refs_1_ = f32[2,128,256]{2,1,0:T(8,128)S(1)} collective-permute-done((f32[2,128,256]{2,1,0:T(8,128)S(1)}, f32[2,128,256]{2,1,0:T(8,128)S(1)}, u32[]{:S(2)}, u32[]{:S(2)}) %collective-permute-start.14) | collective-permute-done | bytes 262176 | tf_op jit(solution)/shard_map/ppermute | solution.py:494
  47.9 2.0 %collective-permute-start.10 = (f32[2,128,256]{2,1,0:T(8,128)S(1)}, f32[2,128,256]{2,1,0:T(8,128)S(1)}, u32[]{:S(2)}, u32[]{:S(2)}) collective-permute-start(f32[2,128,256]{2,1,0:T(8,128)S(1)} %get-tuple-element.94), channel_id=1, source_target_pairs={{0,2},{1,3},{2,0},{3,1},{4,6},{5,7},{6,4},{7,5},{8,10},{9,11},{10,... | collective-permute-start | bytes 786440 | tf_op jit(solution)/shard_map/ppermute | solution.py:494
  50.0 3.6 %collective-permute-done.15.refs_3_ = f32[2,128,256]{2,1,0:T(8,128)S(1)} collective-permute-done((f32[2,128,256]{2,1,0:T(8,128)S(1)}, f32[2,128,256]{2,1,0:T(8,128)S(1)}, u32[]{:S(2)}, u32[]{:S(2)}) %collective-permute-start.15) | collective-permute-done | bytes 262176 | tf_op jit(solution)/shard_map/ppermute | solution.py:494
  53.5 2.1 %collective-permute-start.9 = (f32[2,128,512]{2,1,0:T(8,128)S(1)}, f32[2,128,512]{2,1,0:T(8,128)S(1)}, u32[]{:S(2)}, u32[]{:S(2)}) collective-permute-start(f32[2,128,512]{2,1,0:T(8,128)S(1)} %get-tuple-element.93), channel_id=1, source_target_pairs={{0,4},{1,5},{2,6},{3,7},{4,0},{5,1},{6,2},{7,3},{8,12},{9,13},{10,... | collective-permute-start | bytes 1572872 | tf_op jit(solution)/shard_map/ppermute | solution.py:494
  55.6 0.6 collective-permute-start.12
  56.2 2.9 %collective-permute-done.10.refs_1_ = f32[2,128,256]{2,1,0:T(8,128)S(1)} collective-permute-done((f32[2,128,256]{2,1,0:T(8,128)S(1)}, f32[2,128,256]{2,1,0:T(8,128)S(1)}, u32[]{:S(2)}, u32[]{:S(2)}) %collective-permute-start.10) | collective-permute-done | bytes 262176 | tf_op jit(solution)/shard_map/ppermute | solution.py:494
  59.2 2.0 %collective-permute-start.11 = (f32[2,128,256]{2,1,0:T(8,128)S(1)}, f32[2,128,256]{2,1,0:T(8,128)S(1)}, u32[]{:S(2)}, u32[]{:S(2)}) collective-permute-start(f32[2,128,256]{2,1,0:T(8,128)S(1)} %get-tuple-element.95), channel_id=1, source_target_pairs={{0,2},{1,3},{2,0},{3,1},{4,6},{5,7},{6,4},{7,5},{8,10},{9,11},{10,... | collective-permute-start | bytes 786440 | tf_op jit(solution)/shard_map/ppermute | solution.py:494
  61.2 1.5 %collective-permute-start.13 = (f32[2,128,256]{2,1,0:T(8,128)S(1)}, f32[2,128,256]{2,1,0:T(8,128)S(1)}, u32[]{:S(2)}, u32[]{:S(2)}) collective-permute-start(f32[2,128,256]{2,1,0:T(8,128)S(1)} %get-tuple-element.99), channel_id=1, source_target_pairs={{0,4},{1,5},{2,6},{3,7},{4,0},{5,1},{6,2},{7,3},{8,12},{9,13},{10,... | collective-permute-start | bytes 786440 | tf_op jit(solution)/shard_map/ppermute | solution.py:494
  62.7 3.1 %shard_map.101 = (f32[4,128,1024]{2,1,0:T(8,128)S(1)}, bf16[512,2048]{1,0:T(8,128)(2,1)}) custom-call(s32[8]{0:T(128)S(1)} %iota_xor_fusion.own.refs_0_, bf16[2048,4096]{1,0:T(8,128)(2,1)S(1)} %get-tuple-element.66.refs_1_, f32[2048,128]{1,0:T(8,128)S(1)} %get-tuple-element.67.refs_2_, bf16[2048,1024]{1,0:T(8,128)(2,1)S(1)} %get-tuple-element.70.refs_1_.refs_3_, ...), custom_call_target="tpu_custom_call" | custom-call | flops 2147483648 | tf_op jit(solution)/shard_map/pallas_call | solution.py:104
  65.8 0.3 shard_map.102
  66.1 7.9 %collective-permute-done.12.refs_5_ = f32[2,128,256]{2,1,0:T(8,128)S(1)} collective-permute-done((f32[2,128,256]{2,1,0:T(8,128)S(1)}, f32[2,128,256]{2,1,0:T(8,128)S(1)}, u32[]{:S(2)}, u32[]{:S(2)}) %collective-permute-start.12) | collective-permute-done | bytes 262176 | tf_op jit(solution)/shard_map/ppermute | solution.py:494
  74.0 2.0 %collective-permute-start.6 = (f32[2,128,512]{2,1,0:T(8,128)S(1)}, f32[2,128,512]{2,1,0:T(8,128)S(1)}, u32[]{:S(2)}, u32[]{:S(2)}) collective-permute-start(f32[2,128,512]{2,1,0:T(8,128)S(1)} %get-tuple-element.88), channel_id=1, source_target_pairs={{0,2},{1,3},{2,0},{3,1},{4,6},{5,7},{6,4},{7,5},{8,10},{9,11},{10,... | collective-permute-start | bytes 1572872 | tf_op jit(solution)/shard_map/ppermute | solution.py:494
  76.0 2.1 %collective-permute-start.7 = (f32[2,128,512]{2,1,0:T(8,128)S(1)}, f32[2,128,512]{2,1,0:T(8,128)S(1)}, u32[]{:S(2)}, u32[]{:S(2)}) collective-permute-start(f32[2,128,512]{2,1,0:T(8,128)S(1)} %get-tuple-element.90), channel_id=1, source_target_pairs={{0,4},{1,5},{2,6},{3,7},{4,0},{5,1},{6,2},{7,3},{8,12},{9,13},{10,... | collective-permute-start | bytes 1572872 | tf_op jit(solution)/shard_map/ppermute | solution.py:494
  78.1 0.9 shard_map.103
  79.0 0.9 shard_map.104
  79.9 0.9 shard_map.105
  80.7 1.5 %collective-permute-start.23 = (f32[1,128,512]{2,1,0:T(8,128)S(1)}, f32[1,128,512]{2,1,0:T(8,128)S(1)}, u32[]{:S(2)}, u32[]{:S(2)}) collective-permute-start(f32[1,128,512]{2,1,0:T(8,128)S(1)} %get-tuple-element.127), channel_id=1, source_target_pairs={{0,2},{1,3},{2,0},{3,1},{4,6},{5,7},{6,4},{7,5},{8,10},{9,11},{10,... | collective-permute-start | bytes 786440 | tf_op jit(solution)/shard_map/ppermute | solution.py:494
  82.2 0.6 collective-permute-start.22
  82.8 0.5 collective-permute-start.25
  83.4 11.0 %collective-permute-done.23.refs_2_ = f32[1,128,512]{2,1,0:T(8,128)S(1)} collective-permute-done((f32[1,128,512]{2,1,0:T(8,128)S(1)}, f32[1,128,512]{2,1,0:T(8,128)S(1)}, u32[]{:S(2)}, u32[]{:S(2)}) %collective-permute-start.23) | collective-permute-done | bytes 262176 | tf_op jit(solution)/shard_map/ppermute | solution.py:494
  94.4 2.0 %collective-permute-start.24 = (f32[2,128,256]{2,1,0:T(8,128)S(1)}, f32[2,128,256]{2,1,0:T(8,128)S(1)}, u32[]{:S(2)}, u32[]{:S(2)}) collective-permute-start(f32[2,128,256]{2,1,0:T(8,128)S(1)} %get-tuple-element.115.refs_11_), channel_id=1, source_target_pairs={{0,4},{1,5},{2,6},{3,7},{4,0},{5,1},{6,2},{7,3},{8,12},{9,13},{10,... | collective-permute-start | bytes 786440 | tf_op jit(solution)/shard_map/ppermute | solution.py:494
  96.4 1.5 %collective-permute-start.27 = (f32[2,128,256]{2,1,0:T(8,128)S(1)}, f32[2,128,256]{2,1,0:T(8,128)S(1)}, u32[]{:S(2)}, u32[]{:S(2)}) collective-permute-start(f32[2,128,256]{2,1,0:T(8,128)S(1)} %get-tuple-element.129), channel_id=1, source_target_pairs={{0,2},{1,3},{2,0},{3,1},{4,6},{5,7},{6,4},{7,5},{8,10},{9,11},{10,... | collective-permute-start | bytes 786440 | tf_op jit(solution)/shard_map/ppermute | solution.py:494
  97.9 0.5 collective-permute-start.26
  98.4 0.9 shard_map.106
  99.3 1.5 %collective-permute-start.18 = (f32[128,128]{1,0:T(8,128)S(1)}, f32[128,128]{1,0:T(8,128)S(1)}, u32[]{:S(2)}, u32[]{:S(2)}) collective-permute-start(f32[128,128]{1,0:T(8,128)S(1)} %get-tuple-element.123), channel_id=1, source_target_pairs={{0,4},{1,5},{2,6},{3,7},{4,0},{5,1},{6,2},{7,3},{8,12},{9,13},{10,... | collective-permute-start | bytes 196616 | tf_op jit(solution)/shard_map/ppermute | solution.py:494
  100.8 1.2 collective-permute-start.19
  102.0 5.9 %collective-permute-done.18.refs_1_ = f32[128,128]{1,0:T(8,128)S(1)} collective-permute-done((f32[128,128]{1,0:T(8,128)S(1)}, f32[128,128]{1,0:T(8,128)S(1)}, u32[]{:S(2)}, u32[]{:S(2)}) %collective-permute-start.18) | collective-permute-done | bytes 65568 | tf_op jit(solution)/shard_map/ppermute | solution.py:494
  107.9 2.0 %collective-permute-start.20 = (f32[1,128,512]{2,1,0:T(8,128)S(1)}, f32[1,128,512]{2,1,0:T(8,128)S(1)}, u32[]{:S(2)}, u32[]{:S(2)}) collective-permute-start(f32[1,128,512]{2,1,0:T(8,128)S(1)} %get-tuple-element.125), channel_id=1, source_target_pairs={{0,4},{1,5},{2,6},{3,7},{4,0},{5,1},{6,2},{7,3},{8,12},{9,13},{10,... | collective-permute-start | bytes 786440 | tf_op jit(solution)/shard_map/ppermute | solution.py:494
  109.9 1.5 %collective-permute-start.21 = (f32[1,128,512]{2,1,0:T(8,128)S(1)}, f32[1,128,512]{2,1,0:T(8,128)S(1)}, u32[]{:S(2)}, u32[]{:S(2)}) collective-permute-start(f32[1,128,512]{2,1,0:T(8,128)S(1)} %get-tuple-element.126), channel_id=1, source_target_pairs={{0,2},{1,3},{2,0},{3,1},{4,6},{5,7},{6,4},{7,5},{8,10},{9,11},{10,... | collective-permute-start | bytes 786440 | tf_op jit(solution)/shard_map/ppermute | solution.py:494
  111.4 3.7 %collective-permute-start.30 = (f32[128,256]{1,0:T(8,128)S(1)}, f32[128,256]{1,0:T(8,128)S(1)}, u32[]{:S(2)}, u32[]{:S(2)}) collective-permute-start(f32[128,256]{1,0:T(8,128)S(1)} %shard_map.107.refs_1_.refs_0_), channel_id=1, source_target_pairs={{0,24},{8,16},{16,8},{24,0},{1,25},{9,17},{17,9},{25,1},{2,26},{10... | collective-permute-start | bytes 393224 | tf_op jit(solution)/shard_map/ppermute | solution.py:494
  115.1 0.8 collective-permute-start.28
  115.9 0.9 shard_map.108.refs_0_.refs_6_
  116.8 0.9 shard_map.109.refs_3_
  117.7 0.9 shard_map.110.refs_3_
  118.5 0.8 shard_map.111.refs_3_
  119.4 2.3 %collective-permute-done.29.refs_2_ = f32[128,256]{1,0:T(8,128)S(1)} collective-permute-done((f32[128,256]{1,0:T(8,128)S(1)}, f32[128,256]{1,0:T(8,128)S(1)}, u32[]{:S(2)}, u32[]{:S(2)}) %collective-permute-start.29) | collective-permute-done | bytes 131104 | tf_op jit(solution)/shard_map/ppermute | solution.py:494
  121.7 1.9 %shard_map.113 = f32[512,1024]{1,0:T(8,128)} custom-call(f32[128,256]{1,0:T(8,128)S(1)} %shard_map.107.refs_1_.refs_0_, f32[128,256]{1,0:T(8,128)S(1)} %collective-permute-done.28.refs_1_, f32[128,256]{1,0:T(8,128)S(1)} %collective-permute-done.29.refs_2_, f32[128,256]{1,0:T(8,128)S(1)} %collective-permute-done.30.refs_3_, bf16[128,96]{1,0:T(8,128)(2,1)S(1)} %copy-done.4, ...), custom_call_target="tpu_custom_call" | custom-call | flops 402653184 | bytes 2097152 | tf_op jit(solution)/shard_map/pallas_call | solution.py:406
  123.6 0.8 shard_map.112
  (38 shorter events, 0.3 us)
Async XLA Ops:
  9.6 2.8 %collective-permute-start = (f32[4,128,512]{2,1,0:T(8,128)S(1)}, f32[4,128,512]{2,1,0:T(8,128)S(1)}, u32[]{:S(2)}, u32[]{:S(2)}) collective-permute-start(f32[4,128,512]{2,1,0:T(8,128)S(1)} %get-tuple-element.69.refs_5_), channel_id=1, source_target_pairs={{0,1},{1,0},{2,3},{3,2},{4,5},{5,4},{6,7},{7,6},{8,9},{9,8},{10,11... | collective-permute-start | bytes 3145736 | tf_op jit(solution)/shard_map/ppermute | solution.py:494
  13.8 3.9 %collective-permute-start.1 = (f32[4,128,512]{2,1,0:T(8,128)S(1)}, f32[4,128,512]{2,1,0:T(8,128)S(1)}, u32[]{:S(2)}, u32[]{:S(2)}) collective-permute-start(f32[4,128,512]{2,1,0:T(8,128)S(1)} %shard_map.88.refs_2_), channel_id=1, source_target_pairs={{0,1},{1,0},{2,3},{3,2},{4,5},{5,4},{6,7},{7,6},{8,9},{9,8},{10,11... | collective-permute-start | bytes 3145736 | tf_op jit(solution)/shard_map/ppermute | solution.py:494
  17.4 3.5 %collective-permute-start.2 = (f32[4,128,512]{2,1,0:T(8,128)S(1)}, f32[4,128,512]{2,1,0:T(8,128)S(1)}, u32[]{:S(2)}, u32[]{:S(2)}) collective-permute-start(f32[4,128,512]{2,1,0:T(8,128)S(1)} %get-tuple-element.75.refs_2_), channel_id=1, source_target_pairs={{0,1},{1,0},{2,3},{3,2},{4,5},{5,4},{6,7},{7,6},{8,9},{9,8},{10,11... | collective-permute-start | bytes 3145736 | tf_op jit(solution)/shard_map/ppermute | solution.py:494
  25.4 8.9 %collective-permute-start.4 = (f32[4,128,1024]{2,1,0:T(8,128)S(1)}, f32[4,128,1024]{2,1,0:T(8,128)S(1)}, u32[]{:S(2)}, u32[]{:S(2)}) collective-permute-start(f32[4,128,1024]{2,1,0:T(8,128)S(1)} %get-tuple-element.81.refs_2_), channel_id=1, source_target_pairs={{0,1},{1,0},{2,3},{3,2},{4,5},{5,4},{6,7},{7,6},{8,9},{9,8},{10,11... | collective-permute-start | bytes 6291464 | tf_op jit(solution)/shard_map/ppermute | solution.py:494
  25.8 5.3 %collective-permute-start.3 = (f32[4,128,512]{2,1,0:T(8,128)S(1)}, f32[4,128,512]{2,1,0:T(8,128)S(1)}, u32[]{:S(2)}, u32[]{:S(2)}) collective-permute-start(f32[4,128,512]{2,1,0:T(8,128)S(1)} %shard_map.93.refs_2_), channel_id=1, source_target_pairs={{0,1},{1,0},{2,3},{3,2},{4,5},{5,4},{6,7},{7,6},{8,9},{9,8},{10,11... | collective-permute-start | bytes 3145736 | tf_op jit(solution)/shard_map/ppermute | solution.py:494
  37.8 23.4 %collective-permute-start.5 = (f32[4,128,1024]{2,1,0:T(8,128)S(1)}, f32[4,128,1024]{2,1,0:T(8,128)S(1)}, u32[]{:S(2)}, u32[]{:S(2)}) collective-permute-start(f32[4,128,1024]{2,1,0:T(8,128)S(1)} %get-tuple-element.85.refs_4_), channel_id=1, source_target_pairs={{0,1},{1,0},{2,3},{3,2},{4,5},{5,4},{6,7},{7,6},{8,9},{9,8},{10,11... | collective-permute-start | bytes 6291464 | tf_op jit(solution)/shard_map/ppermute | solution.py:494
  38.2 9.7 %collective-permute-start.14 = (f32[2,128,256]{2,1,0:T(8,128)S(1)}, f32[2,128,256]{2,1,0:T(8,128)S(1)}, u32[]{:S(2)}, u32[]{:S(2)}) collective-permute-start(f32[2,128,256]{2,1,0:T(8,128)S(1)} %get-tuple-element.100), channel_id=1, source_target_pairs={{0,2},{1,3},{2,0},{3,1},{4,6},{5,7},{6,4},{7,5},{8,10},{9,11},{10,... | collective-permute-start | bytes 786440 | tf_op jit(solution)/shard_map/ppermute | solution.py:494
  40.8 9.2 %collective-permute-start.16 = (f32[2,128,256]{2,1,0:T(8,128)S(1)}, f32[2,128,256]{2,1,0:T(8,128)S(1)}, u32[]{:S(2)}, u32[]{:S(2)}) collective-permute-start(f32[2,128,256]{2,1,0:T(8,128)S(1)} %get-tuple-element.103), channel_id=1, source_target_pairs={{0,4},{1,5},{2,6},{3,7},{4,0},{5,1},{6,2},{7,3},{8,12},{9,13},{10,... | collective-permute-start | bytes 786440 | tf_op jit(solution)/shard_map/ppermute | solution.py:494
  42.3 11.2 %collective-permute-start.15 = (f32[2,128,256]{2,1,0:T(8,128)S(1)}, f32[2,128,256]{2,1,0:T(8,128)S(1)}, u32[]{:S(2)}, u32[]{:S(2)}) collective-permute-start(f32[2,128,256]{2,1,0:T(8,128)S(1)} %get-tuple-element.101), channel_id=1, source_target_pairs={{0,2},{1,3},{2,0},{3,1},{4,6},{5,7},{6,4},{7,5},{8,10},{9,11},{10,... | collective-permute-start | bytes 786440 | tf_op jit(solution)/shard_map/ppermute | solution.py:494
  42.8 12.8 %collective-permute-start.17 = (f32[2,128,256]{2,1,0:T(8,128)S(1)}, f32[2,128,256]{2,1,0:T(8,128)S(1)}, u32[]{:S(2)}, u32[]{:S(2)}) collective-permute-start(f32[2,128,256]{2,1,0:T(8,128)S(1)} %get-tuple-element.105), channel_id=1, source_target_pairs={{0,4},{1,5},{2,6},{3,7},{4,0},{5,1},{6,2},{7,3},{8,12},{9,13},{10,... | collective-permute-start | bytes 786440 | tf_op jit(solution)/shard_map/ppermute | solution.py:494
  47.9 11.2 %collective-permute-start.10 = (f32[2,128,256]{2,1,0:T(8,128)S(1)}, f32[2,128,256]{2,1,0:T(8,128)S(1)}, u32[]{:S(2)}, u32[]{:S(2)}) collective-permute-start(f32[2,128,256]{2,1,0:T(8,128)S(1)} %get-tuple-element.94), channel_id=1, source_target_pairs={{0,2},{1,3},{2,0},{3,1},{4,6},{5,7},{6,4},{7,5},{8,10},{9,11},{10,... | collective-permute-start | bytes 786440 | tf_op jit(solution)/shard_map/ppermute | solution.py:494
  50.0 29.9 %collective-permute-start.8 = (f32[2,128,512]{2,1,0:T(8,128)S(1)}, f32[2,128,512]{2,1,0:T(8,128)S(1)}, u32[]{:S(2)}, u32[]{:S(2)}) collective-permute-start(f32[2,128,512]{2,1,0:T(8,128)S(1)} %get-tuple-element.91), channel_id=1, source_target_pairs={{0,2},{1,3},{2,0},{3,1},{4,6},{5,7},{6,4},{7,5},{8,10},{9,11},{10,... | collective-permute-start | bytes 1572872 | tf_op jit(solution)/shard_map/ppermute | solution.py:494
  53.5 26.3 %collective-permute-start.9 = (f32[2,128,512]{2,1,0:T(8,128)S(1)}, f32[2,128,512]{2,1,0:T(8,128)S(1)}, u32[]{:S(2)}, u32[]{:S(2)}) collective-permute-start(f32[2,128,512]{2,1,0:T(8,128)S(1)} %get-tuple-element.93), channel_id=1, source_target_pairs={{0,4},{1,5},{2,6},{3,7},{4,0},{5,1},{6,2},{7,3},{8,12},{9,13},{10,... | collective-permute-start | bytes 1572872 | tf_op jit(solution)/shard_map/ppermute | solution.py:494
  55.6 18.4 %collective-permute-start.12 = (f32[2,128,256]{2,1,0:T(8,128)S(1)}, f32[2,128,256]{2,1,0:T(8,128)S(1)}, u32[]{:S(2)}, u32[]{:S(2)}) collective-permute-start(f32[2,128,256]{2,1,0:T(8,128)S(1)} %get-tuple-element.97), channel_id=1, source_target_pairs={{0,4},{1,5},{2,6},{3,7},{4,0},{5,1},{6,2},{7,3},{8,12},{9,13},{10,... | collective-permute-start | bytes 786440 | tf_op jit(solution)/shard_map/ppermute | solution.py:494
  59.2 16.9 %collective-permute-start.11 = (f32[2,128,256]{2,1,0:T(8,128)S(1)}, f32[2,128,256]{2,1,0:T(8,128)S(1)}, u32[]{:S(2)}, u32[]{:S(2)}) collective-permute-start(f32[2,128,256]{2,1,0:T(8,128)S(1)} %get-tuple-element.95), channel_id=1, source_target_pairs={{0,2},{1,3},{2,0},{3,1},{4,6},{5,7},{6,4},{7,5},{8,10},{9,11},{10,... | collective-permute-start | bytes 786440 | tf_op jit(solution)/shard_map/ppermute | solution.py:494
  61.2 17.8 %collective-permute-start.13 = (f32[2,128,256]{2,1,0:T(8,128)S(1)}, f32[2,128,256]{2,1,0:T(8,128)S(1)}, u32[]{:S(2)}, u32[]{:S(2)}) collective-permute-start(f32[2,128,256]{2,1,0:T(8,128)S(1)} %get-tuple-element.99), channel_id=1, source_target_pairs={{0,4},{1,5},{2,6},{3,7},{4,0},{5,1},{6,2},{7,3},{8,12},{9,13},{10,... | collective-permute-start | bytes 786440 | tf_op jit(solution)/shard_map/ppermute | solution.py:494
  65.8 12.3 %copy-start = (f32[1,512,1024]{2,1,0:T(8,128)S(1)}, f32[1,512,1024]{2,1,0:T(8,128)}, u32[]{:S(2)}) copy-start(f32[1,512,1024]{2,1,0:T(8,128)} %refs_4_.3) | copy-start | bytes 6291460
  65.8 12.3 %copy-start.1 = (bf16[768,64]{1,0:T(8,128)(2,1)S(1)}, bf16[768,64]{1,0:T(8,128)(2,1)}, u32[]{:S(2)}) copy-start(bf16[768,64]{1,0:T(8,128)(2,1)} %constant.28.refs_10_.refs_6_) | copy-start | bytes 294916
  65.8 12.3 %copy-start.2 = (bf16[32,384]{1,0:T(8,128)(2,1)S(1)}, bf16[32,384]{1,0:T(8,128)(2,1)}, u32[]{:S(2)}) copy-start(bf16[32,384]{1,0:T(8,128)(2,1)} %constant.23.refs_9_.refs_5_) | copy-start | bytes 73732
  74.0 22.4 %collective-permute-start.6 = (f32[2,128,512]{2,1,0:T(8,128)S(1)}, f32[2,128,512]{2,1,0:T(8,128)S(1)}, u32[]{:S(2)}, u32[]{:S(2)}) collective-permute-start(f32[2,128,512]{2,1,0:T(8,128)S(1)} %get-tuple-element.88), channel_id=1, source_target_pairs={{0,2},{1,3},{2,0},{3,1},{4,6},{5,7},{6,4},{7,5},{8,10},{9,11},{10,... | collective-permute-start | bytes 1572872 | tf_op jit(solution)/shard_map/ppermute | solution.py:494
  76.0 21.9 %collective-permute-start.7 = (f32[2,128,512]{2,1,0:T(8,128)S(1)}, f32[2,128,512]{2,1,0:T(8,128)S(1)}, u32[]{:S(2)}, u32[]{:S(2)}) collective-permute-start(f32[2,128,512]{2,1,0:T(8,128)S(1)} %get-tuple-element.90), channel_id=1, source_target_pairs={{0,4},{1,5},{2,6},{3,7},{4,0},{5,1},{6,2},{7,3},{8,12},{9,13},{10,... | collective-permute-start | bytes 1572872 | tf_op jit(solution)/shard_map/ppermute | solution.py:494
  80.7 13.7 %collective-permute-start.23 = (f32[1,128,512]{2,1,0:T(8,128)S(1)}, f32[1,128,512]{2,1,0:T(8,128)S(1)}, u32[]{:S(2)}, u32[]{:S(2)}) collective-permute-start(f32[1,128,512]{2,1,0:T(8,128)S(1)} %get-tuple-element.127), channel_id=1, source_target_pairs={{0,2},{1,3},{2,0},{3,1},{4,6},{5,7},{6,4},{7,5},{8,10},{9,11},{10,... | collective-permute-start | bytes 786440 | tf_op jit(solution)/shard_map/ppermute | solution.py:494
  82.2 17.1 %collective-permute-start.22 = (f32[1,128,512]{2,1,0:T(8,128)S(1)}, f32[1,128,512]{2,1,0:T(8,128)S(1)}, u32[]{:S(2)}, u32[]{:S(2)}) collective-permute-start(f32[1,128,512]{2,1,0:T(8,128)S(1)} %get-tuple-element.120.refs_11_), channel_id=1, source_target_pairs={{0,4},{1,5},{2,6},{3,7},{4,0},{5,1},{6,2},{7,3},{8,12},{9,13},{10,... | collective-permute-start | bytes 786440 | tf_op jit(solution)/shard_map/ppermute | solution.py:494
  82.8 18.0 %collective-permute-start.25 = (f32[2,128,256]{2,1,0:T(8,128)S(1)}, f32[2,128,256]{2,1,0:T(8,128)S(1)}, u32[]{:S(2)}, u32[]{:S(2)}) collective-permute-start(f32[2,128,256]{2,1,0:T(8,128)S(1)} %get-tuple-element.128), channel_id=1, source_target_pairs={{0,2},{1,3},{2,0},{3,1},{4,6},{5,7},{6,4},{7,5},{8,10},{9,11},{10,... | collective-permute-start | bytes 786440 | tf_op jit(solution)/shard_map/ppermute | solution.py:494
  94.4 17.0 %collective-permute-start.24 = (f32[2,128,256]{2,1,0:T(8,128)S(1)}, f32[2,128,256]{2,1,0:T(8,128)S(1)}, u32[]{:S(2)}, u32[]{:S(2)}) collective-permute-start(f32[2,128,256]{2,1,0:T(8,128)S(1)} %get-tuple-element.115.refs_11_), channel_id=1, source_target_pairs={{0,4},{1,5},{2,6},{3,7},{4,0},{5,1},{6,2},{7,3},{8,12},{9,13},{10,... | collective-permute-start | bytes 786440 | tf_op jit(solution)/shard_map/ppermute | solution.py:494
  96.4 18.7 %collective-permute-start.27 = (f32[2,128,256]{2,1,0:T(8,128)S(1)}, f32[2,128,256]{2,1,0:T(8,128)S(1)}, u32[]{:S(2)}, u32[]{:S(2)}) collective-permute-start(f32[2,128,256]{2,1,0:T(8,128)S(1)} %get-tuple-element.129), channel_id=1, source_target_pairs={{0,2},{1,3},{2,0},{3,1},{4,6},{5,7},{6,4},{7,5},{8,10},{9,11},{10,... | collective-permute-start | bytes 786440 | tf_op jit(solution)/shard_map/ppermute | solution.py:494
  97.9 17.2 %collective-permute-start.26 = (f32[2,128,256]{2,1,0:T(8,128)S(1)}, f32[2,128,256]{2,1,0:T(8,128)S(1)}, u32[]{:S(2)}, u32[]{:S(2)}) collective-permute-start(f32[2,128,256]{2,1,0:T(8,128)S(1)} %get-tuple-element.110.refs_15_), channel_id=1, source_target_pairs={{0,4},{1,5},{2,6},{3,7},{4,0},{5,1},{6,2},{7,3},{8,12},{9,13},{10,... | collective-permute-start | bytes 786440 | tf_op jit(solution)/shard_map/ppermute | solution.py:494
  98.4 17.5 %copy-start.3 = (bf16[192,256]{1,0:T(8,128)(2,1)S(1)}, bf16[192,256]{1,0:T(8,128)(2,1)}, u32[]{:S(2)}) copy-start(bf16[192,256]{1,0:T(8,128)(2,1)} %constant.38.refs_3_.refs_5_) | copy-start | bytes 294916
  98.4 17.5 %copy-start.4 = (bf16[128,96]{1,0:T(8,128)(2,1)S(1)}, bf16[128,96]{1,0:T(8,128)(2,1)}, u32[]{:S(2)}) copy-start(bf16[128,96]{1,0:T(8,128)(2,1)} %constant.33.refs_2_.refs_4_) | copy-start | bytes 73732
  99.3 8.6 %collective-permute-start.18 = (f32[128,128]{1,0:T(8,128)S(1)}, f32[128,128]{1,0:T(8,128)S(1)}, u32[]{:S(2)}, u32[]{:S(2)}) collective-permute-start(f32[128,128]{1,0:T(8,128)S(1)} %get-tuple-element.123), channel_id=1, source_target_pairs={{0,4},{1,5},{2,6},{3,7},{4,0},{5,1},{6,2},{7,3},{8,12},{9,13},{10,... | collective-permute-start | bytes 196616 | tf_op jit(solution)/shard_map/ppermute | solution.py:494
  100.8 9.1 %collective-permute-start.19 = (f32[128,128]{1,0:T(8,128)S(1)}, f32[128,128]{1,0:T(8,128)S(1)}, u32[]{:S(2)}, u32[]{:S(2)}) collective-permute-start(f32[128,128]{1,0:T(8,128)S(1)} %get-tuple-element.124), channel_id=1, source_target_pairs={{0,2},{1,3},{2,0},{3,1},{4,6},{5,7},{6,4},{7,5},{8,10},{9,11},{10,... | collective-permute-start | bytes 196616 | tf_op jit(solution)/shard_map/ppermute | solution.py:494
  107.9 15.7 %collective-permute-start.20 = (f32[1,128,512]{2,1,0:T(8,128)S(1)}, f32[1,128,512]{2,1,0:T(8,128)S(1)}, u32[]{:S(2)}, u32[]{:S(2)}) collective-permute-start(f32[1,128,512]{2,1,0:T(8,128)S(1)} %get-tuple-element.125), channel_id=1, source_target_pairs={{0,4},{1,5},{2,6},{3,7},{4,0},{5,1},{6,2},{7,3},{8,12},{9,13},{10,... | collective-permute-start | bytes 786440 | tf_op jit(solution)/shard_map/ppermute | solution.py:494
  109.9 13.7 %collective-permute-start.21 = (f32[1,128,512]{2,1,0:T(8,128)S(1)}, f32[1,128,512]{2,1,0:T(8,128)S(1)}, u32[]{:S(2)}, u32[]{:S(2)}) collective-permute-start(f32[1,128,512]{2,1,0:T(8,128)S(1)} %get-tuple-element.126), channel_id=1, source_target_pairs={{0,2},{1,3},{2,0},{3,1},{4,6},{5,7},{6,4},{7,5},{8,10},{9,11},{10,... | collective-permute-start | bytes 786440 | tf_op jit(solution)/shard_map/ppermute | solution.py:494
  111.4 8.0 %collective-permute-start.30 = (f32[128,256]{1,0:T(8,128)S(1)}, f32[128,256]{1,0:T(8,128)S(1)}, u32[]{:S(2)}, u32[]{:S(2)}) collective-permute-start(f32[128,256]{1,0:T(8,128)S(1)} %shard_map.107.refs_1_.refs_0_), channel_id=1, source_target_pairs={{0,24},{8,16},{16,8},{24,0},{1,25},{9,17},{17,9},{25,1},{2,26},{10... | collective-permute-start | bytes 393224 | tf_op jit(solution)/shard_map/ppermute | solution.py:494
  115.1 6.6 %collective-permute-start.29 = (f32[128,256]{1,0:T(8,128)S(1)}, f32[128,256]{1,0:T(8,128)S(1)}, u32[]{:S(2)}, u32[]{:S(2)}) collective-permute-start(f32[128,256]{1,0:T(8,128)S(1)} %shard_map.107.refs_1_.refs_0_), channel_id=1, source_target_pairs={{0,16},{8,24},{16,0},{24,8},{1,17},{9,25},{17,1},{25,9},{2,18},{10... | collective-permute-start | bytes 393224 | tf_op jit(solution)/shard_map/ppermute | solution.py:494
  115.1 6.6 %collective-permute-start.28 = (f32[128,256]{1,0:T(8,128)S(1)}, f32[128,256]{1,0:T(8,128)S(1)}, u32[]{:S(2)}, u32[]{:S(2)}) collective-permute-start(f32[128,256]{1,0:T(8,128)S(1)} %shard_map.107.refs_1_.refs_0_), channel_id=1, source_target_pairs={{0,8},{8,0},{16,24},{24,16},{1,9},{9,1},{17,25},{25,17},{2,10},{10... | collective-permute-start | bytes 393224 | tf_op jit(solution)/shard_map/ppermute | solution.py:494

commit v3 on v2

--- a/solution.py
+++ b/solution.py
@@ -9,7 +9,7 @@
 CH = 64
 BAND = 16
 EPS = 1e-05
-LATE = (1, 5)
+LATE = (5,)
 ROWS = 128
 SPAN = 256
 
@@ -134,8 +134,14 @@
     group = 64
     steps = tokens // tile
     parts = [columns(side, cols, q, w) for side in range(2)]
-
-    def kernel(own, x_hbm, c_hbm, x_ref, c_ref, s_ref, p_ref, xt_ref, x_sem, c_sem):
+    others = [
+        slice(lo, hi)
+        for side in range(2)
+        for lo, hi in ((side * cols // 2, parts[side].start), (parts[side].stop, (side + 1) * cols // 2))
+        if lo < hi
+    ]
+
+    def kernel(own, x_hbm, c_hbm, x_ref, c_ref, s_ref, p_ref, xt_ref, xe_ref, x_sem, c_sem):
         def rows_at(i):
             return pl.ds(pl.multiple_of(i * tile, tile), tile)
 
@@ -161,10 +167,11 @@
 
         def turn(i, now):
             at = rows_at(i)
-            for j in range(half):
-                lanes = pl.ds(pl.multiple_of(own[2 * j + 1] * rows + off, 128), r)
-                value = (x_ref[at, lanes].astype(F32) * now).astype(jnp.bfloat16)
-                xt_ref[j * r : (j + 1) * r, at] = value.T
+            for parity, out in ((1, xt_ref), (0, xe_ref)):
+                for j in range(half):
+                    lanes = pl.ds(pl.multiple_of(own[2 * j + parity] * rows + off, 128), r)
+                    value = (x_ref[at, lanes].astype(F32) * now).astype(jnp.bfloat16)
+                    out[j * r : (j + 1) * r, at] = value.T
 
         def both(i, _):
             piece(i + 1).wait()
@@ -175,12 +182,15 @@
             return 0
 
         near = [
-            pltpu.make_async_copy(c_hbm.at[:, at], c_ref.at[:, at], c_sem.at[side])
-            for side, at in enumerate(parts)
+            pltpu.make_async_copy(c_hbm.at[:, at], c_ref.at[:, at], c_sem.at[k])
+            for k, at in enumerate(parts + others)
         ]
+        near, rest = near[:2], near[2:]
         for copy in near:
             copy.start()
         lax.fori_loop(0, steps, begin, 0)
+        for copy in rest:
+            copy.start()
         piece(0).wait()
         s_ref[rows_at(0), :] = scales(0)
         lax.fori_loop(0, steps - 2, both, 0)
@@ -197,6 +207,8 @@
             p_ref[:, :, side * w : (side + 1) * w] += jnp.dot(
                 xt_ref[:, cut:], c_ref[cut:, parts[side]], preferred_element_type=F32
             ).reshape(half, r, w)
+        for copy in rest:
+            copy.wait()
 
     return pl.pallas_call(
         kernel,
@@ -206,12 +218,13 @@
             pltpu.VMEM((tokens, 128), F32),
             pltpu.VMEM((half, r, 2 * w), F32),
             pltpu.VMEM((half * r, tokens), jnp.bfloat16),
+            pltpu.VMEM((half * r, tokens), jnp.bfloat16),
         ),
         in_specs=[SMEM, ANY, ANY],
-        out_specs=(VMEM,) * 5,
+        out_specs=(VMEM,) * 6,
         scratch_shapes=[
             pltpu.SemaphoreType.DMA((steps,)),
-            pltpu.SemaphoreType.DMA((2,)),
+            pltpu.SemaphoreType.DMA((2 + len(others),)),
         ],
         compiler_params=pltpu.CompilerParams(vmem_limit_bytes=12 << 20),
         cost_estimate=cost(4 * tokens * half * r * w, 2 * tokens * (width + cols)),
@@ -243,41 +256,6 @@
     return on_chip(
         kernel, [x, scale, c], tokens,
         [shape, ((half * r, x.shape[0]), jnp.bfloat16)], owners=owners, flops=flops,
-    )
-
-
-def second_call(x, scale, c, c_hbm, owners, n, rows, chunk, tokens):
-    off, q, w = chunk
-    cols = c.shape[1]
-    half = n // 2
-    parts = [columns(side, cols, q, w) for side in range(2)]
-    others = [
-        slice(lo, hi)
-        for side in range(2)
-        for lo, hi in ((side * cols // 2, parts[side].start), (parts[side].stop, (side + 1) * cols // 2))
-        if lo < hi
-    ]
-
-    def kernel(own, x_ref, s_ref, old_ref, from_ref, out_ref, c_ref, xt_ref, sem):
-        rest = [
-            pltpu.make_async_copy(from_ref.at[:, at], c_ref.at[:, at], sem.at[k])
-            for k, at in enumerate(others)
-        ]
-        for copy in rest:
-            copy.start()
-        fill(xt_ref, x_ref, s_ref, [own[2 * j] * rows + off for j in range(half)], ROWS)
-        for side in range(2):
-            out_ref[:, :, side * w : (side + 1) * w] = jnp.dot(
-                xt_ref[...], c_ref[:, parts[side]], preferred_element_type=F32
-            ).reshape(half, ROWS, w)
-        for copy in rest:
-            copy.wait()
-
-    return on_chip(
-        kernel, [x, scale, c], tokens,
-        [(half, ROWS, 2 * w), (c.shape, c.dtype), ((half * ROWS, x.shape[0]), x.dtype)],
-        [pltpu.SemaphoreType.DMA((max(len(others), 1),))], owners, 4 * c.shape[0] * half * ROWS * w,
-        aliases={2: 1}, far=[c_hbm],
     )
 
 
@@ -495,10 +473,9 @@
 
     row_groups = chunks_of(rows, wide)
     chunks = [chunk for group in row_groups for chunk in group]
-    c_hbm = c
-    x, c, scale, odd, xt = first_call(x, c, owners, n, rows, chunks[0])
+    x, c, scale, odd, *xts = first_call(x, c, owners, n, rows, chunks[0])
     token = odd
-    kept = {(1, chunks[0][0]): xt}
+    kept = {(1, chunks[0][0]): xts[0], (0, chunks[0][0]): xts[1]}
 
     def product(k, parity):
         at = parity, chunks[k][0]
@@ -510,12 +487,7 @@
     got = swap(odd, 1)
     state = []
     for k, chunk in enumerate(chunks):
-        if k == 0:
-            even, c, kept[0, chunk[0]] = second_call(
-                x, scale, c, c_hbm, owners, n, rows, chunk, [token]
-            )
-        else:
-            even = product(k, 0)
+        even = product(k, 0)
         token = even
         here = got
         if k + 1 < len(chunks) and k + 1 not in LATE:

time: 125 us -> 124 us (level)
  transfers between devices with their start and end apart: 31 -> 31, of which waited for: 9 -> 8; matrix products, arithmetic and copies ran while one was open for 0% -> 0% of each run, Pallas kernels for 19% -> 20%
where the time goes in v3:
time: 124 us
  waiting for transfers between devices  44.7 us (36%)
  Pallas kernels  42.6 us (34%)
  starting transfers between devices  35.8 us (29%)
    ppermute x31, waiting for transfers between devices, swap(): return lax.ppermute(value, axis, [(i, i ^ bit) for i in range(size)])  44.7 us
    ppermute x31, starting transfers between devices, swap(): return lax.ppermute(value, axis, [(i, i ^ bit) for i in range(size)])  35.8 us
    pallas_call x23, Pallas kernels, on_chip(): pl.pallas_call(run, out_shape=tuple((pltpu.VMEM(shape, kind) for shape, k...  28 us
    pallas_call x1, Pallas kernels, first_call(): pl.pallas_call(kernel, out_shape=(pltpu.VMEM(x.shape, x.dtype), pltpu.VME...  9.25 us
    pallas_call x5, Pallas kernels, outward(): pl.pallas_call(run, out_shape=jax.ShapeDtypeStruct(shape, F32), in_specs=...  5.27 us
  transfers between devices with their start and end apart: 31, of which 8 were waited for; matrix products, arithmetic and copies ran while one was open for 0% of the time, Pallas kernels for 20%

profile of v3, /device:TPU:0, one launch (start us, length us, event | category | flops | bytes accessed | tf_op | source)
XLA Modules:
  0.0 124.0 jit_solution(1013866560549687364)
XLA Ops:
  0.6 9.2 %first.1 = (bf16[2048,4096]{1,0:T(8,128)(2,1)S(1)}, bf16[2048,1024]{1,0:T(8,128)(2,1)S(1)}, f32[2048,128]{1,0:T(8,128)S(1)}, f32[4,128,512]{2,1,0:T(8,128)S(1)},...) custom-call(s32[8]{0:T(128)S(1)} %iota_xor_fusion.own.refs_0_, bf16[2048,4096]{1,0:T(8,128)(2,1)} %bitcast.2, ...), custom_call_target="tpu_custom_call" | custom-call | flops 1073741824 | bytes 20971520 | tf_op jit(solution)/shard_map/first/pallas_call | solution.py:213
  9.9 0.5 collective-permute-start
  10.4 1.3 %shard_map.86.refs_2_.refs_0_ = f32[4,128,512]{2,1,0:T(8,128)S(1)} custom-call(bf16[512,2048]{1,0:T(8,128)(2,1)S(1)} %get-tuple-element.67.refs_0_, bf16[2048,1024]{1,0:T(8,128)(2,1)S(1)} %get-tuple-element.66.refs_1_.refs_3_, f32[4,128,512]{2,1,0:T(8,128)S(1)} %get-tuple-element.68.refs_2_), custom_call_target="tpu_custom_call" | custom-call | flops 1073741824 | tf_op jit(solution)/shard_map/pallas_call | solution.py:104
  11.7 1.3 %shard_map.87.refs_2_ = f32[4,128,512]{2,1,0:T(8,128)S(1)} custom-call(bf16[512,2048]{1,0:T(8,128)(2,1)S(1)} %get-tuple-element.69.refs_0_, bf16[2048,1024]{1,0:T(8,128)(2,1)S(1)} %get-tuple-element.66.refs_1_.refs_3_, f32[4,128,512]{2,1,0:T(8,128)S(1)} %shard_map.86.refs_2_.refs_0_), custom_call_target="tpu_custom_call" | custom-call | flops 1073741824 | tf_op jit(solution)/shard_map/pallas_call | solution.py:104
  13.0 0.1 collective-permute-start.1
  13.1 0.1 shard_map.88
  13.2 1.3 %shard_map.89.refs_4_.refs_0_ = f32[4,128,512]{2,1,0:T(8,128)S(1)} custom-call(bf16[512,2048]{1,0:T(8,128)(2,1)S(1)} %get-tuple-element.67.refs_0_, bf16[2048,1024]{1,0:T(8,128)(2,1)S(1)} %get-tuple-element.66.refs_1_.refs_3_, f32[2,128,256]{2,1,0:T(8,128)S(1)} %get-tuple-element.70.refs_2_.refs_0_), custom_call_target="tpu_custom_call" | custom-call | flops 1073741824 | tf_op jit(solution)/shard_map/pallas_call | solution.py:104
  14.5 1.9 %shard_map.90 = (f32[4,128,512]{2,1,0:T(8,128)S(1)}, bf16[512,2048]{1,0:T(8,128)(2,1)S(1)}) custom-call(s32[8]{0:T(128)S(1)} %iota_xor_fusion.own.refs_0_, bf16[2048,4096]{1,0:T(8,128)(2,1)S(1)} %get-tuple-element.64.refs_1_, f32[2048,128]{1,0:T(8,128)S(1)} %get-tuple-element.65.refs_2_, bf16[2048,1024]{1,0:T(8,128)(2,1)S(1)} %get-tuple-element.66.refs_1_.refs_3_, ...), custom_call_target="tpu_custom_call" | custom-call | flops 1073741824 | tf_op jit(solution)/shard_map/pallas_call | solution.py:104
  16.4 0.6 collective-permute-start.2
  17.0 0.1 shard_map.91
  17.1 1.9 %shard_map.92 = (f32[4,128,512]{2,1,0:T(8,128)S(1)}, bf16[512,2048]{1,0:T(8,128)(2,1)S(1)}) custom-call(s32[8]{0:T(128)S(1)} %iota_xor_fusion.own.refs_0_, bf16[2048,4096]{1,0:T(8,128)(2,1)S(1)} %get-tuple-element.64.refs_1_, f32[2048,128]{1,0:T(8,128)S(1)} %get-tuple-element.65.refs_2_, bf16[2048,1024]{1,0:T(8,128)(2,1)S(1)} %get-tuple-element.66.refs_1_.refs_3_, ...), custom_call_target="tpu_custom_call" | custom-call | flops 1073741824 | tf_op jit(solution)/shard_map/pallas_call | solution.py:104
  19.1 1.2 %shard_map.93.refs_2_ = f32[4,128,512]{2,1,0:T(8,128)S(1)} custom-call(bf16[512,2048]{1,0:T(8,128)(2,1)S(1)} %get-tuple-element.75.refs_0_, bf16[2048,1024]{1,0:T(8,128)(2,1)S(1)} %get-tuple-element.66.refs_1_.refs_3_, f32[4,128,512]{2,1,0:T(8,128)S(1)} %get-tuple-element.74.refs_2_.refs_0_), custom_call_target="tpu_custom_call" | custom-call | flops 1073741824 | tf_op jit(solution)/shard_map/pallas_call | solution.py:104
  20.3 0.1 shard_map.94
  20.5 1.3 %shard_map.95.refs_4_.refs_0_ = f32[4,128,512]{2,1,0:T(8,128)S(1)} custom-call(bf16[512,2048]{1,0:T(8,128)(2,1)S(1)} %get-tuple-element.73.refs_0_, bf16[2048,1024]{1,0:T(8,128)(2,1)S(1)} %get-tuple-element.66.refs_1_.refs_3_, f32[2,128,256]{2,1,0:T(8,128)S(1)} %get-tuple-element.76.refs_2_.refs_0_), custom_call_target="tpu_custom_call" | custom-call | flops 1073741824 | tf_op jit(solution)/shard_map/pallas_call | solution.py:104
  21.7 3.0 %shard_map.96 = (f32[4,128,1024]{2,1,0:T(8,128)S(1)}, bf16[512,2048]{1,0:T(8,128)(2,1)}) custom-call(s32[8]{0:T(128)S(1)} %iota_xor_fusion.own.refs_0_, bf16[2048,4096]{1,0:T(8,128)(2,1)S(1)} %get-tuple-element.64.refs_1_, f32[2048,128]{1,0:T(8,128)S(1)} %get-tuple-element.65.refs_2_, bf16[2048,1024]{1,0:T(8,128)(2,1)S(1)} %get-tuple-element.66.refs_1_.refs_3_, ...), custom_call_target="tpu_custom_call" | custom-call | flops 2147483648 | tf_op jit(solution)/shard_map/pallas_call | solution.py:104
  24.7 0.1 collective-permute-start.4
  24.8 0.4 collective-permute-start.3
  25.3 5.1 %collective-permute-done.3.refs_1_ = f32[4,128,512]{2,1,0:T(8,128)S(1)} collective-permute-done((f32[4,128,512]{2,1,0:T(8,128)S(1)}, f32[4,128,512]{2,1,0:T(8,128)S(1)}, u32[]{:S(2)}, u32[]{:S(2)}) %collective-permute-start.3) | collective-permute-done | bytes 1048608 | tf_op jit(solution)/shard_map/ppermute | solution.py:472
  30.4 0.1 shard_map.97
  30.6 3.0 %shard_map.98 = (f32[4,128,1024]{2,1,0:T(8,128)S(1)}, bf16[512,2048]{1,0:T(8,128)(2,1)}) custom-call(s32[8]{0:T(128)S(1)} %iota_xor_fusion.own.refs_0_, bf16[2048,4096]{1,0:T(8,128)(2,1)S(1)} %get-tuple-element.64.refs_1_, f32[2048,128]{1,0:T(8,128)S(1)} %get-tuple-element.65.refs_2_, bf16[2048,1024]{1,0:T(8,128)(2,1)S(1)} %get-tuple-element.66.refs_1_.refs_3_, ...), custom_call_target="tpu_custom_call" | custom-call | flops 2147483648 | tf_op jit(solution)/shard_map/pallas_call | solution.py:104
  33.6 0.3 shard_map.99
  33.9 3.2 %shard_map.100 = (f32[4,128,1024]{2,1,0:T(8,128)S(1)}, bf16[512,2048]{1,0:T(8,128)(2,1)}) custom-call(s32[8]{0:T(128)S(1)} %iota_xor_fusion.own.refs_0_, bf16[2048,4096]{1,0:T(8,128)(2,1)S(1)} %get-tuple-element.64.refs_1_, f32[2048,128]{1,0:T(8,128)S(1)} %get-tuple-element.65.refs_2_, bf16[2048,1024]{1,0:T(8,128)(2,1)S(1)} %get-tuple-element.66.refs_1_.refs_3_, ...), custom_call_target="tpu_custom_call" | custom-call | flops 2147483648 | tf_op jit(solution)/shard_map/pallas_call | solution.py:104
  37.1 0.2 collective-permute-start.5
  37.3 2.9 %collective-permute-start.14 = (f32[2,128,256]{2,1,0:T(8,128)S(1)}, f32[2,128,256]{2,1,0:T(8,128)S(1)}, u32[]{:S(2)}, u32[]{:S(2)}) collective-permute-start(f32[2,128,256]{2,1,0:T(8,128)S(1)} %get-tuple-element.96), channel_id=1, source_target_pairs={{0,2},{1,3},{2,0},{3,1},{4,6},{5,7},{6,4},{7,5},{8,10},{9,11},{10,... | collective-permute-start | bytes 786440 | tf_op jit(solution)/shard_map/ppermute | solution.py:472
  40.2 1.5 %collective-permute-start.16 = (f32[2,128,256]{2,1,0:T(8,128)S(1)}, f32[2,128,256]{2,1,0:T(8,128)S(1)}, u32[]{:S(2)}, u32[]{:S(2)}) collective-permute-start(f32[2,128,256]{2,1,0:T(8,128)S(1)} %get-tuple-element.99), channel_id=1, source_target_pairs={{0,4},{1,5},{2,6},{3,7},{4,0},{5,1},{6,2},{7,3},{8,12},{9,13},{10,... | collective-permute-start | bytes 786440 | tf_op jit(solution)/shard_map/ppermute | solution.py:472
  41.7 0.5 collective-permute-start.15
  42.2 5.1 %collective-permute-done.14.refs_1_ = f32[2,128,256]{2,1,0:T(8,128)S(1)} collective-permute-done((f32[2,128,256]{2,1,0:T(8,128)S(1)}, f32[2,128,256]{2,1,0:T(8,128)S(1)}, u32[]{:S(2)}, u32[]{:S(2)}) %collective-permute-start.14) | collective-permute-done | bytes 262176 | tf_op jit(solution)/shard_map/ppermute | solution.py:472
  47.3 2.0 %collective-permute-start.10 = (f32[2,128,256]{2,1,0:T(8,128)S(1)}, f32[2,128,256]{2,1,0:T(8,128)S(1)}, u32[]{:S(2)}, u32[]{:S(2)}) collective-permute-start(f32[2,128,256]{2,1,0:T(8,128)S(1)} %get-tuple-element.90), channel_id=1, source_target_pairs={{0,2},{1,3},{2,0},{3,1},{4,6},{5,7},{6,4},{7,5},{8,10},{9,11},{10,... | collective-permute-start | bytes 786440 | tf_op jit(solution)/shard_map/ppermute | solution.py:472
  49.4 3.6 %collective-permute-done.15.refs_3_ = f32[2,128,256]{2,1,0:T(8,128)S(1)} collective-permute-done((f32[2,128,256]{2,1,0:T(8,128)S(1)}, f32[2,128,256]{2,1,0:T(8,128)S(1)}, u32[]{:S(2)}, u32[]{:S(2)}) %collective-permute-start.15) | collective-permute-done | bytes 262176 | tf_op jit(solution)/shard_map/ppermute | solution.py:472
  52.9 2.1 %collective-permute-start.9 = (f32[2,128,512]{2,1,0:T(8,128)S(1)}, f32[2,128,512]{2,1,0:T(8,128)S(1)}, u32[]{:S(2)}, u32[]{:S(2)}) collective-permute-start(f32[2,128,512]{2,1,0:T(8,128)S(1)} %get-tuple-element.89), channel_id=1, source_target_pairs={{0,4},{1,5},{2,6},{3,7},{4,0},{5,1},{6,2},{7,3},{8,12},{9,13},{10,... | collective-permute-start | bytes 1572872 | tf_op jit(solution)/shard_map/ppermute | solution.py:472
  55.0 0.4 collective-permute-start.12
  55.4 3.2 %collective-permute-done.10.refs_1_ = f32[2,128,256]{2,1,0:T(8,128)S(1)} collective-permute-done((f32[2,128,256]{2,1,0:T(8,128)S(1)}, f32[2,128,256]{2,1,0:T(8,128)S(1)}, u32[]{:S(2)}, u32[]{:S(2)}) %collective-permute-start.10) | collective-permute-done | bytes 262176 | tf_op jit(solution)/shard_map/ppermute | solution.py:472
  58.6 2.0 %collective-permute-start.11 = (f32[2,128,256]{2,1,0:T(8,128)S(1)}, f32[2,128,256]{2,1,0:T(8,128)S(1)}, u32[]{:S(2)}, u32[]{:S(2)}) collective-permute-start(f32[2,128,256]{2,1,0:T(8,128)S(1)} %get-tuple-element.91), channel_id=1, source_target_pairs={{0,2},{1,3},{2,0},{3,1},{4,6},{5,7},{6,4},{7,5},{8,10},{9,11},{10,... | collective-permute-start | bytes 786440 | tf_op jit(solution)/shard_map/ppermute | solution.py:472
  60.6 1.5 %collective-permute-start.13 = (f32[2,128,256]{2,1,0:T(8,128)S(1)}, f32[2,128,256]{2,1,0:T(8,128)S(1)}, u32[]{:S(2)}, u32[]{:S(2)}) collective-permute-start(f32[2,128,256]{2,1,0:T(8,128)S(1)} %get-tuple-element.95), channel_id=1, source_target_pairs={{0,4},{1,5},{2,6},{3,7},{4,0},{5,1},{6,2},{7,3},{8,12},{9,13},{10,... | collective-permute-start | bytes 786440 | tf_op jit(solution)/shard_map/ppermute | solution.py:472
  62.1 3.1 %shard_map.101 = (f32[4,128,1024]{2,1,0:T(8,128)S(1)}, bf16[512,2048]{1,0:T(8,128)(2,1)}) custom-call(s32[8]{0:T(128)S(1)} %iota_xor_fusion.own.refs_0_, bf16[2048,4096]{1,0:T(8,128)(2,1)S(1)} %get-tuple-element.64.refs_1_, f32[2048,128]{1,0:T(8,128)S(1)} %get-tuple-element.65.refs_2_, bf16[2048,1024]{1,0:T(8,128)(2,1)S(1)} %get-tuple-element.66.refs_1_.refs_3_, ...), custom_call_target="tpu_custom_call" | custom-call | flops 2147483648 | tf_op jit(solution)/shard_map/pallas_call | solution.py:104
  65.2 0.3 shard_map.102
  65.5 7.9 %collective-permute-done.12.refs_5_ = f32[2,128,256]{2,1,0:T(8,128)S(1)} collective-permute-done((f32[2,128,256]{2,1,0:T(8,128)S(1)}, f32[2,128,256]{2,1,0:T(8,128)S(1)}, u32[]{:S(2)}, u32[]{:S(2)}) %collective-permute-start.12) | collective-permute-done | bytes 262176 | tf_op jit(solution)/shard_map/ppermute | solution.py:472
  73.4 2.0 %collective-permute-start.6 = (f32[2,128,512]{2,1,0:T(8,128)S(1)}, f32[2,128,512]{2,1,0:T(8,128)S(1)}, u32[]{:S(2)}, u32[]{:S(2)}) collective-permute-start(f32[2,128,512]{2,1,0:T(8,128)S(1)} %get-tuple-element.84), channel_id=1, source_target_pairs={{0,2},{1,3},{2,0},{3,1},{4,6},{5,7},{6,4},{7,5},{8,10},{9,11},{10,... | collective-permute-start | bytes 1572872 | tf_op jit(solution)/shard_map/ppermute | solution.py:472
  75.4 2.1 %collective-permute-start.7 = (f32[2,128,512]{2,1,0:T(8,128)S(1)}, f32[2,128,512]{2,1,0:T(8,128)S(1)}, u32[]{:S(2)}, u32[]{:S(2)}) collective-permute-start(f32[2,128,512]{2,1,0:T(8,128)S(1)} %get-tuple-element.86), channel_id=1, source_target_pairs={{0,4},{1,5},{2,6},{3,7},{4,0},{5,1},{6,2},{7,3},{8,12},{9,13},{10,... | collective-permute-start | bytes 1572872 | tf_op jit(solution)/shard_map/ppermute | solution.py:472
  77.5 0.9 shard_map.103
  78.4 0.9 shard_map.104
  79.3 0.9 shard_map.105
  80.1 1.5 %collective-permute-start.23 = (f32[1,128,512]{2,1,0:T(8,128)S(1)}, f32[1,128,512]{2,1,0:T(8,128)S(1)}, u32[]{:S(2)}, u32[]{:S(2)}) collective-permute-start(f32[1,128,512]{2,1,0:T(8,128)S(1)} %get-tuple-element.123), channel_id=1, source_target_pairs={{0,2},{1,3},{2,0},{3,1},{4,6},{5,7},{6,4},{7,5},{8,10},{9,11},{10,... | collective-permute-start | bytes 786440 | tf_op jit(solution)/shard_map/ppermute | solution.py:472
  81.6 0.5 collective-permute-start.22
  82.1 0.2 collective-permute-start.25
  82.3 11.5 %collective-permute-done.23.refs_2_ = f32[1,128,512]{2,1,0:T(8,128)S(1)} collective-permute-done((f32[1,128,512]{2,1,0:T(8,128)S(1)}, f32[1,128,512]{2,1,0:T(8,128)S(1)}, u32[]{:S(2)}, u32[]{:S(2)}) %collective-permute-start.23) | collective-permute-done | bytes 262176 | tf_op jit(solution)/shard_map/ppermute | solution.py:472
  93.8 2.0 %collective-permute-start.24 = (f32[2,128,256]{2,1,0:T(8,128)S(1)}, f32[2,128,256]{2,1,0:T(8,128)S(1)}, u32[]{:S(2)}, u32[]{:S(2)}) collective-permute-start(f32[2,128,256]{2,1,0:T(8,128)S(1)} %get-tuple-element.111.refs_11_), channel_id=1, source_target_pairs={{0,4},{1,5},{2,6},{3,7},{4,0},{5,1},{6,2},{7,3},{8,12},{9,13},{10,... | collective-permute-start | bytes 786440 | tf_op jit(solution)/shard_map/ppermute | solution.py:472
  95.8 1.5 %collective-permute-start.27 = (f32[2,128,256]{2,1,0:T(8,128)S(1)}, f32[2,128,256]{2,1,0:T(8,128)S(1)}, u32[]{:S(2)}, u32[]{:S(2)}) collective-permute-start(f32[2,128,256]{2,1,0:T(8,128)S(1)} %get-tuple-element.125), channel_id=1, source_target_pairs={{0,2},{1,3},{2,0},{3,1},{4,6},{5,7},{6,4},{7,5},{8,10},{9,11},{10,... | collective-permute-start | bytes 786440 | tf_op jit(solution)/shard_map/ppermute | solution.py:472
  97.3 0.5 collective-permute-start.26
  97.8 0.9 shard_map.106
  98.7 1.5 %collective-permute-start.18 = (f32[128,128]{1,0:T(8,128)S(1)}, f32[128,128]{1,0:T(8,128)S(1)}, u32[]{:S(2)}, u32[]{:S(2)}) collective-permute-start(f32[128,128]{1,0:T(8,128)S(1)} %get-tuple-element.119), channel_id=1, source_target_pairs={{0,4},{1,5},{2,6},{3,7},{4,0},{5,1},{6,2},{7,3},{8,12},{9,13},{10,... | collective-permute-start | bytes 196616 | tf_op jit(solution)/shard_map/ppermute | solution.py:472
  100.3 1.2 collective-permute-start.19
  101.4 5.9 %collective-permute-done.18.refs_1_ = f32[128,128]{1,0:T(8,128)S(1)} collective-permute-done((f32[128,128]{1,0:T(8,128)S(1)}, f32[128,128]{1,0:T(8,128)S(1)}, u32[]{:S(2)}, u32[]{:S(2)}) %collective-permute-start.18) | collective-permute-done | bytes 65568 | tf_op jit(solution)/shard_map/ppermute | solution.py:472
  107.3 2.0 %collective-permute-start.20 = (f32[1,128,512]{2,1,0:T(8,128)S(1)}, f32[1,128,512]{2,1,0:T(8,128)S(1)}, u32[]{:S(2)}, u32[]{:S(2)}) collective-permute-start(f32[1,128,512]{2,1,0:T(8,128)S(1)} %get-tuple-element.121), channel_id=1, source_target_pairs={{0,4},{1,5},{2,6},{3,7},{4,0},{5,1},{6,2},{7,3},{8,12},{9,13},{10,... | collective-permute-start | bytes 786440 | tf_op jit(solution)/shard_map/ppermute | solution.py:472
  109.3 1.5 %collective-permute-start.21 = (f32[1,128,512]{2,1,0:T(8,128)S(1)}, f32[1,128,512]{2,1,0:T(8,128)S(1)}, u32[]{:S(2)}, u32[]{:S(2)}) collective-permute-start(f32[1,128,512]{2,1,0:T(8,128)S(1)} %get-tuple-element.122), channel_id=1, source_target_pairs={{0,2},{1,3},{2,0},{3,1},{4,6},{5,7},{6,4},{7,5},{8,10},{9,11},{10,... | collective-permute-start | bytes 786440 | tf_op jit(solution)/shard_map/ppermute | solution.py:472
  110.8 3.7 %collective-permute-start.30 = (f32[128,256]{1,0:T(8,128)S(1)}, f32[128,256]{1,0:T(8,128)S(1)}, u32[]{:S(2)}, u32[]{:S(2)}) collective-permute-start(f32[128,256]{1,0:T(8,128)S(1)} %shard_map.107.refs_1_.refs_0_), channel_id=1, source_target_pairs={{0,24},{8,16},{16,8},{24,0},{1,25},{9,17},{17,9},{25,1},{2,26},{10... | collective-permute-start | bytes 393224 | tf_op jit(solution)/shard_map/ppermute | solution.py:472
  114.5 0.8 collective-permute-start.28
  115.3 0.9 shard_map.108.refs_0_.refs_6_
  116.2 0.9 shard_map.109.refs_3_
  117.1 0.9 shard_map.110.refs_3_
  117.9 0.8 shard_map.111.refs_3_
  118.8 2.3 %collective-permute-done.29.refs_2_ = f32[128,256]{1,0:T(8,128)S(1)} collective-permute-done((f32[128,256]{1,0:T(8,128)S(1)}, f32[128,256]{1,0:T(8,128)S(1)}, u32[]{:S(2)}, u32[]{:S(2)}) %collective-permute-start.29) | collective-permute-done | bytes 131104 | tf_op jit(solution)/shard_map/ppermute | solution.py:472
  121.1 1.9 %shard_map.113 = f32[512,1024]{1,0:T(8,128)} custom-call(f32[128,256]{1,0:T(8,128)S(1)} %shard_map.107.refs_1_.refs_0_, f32[128,256]{1,0:T(8,128)S(1)} %collective-permute-done.28.refs_1_, f32[128,256]{1,0:T(8,128)S(1)} %collective-permute-done.29.refs_2_, f32[128,256]{1,0:T(8,128)S(1)} %collective-permute-done.30.refs_3_, bf16[128,96]{1,0:T(8,128)(2,1)S(1)} %copy-done.4, ...), custom_call_target="tpu_custom_call" | custom-call | flops 402653184 | bytes 2097152 | tf_op jit(solution)/shard_map/pallas_call | solution.py:384
  123.0 0.8 shard_map.112
  (38 shorter events, 0.2 us)
Async XLA Ops:
  9.9 3.2 %collective-permute-start = (f32[4,128,512]{2,1,0:T(8,128)S(1)}, f32[4,128,512]{2,1,0:T(8,128)S(1)}, u32[]{:S(2)}, u32[]{:S(2)}) collective-permute-start(f32[4,128,512]{2,1,0:T(8,128)S(1)} %get-tuple-element.68.refs_2_), channel_id=1, source_target_pairs={{0,1},{1,0},{2,3},{3,2},{4,5},{5,4},{6,7},{7,6},{8,9},{9,8},{10,11... | collective-permute-start | bytes 3145736 | tf_op jit(solution)/shard_map/ppermute | solution.py:472
  13.0 4.0 %collective-permute-start.1 = (f32[4,128,512]{2,1,0:T(8,128)S(1)}, f32[4,128,512]{2,1,0:T(8,128)S(1)}, u32[]{:S(2)}, u32[]{:S(2)}) collective-permute-start(f32[4,128,512]{2,1,0:T(8,128)S(1)} %shard_map.87.refs_2_), channel_id=1, source_target_pairs={{0,1},{1,0},{2,3},{3,2},{4,5},{5,4},{6,7},{7,6},{8,9},{9,8},{10,11... | collective-permute-start | bytes 3145736 | tf_op jit(solution)/shard_map/ppermute | solution.py:472
  16.4 3.9 %collective-permute-start.2 = (f32[4,128,512]{2,1,0:T(8,128)S(1)}, f32[4,128,512]{2,1,0:T(8,128)S(1)}, u32[]{:S(2)}, u32[]{:S(2)}) collective-permute-start(f32[4,128,512]{2,1,0:T(8,128)S(1)} %get-tuple-element.71.refs_2_), channel_id=1, source_target_pairs={{0,1},{1,0},{2,3},{3,2},{4,5},{5,4},{6,7},{7,6},{8,9},{9,8},{10,11... | collective-permute-start | bytes 3145736 | tf_op jit(solution)/shard_map/ppermute | solution.py:472
  24.7 8.9 %collective-permute-start.4 = (f32[4,128,1024]{2,1,0:T(8,128)S(1)}, f32[4,128,1024]{2,1,0:T(8,128)S(1)}, u32[]{:S(2)}, u32[]{:S(2)}) collective-permute-start(f32[4,128,1024]{2,1,0:T(8,128)S(1)} %get-tuple-element.77.refs_2_), channel_id=1, source_target_pairs={{0,1},{1,0},{2,3},{3,2},{4,5},{5,4},{6,7},{7,6},{8,9},{9,8},{10,11... | collective-permute-start | bytes 6291464 | tf_op jit(solution)/shard_map/ppermute | solution.py:472
  24.8 5.6 %collective-permute-start.3 = (f32[4,128,512]{2,1,0:T(8,128)S(1)}, f32[4,128,512]{2,1,0:T(8,128)S(1)}, u32[]{:S(2)}, u32[]{:S(2)}) collective-permute-start(f32[4,128,512]{2,1,0:T(8,128)S(1)} %shard_map.93.refs_2_), channel_id=1, source_target_pairs={{0,1},{1,0},{2,3},{3,2},{4,5},{5,4},{6,7},{7,6},{8,9},{9,8},{10,11... | collective-permute-start | bytes 3145736 | tf_op jit(solution)/shard_map/ppermute | solution.py:472
  37.1 23.5 %collective-permute-start.5 = (f32[4,128,1024]{2,1,0:T(8,128)S(1)}, f32[4,128,1024]{2,1,0:T(8,128)S(1)}, u32[]{:S(2)}, u32[]{:S(2)}) collective-permute-start(f32[4,128,1024]{2,1,0:T(8,128)S(1)} %get-tuple-element.81.refs_4_), channel_id=1, source_target_pairs={{0,1},{1,0},{2,3},{3,2},{4,5},{5,4},{6,7},{7,6},{8,9},{9,8},{10,11... | collective-permute-start | bytes 6291464 | tf_op jit(solution)/shard_map/ppermute | solution.py:472
  37.3 10.0 %collective-permute-start.14 = (f32[2,128,256]{2,1,0:T(8,128)S(1)}, f32[2,128,256]{2,1,0:T(8,128)S(1)}, u32[]{:S(2)}, u32[]{:S(2)}) collective-permute-start(f32[2,128,256]{2,1,0:T(8,128)S(1)} %get-tuple-element.96), channel_id=1, source_target_pairs={{0,2},{1,3},{2,0},{3,1},{4,6},{5,7},{6,4},{7,5},{8,10},{9,11},{10,... | collective-permute-start | bytes 786440 | tf_op jit(solution)/shard_map/ppermute | solution.py:472
  40.2 9.2 %collective-permute-start.16 = (f32[2,128,256]{2,1,0:T(8,128)S(1)}, f32[2,128,256]{2,1,0:T(8,128)S(1)}, u32[]{:S(2)}, u32[]{:S(2)}) collective-permute-start(f32[2,128,256]{2,1,0:T(8,128)S(1)} %get-tuple-element.99), channel_id=1, source_target_pairs={{0,4},{1,5},{2,6},{3,7},{4,0},{5,1},{6,2},{7,3},{8,12},{9,13},{10,... | collective-permute-start | bytes 786440 | tf_op jit(solution)/shard_map/ppermute | solution.py:472
  41.7 11.2 %collective-permute-start.15 = (f32[2,128,256]{2,1,0:T(8,128)S(1)}, f32[2,128,256]{2,1,0:T(8,128)S(1)}, u32[]{:S(2)}, u32[]{:S(2)}) collective-permute-start(f32[2,128,256]{2,1,0:T(8,128)S(1)} %get-tuple-element.97), channel_id=1, source_target_pairs={{0,2},{1,3},{2,0},{3,1},{4,6},{5,7},{6,4},{7,5},{8,10},{9,11},{10,... | collective-permute-start | bytes 786440 | tf_op jit(solution)/shard_map/ppermute | solution.py:472
  42.2 12.8 %collective-permute-start.17 = (f32[2,128,256]{2,1,0:T(8,128)S(1)}, f32[2,128,256]{2,1,0:T(8,128)S(1)}, u32[]{:S(2)}, u32[]{:S(2)}) collective-permute-start(f32[2,128,256]{2,1,0:T(8,128)S(1)} %get-tuple-element.101), channel_id=1, source_target_pairs={{0,4},{1,5},{2,6},{3,7},{4,0},{5,1},{6,2},{7,3},{8,12},{9,13},{10,... | collective-permute-start | bytes 786440 | tf_op jit(solution)/shard_map/ppermute | solution.py:472
  47.3 11.2 %collective-permute-start.10 = (f32[2,128,256]{2,1,0:T(8,128)S(1)}, f32[2,128,256]{2,1,0:T(8,128)S(1)}, u32[]{:S(2)}, u32[]{:S(2)}) collective-permute-start(f32[2,128,256]{2,1,0:T(8,128)S(1)} %get-tuple-element.90), channel_id=1, source_target_pairs={{0,2},{1,3},{2,0},{3,1},{4,6},{5,7},{6,4},{7,5},{8,10},{9,11},{10,... | collective-permute-start | bytes 786440 | tf_op jit(solution)/shard_map/ppermute | solution.py:472
  49.4 29.9 %collective-permute-start.8 = (f32[2,128,512]{2,1,0:T(8,128)S(1)}, f32[2,128,512]{2,1,0:T(8,128)S(1)}, u32[]{:S(2)}, u32[]{:S(2)}) collective-permute-start(f32[2,128,512]{2,1,0:T(8,128)S(1)} %get-tuple-element.87), channel_id=1, source_target_pairs={{0,2},{1,3},{2,0},{3,1},{4,6},{5,7},{6,4},{7,5},{8,10},{9,11},{10,... | collective-permute-start | bytes 1572872 | tf_op jit(solution)/shard_map/ppermute | solution.py:472
  52.9 26.3 %collective-permute-start.9 = (f32[2,128,512]{2,1,0:T(8,128)S(1)}, f32[2,128,512]{2,1,0:T(8,128)S(1)}, u32[]{:S(2)}, u32[]{:S(2)}) collective-permute-start(f32[2,128,512]{2,1,0:T(8,128)S(1)} %get-tuple-element.89), channel_id=1, source_target_pairs={{0,4},{1,5},{2,6},{3,7},{4,0},{5,1},{6,2},{7,3},{8,12},{9,13},{10,... | collective-permute-start | bytes 1572872 | tf_op jit(solution)/shard_map/ppermute | solution.py:472
  55.0 18.4 %collective-permute-start.12 = (f32[2,128,256]{2,1,0:T(8,128)S(1)}, f32[2,128,256]{2,1,0:T(8,128)S(1)}, u32[]{:S(2)}, u32[]{:S(2)}) collective-permute-start(f32[2,128,256]{2,1,0:T(8,128)S(1)} %get-tuple-element.93), channel_id=1, source_target_pairs={{0,4},{1,5},{2,6},{3,7},{4,0},{5,1},{6,2},{7,3},{8,12},{9,13},{10,... | collective-permute-start | bytes 786440 | tf_op jit(solution)/shard_map/ppermute | solution.py:472
  58.6 16.9 %collective-permute-start.11 = (f32[2,128,256]{2,1,0:T(8,128)S(1)}, f32[2,128,256]{2,1,0:T(8,128)S(1)}, u32[]{:S(2)}, u32[]{:S(2)}) collective-permute-start(f32[2,128,256]{2,1,0:T(8,128)S(1)} %get-tuple-element.91), channel_id=1, source_target_pairs={{0,2},{1,3},{2,0},{3,1},{4,6},{5,7},{6,4},{7,5},{8,10},{9,11},{10,... | collective-permute-start | bytes 786440 | tf_op jit(solution)/shard_map/ppermute | solution.py:472
  60.6 17.8 %collective-permute-start.13 = (f32[2,128,256]{2,1,0:T(8,128)S(1)}, f32[2,128,256]{2,1,0:T(8,128)S(1)}, u32[]{:S(2)}, u32[]{:S(2)}) collective-permute-start(f32[2,128,256]{2,1,0:T(8,128)S(1)} %get-tuple-element.95), channel_id=1, source_target_pairs={{0,4},{1,5},{2,6},{3,7},{4,0},{5,1},{6,2},{7,3},{8,12},{9,13},{10,... | collective-permute-start | bytes 786440 | tf_op jit(solution)/shard_map/ppermute | solution.py:472
  65.2 12.3 %copy-start = (f32[1,512,1024]{2,1,0:T(8,128)S(1)}, f32[1,512,1024]{2,1,0:T(8,128)}, u32[]{:S(2)}) copy-start(f32[1,512,1024]{2,1,0:T(8,128)} %refs_4_.3) | copy-start | bytes 6291460
  65.2 12.3 %copy-start.1 = (bf16[768,64]{1,0:T(8,128)(2,1)S(1)}, bf16[768,64]{1,0:T(8,128)(2,1)}, u32[]{:S(2)}) copy-start(bf16[768,64]{1,0:T(8,128)(2,1)} %constant.28.refs_10_.refs_6_) | copy-start | bytes 294916
  65.2 12.3 %copy-start.2 = (bf16[32,384]{1,0:T(8,128)(2,1)S(1)}, bf16[32,384]{1,0:T(8,128)(2,1)}, u32[]{:S(2)}) copy-start(bf16[32,384]{1,0:T(8,128)(2,1)} %constant.23.refs_9_.refs_5_) | copy-start | bytes 73732
  73.4 22.4 %collective-permute-start.6 = (f32[2,128,512]{2,1,0:T(8,128)S(1)}, f32[2,128,512]{2,1,0:T(8,128)S(1)}, u32[]{:S(2)}, u32[]{:S(2)}) collective-permute-start(f32[2,128,512]{2,1,0:T(8,128)S(1)} %get-tuple-element.84), channel_id=1, source_target_pairs={{0,2},{1,3},{2,0},{3,1},{4,6},{5,7},{6,4},{7,5},{8,10},{9,11},{10,... | collective-permute-start | bytes 1572872 | tf_op jit(solution)/shard_map/ppermute | solution.py:472
  75.4 21.9 %collective-permute-start.7 = (f32[2,128,512]{2,1,0:T(8,128)S(1)}, f32[2,128,512]{2,1,0:T(8,128)S(1)}, u32[]{:S(2)}, u32[]{:S(2)}) collective-permute-start(f32[2,128,512]{2,1,0:T(8,128)S(1)} %get-tuple-element.86), channel_id=1, source_target_pairs={{0,4},{1,5},{2,6},{3,7},{4,0},{5,1},{6,2},{7,3},{8,12},{9,13},{10,... | collective-permute-start | bytes 1572872 | tf_op jit(solution)/shard_map/ppermute | solution.py:472
  80.1 13.7 %collective-permute-start.23 = (f32[1,128,512]{2,1,0:T(8,128)S(1)}, f32[1,128,512]{2,1,0:T(8,128)S(1)}, u32[]{:S(2)}, u32[]{:S(2)}) collective-permute-start(f32[1,128,512]{2,1,0:T(8,128)S(1)} %get-tuple-element.123), channel_id=1, source_target_pairs={{0,2},{1,3},{2,0},{3,1},{4,6},{5,7},{6,4},{7,5},{8,10},{9,11},{10,... | collective-permute-start | bytes 786440 | tf_op jit(solution)/shard_map/ppermute | solution.py:472
  81.6 17.1 %collective-permute-start.22 = (f32[1,128,512]{2,1,0:T(8,128)S(1)}, f32[1,128,512]{2,1,0:T(8,128)S(1)}, u32[]{:S(2)}, u32[]{:S(2)}) collective-permute-start(f32[1,128,512]{2,1,0:T(8,128)S(1)} %get-tuple-element.116.refs_11_), channel_id=1, source_target_pairs={{0,4},{1,5},{2,6},{3,7},{4,0},{5,1},{6,2},{7,3},{8,12},{9,13},{10,... | collective-permute-start | bytes 786440 | tf_op jit(solution)/shard_map/ppermute | solution.py:472
  82.1 18.1 %collective-permute-start.25 = (f32[2,128,256]{2,1,0:T(8,128)S(1)}, f32[2,128,256]{2,1,0:T(8,128)S(1)}, u32[]{:S(2)}, u32[]{:S(2)}) collective-permute-start(f32[2,128,256]{2,1,0:T(8,128)S(1)} %get-tuple-element.124), channel_id=1, source_target_pairs={{0,2},{1,3},{2,0},{3,1},{4,6},{5,7},{6,4},{7,5},{8,10},{9,11},{10,... | collective-permute-start | bytes 786440 | tf_op jit(solution)/shard_map/ppermute | solution.py:472
  93.8 17.0 %collective-permute-start.24 = (f32[2,128,256]{2,1,0:T(8,128)S(1)}, f32[2,128,256]{2,1,0:T(8,128)S(1)}, u32[]{:S(2)}, u32[]{:S(2)}) collective-permute-start(f32[2,128,256]{2,1,0:T(8,128)S(1)} %get-tuple-element.111.refs_11_), channel_id=1, source_target_pairs={{0,4},{1,5},{2,6},{3,7},{4,0},{5,1},{6,2},{7,3},{8,12},{9,13},{10,... | collective-permute-start | bytes 786440 | tf_op jit(solution)/shard_map/ppermute | solution.py:472
  95.8 18.7 %collective-permute-start.27 = (f32[2,128,256]{2,1,0:T(8,128)S(1)}, f32[2,128,256]{2,1,0:T(8,128)S(1)}, u32[]{:S(2)}, u32[]{:S(2)}) collective-permute-start(f32[2,128,256]{2,1,0:T(8,128)S(1)} %get-tuple-element.125), channel_id=1, source_target_pairs={{0,2},{1,3},{2,0},{3,1},{4,6},{5,7},{6,4},{7,5},{8,10},{9,11},{10,... | collective-permute-start | bytes 786440 | tf_op jit(solution)/shard_map/ppermute | solution.py:472
  97.3 17.2 %collective-permute-start.26 = (f32[2,128,256]{2,1,0:T(8,128)S(1)}, f32[2,128,256]{2,1,0:T(8,128)S(1)}, u32[]{:S(2)}, u32[]{:S(2)}) collective-permute-start(f32[2,128,256]{2,1,0:T(8,128)S(1)} %get-tuple-element.106.refs_15_), channel_id=1, source_target_pairs={{0,4},{1,5},{2,6},{3,7},{4,0},{5,1},{6,2},{7,3},{8,12},{9,13},{10,... | collective-permute-start | bytes 786440 | tf_op jit(solution)/shard_map/ppermute | solution.py:472
  97.8 17.5 %copy-start.3 = (bf16[192,256]{1,0:T(8,128)(2,1)S(1)}, bf16[192,256]{1,0:T(8,128)(2,1)}, u32[]{:S(2)}) copy-start(bf16[192,256]{1,0:T(8,128)(2,1)} %constant.38.refs_3_.refs_5_) | copy-start | bytes 294916
  97.8 17.5 %copy-start.4 = (bf16[128,96]{1,0:T(8,128)(2,1)S(1)}, bf16[128,96]{1,0:T(8,128)(2,1)}, u32[]{:S(2)}) copy-start(bf16[128,96]{1,0:T(8,128)(2,1)} %constant.33.refs_2_.refs_4_) | copy-start | bytes 73732
  98.7 8.6 %collective-permute-start.18 = (f32[128,128]{1,0:T(8,128)S(1)}, f32[128,128]{1,0:T(8,128)S(1)}, u32[]{:S(2)}, u32[]{:S(2)}) collective-permute-start(f32[128,128]{1,0:T(8,128)S(1)} %get-tuple-element.119), channel_id=1, source_target_pairs={{0,4},{1,5},{2,6},{3,7},{4,0},{5,1},{6,2},{7,3},{8,12},{9,13},{10,... | collective-permute-start | bytes 196616 | tf_op jit(solution)/shard_map/ppermute | solution.py:472
  100.3 9.1 %collective-permute-start.19 = (f32[128,128]{1,0:T(8,128)S(1)}, f32[128,128]{1,0:T(8,128)S(1)}, u32[]{:S(2)}, u32[]{:S(2)}) collective-permute-start(f32[128,128]{1,0:T(8,128)S(1)} %get-tuple-element.120), channel_id=1, source_target_pairs={{0,2},{1,3},{2,0},{3,1},{4,6},{5,7},{6,4},{7,5},{8,10},{9,11},{10,... | collective-permute-start | bytes 196616 | tf_op jit(solution)/shard_map/ppermute | solution.py:472
  107.3 15.7 %collective-permute-start.20 = (f32[1,128,512]{2,1,0:T(8,128)S(1)}, f32[1,128,512]{2,1,0:T(8,128)S(1)}, u32[]{:S(2)}, u32[]{:S(2)}) collective-permute-start(f32[1,128,512]{2,1,0:T(8,128)S(1)} %get-tuple-element.121), channel_id=1, source_target_pairs={{0,4},{1,5},{2,6},{3,7},{4,0},{5,1},{6,2},{7,3},{8,12},{9,13},{10,... | collective-permute-start | bytes 786440 | tf_op jit(solution)/shard_map/ppermute | solution.py:472
  109.3 13.7 %collective-permute-start.21 = (f32[1,128,512]{2,1,0:T(8,128)S(1)}, f32[1,128,512]{2,1,0:T(8,128)S(1)}, u32[]{:S(2)}, u32[]{:S(2)}) collective-permute-start(f32[1,128,512]{2,1,0:T(8,128)S(1)} %get-tuple-element.122), channel_id=1, source_target_pairs={{0,2},{1,3},{2,0},{3,1},{4,6},{5,7},{6,4},{7,5},{8,10},{9,11},{10,... | collective-permute-start | bytes 786440 | tf_op jit(solution)/shard_map/ppermute | solution.py:472
  110.8 8.0 %collective-permute-start.30 = (f32[128,256]{1,0:T(8,128)S(1)}, f32[128,256]{1,0:T(8,128)S(1)}, u32[]{:S(2)}, u32[]{:S(2)}) collective-permute-start(f32[128,256]{1,0:T(8,128)S(1)} %shard_map.107.refs_1_.refs_0_), channel_id=1, source_target_pairs={{0,24},{8,16},{16,8},{24,0},{1,25},{9,17},{17,9},{25,1},{2,26},{10... | collective-permute-start | bytes 393224 | tf_op jit(solution)/shard_map/ppermute | solution.py:472
  114.5 6.6 %collective-permute-start.29 = (f32[128,256]{1,0:T(8,128)S(1)}, f32[128,256]{1,0:T(8,128)S(1)}, u32[]{:S(2)}, u32[]{:S(2)}) collective-permute-start(f32[128,256]{1,0:T(8,128)S(1)} %shard_map.107.refs_1_.refs_0_), channel_id=1, source_target_pairs={{0,16},{8,24},{16,0},{24,8},{1,17},{9,25},{17,1},{25,9},{2,18},{10... | collective-permute-start | bytes 393224 | tf_op jit(solution)/shard_map/ppermute | solution.py:472
  114.5 6.6 %collective-permute-start.28 = (f32[128,256]{1,0:T(8,128)S(1)}, f32[128,256]{1,0:T(8,128)S(1)}, u32[]{:S(2)}, u32[]{:S(2)}) collective-permute-start(f32[128,256]{1,0:T(8,128)S(1)} %shard_map.107.refs_1_.refs_0_), channel_id=1, source_target_pairs={{0,8},{8,0},{16,24},{24,16},{1,9},{9,1},{17,25},{25,17},{2,10},{10... | collective-permute-start | bytes 393224 | tf_op jit(solution)/shard_map/ppermute | solution.py:472

commit v4 on v3

--- a/solution.py
+++ b/solution.py
@@ -9,7 +9,6 @@
 CH = 64
 BAND = 16
 EPS = 1e-05
-LATE = (5,)
 ROWS = 128
 SPAN = 256
 
@@ -124,7 +123,11 @@
     return slice(side * cols // 2 + q, side * cols // 2 + q + w)
 
 
-def first_call(x, c, owners, n, rows, chunk):
+def picked(xt_ref, masks, r, at=slice(None)):
+    return jnp.concatenate([xt_ref[m // 2 * r : (m // 2 + 1) * r, at] for m in masks], axis=0)
+
+
+def first_call(x, c, owners, n, rows, chunk, masks):
     off, q, w = chunk
     r = ROWS
     tokens, width = x.shape
@@ -199,14 +202,16 @@
         cut = (steps - 2) * tile
         for side in range(2):
             p_ref[:, :, side * w : (side + 1) * w] = jnp.dot(
-                xt_ref[:, :cut], c_ref[:cut, parts[side]], preferred_element_type=F32
-            ).reshape(half, r, w)
+                picked(xt_ref, masks[side], r, slice(0, cut)), c_ref[:cut, parts[side]],
+                preferred_element_type=F32,
+            ).reshape(-1, r, w)
         both(steps - 2, 0)
         turn(steps - 1, s_ref[rows_at(steps - 1), :])
         for side in range(2):
             p_ref[:, :, side * w : (side + 1) * w] += jnp.dot(
-                xt_ref[:, cut:], c_ref[cut:, parts[side]], preferred_element_type=F32
-            ).reshape(half, r, w)
+                picked(xt_ref, masks[side], r, slice(cut, tokens)), c_ref[cut:, parts[side]],
+                preferred_element_type=F32,
+            ).reshape(-1, r, w)
         for copy in rest:
             copy.wait()
 
@@ -216,7 +221,7 @@
             pltpu.VMEM(x.shape, x.dtype),
             pltpu.VMEM(c.shape, c.dtype),
             pltpu.VMEM((tokens, 128), F32),
-            pltpu.VMEM((half, r, 2 * w), F32),
+            pltpu.VMEM((len(masks[0]), r, 2 * w), F32),
             pltpu.VMEM((half * r, tokens), jnp.bfloat16),
             pltpu.VMEM((half * r, tokens), jnp.bfloat16),
         ),
@@ -232,7 +237,7 @@
     )(owners, *[pltpu.with_memory_space_constraint(a, pltpu.HBM) for a in (x, c)])
 
 
-def product_call(x, scale, c, owners, n, rows, chunk, parity, xt, tokens):
+def product_call(x, scale, c, owners, n, rows, chunk, parity, masks, xt, tokens):
     off, q, w = chunk
     r = ROWS
     cols = c.shape[1]
@@ -241,15 +246,16 @@
     def multiply(xt_ref, c_ref, out_ref):
         for side in range(2):
             out_ref[:, :, side * w : (side + 1) * w] = jnp.dot(
-                xt_ref[...], c_ref[:, columns(side, cols, q, w)], preferred_element_type=F32
-            ).reshape(half, r, w)
+                picked(xt_ref, masks[side], r), c_ref[:, columns(side, cols, q, w)],
+                preferred_element_type=F32,
+            ).reshape(-1, r, w)
 
     def kernel(own, x_ref, s_ref, c_ref, out_ref, xt_ref):
         fill(xt_ref, x_ref, s_ref, [own[2 * j + parity] * rows + off for j in range(half)], r)
         multiply(xt_ref, c_ref, out_ref)
 
-    shape = (half, r, 2 * w)
-    flops = 4 * x.shape[0] * half * r * w
+    shape = (len(masks[0]), r, 2 * w)
+    flops = 4 * x.shape[0] * len(masks[0]) * r * w
     if xt is not None:
         (out,) = on_chip(multiply, [xt, c], tokens, [shape], flops=flops)
         return out, xt
@@ -259,24 +265,22 @@
     )
 
 
-def part_call(even, got, sends, keeps, tokens):
+def part_call(even, got, picks, tokens):
     r, w = even.shape[1], even.shape[2] // 2
 
     def kernel(even_ref, got_ref, *outs):
         for side in range(2):
             at = slice(side * w, (side + 1) * w)
-            for out, masks in ((outs[2 * side], sends[side]), (outs[2 * side + 1], keeps[side])):
-                for k, m in enumerate(masks):
-                    out[k] = even_ref[m // 2, :, at] + got_ref[m // 2, :, at]
-
-    shapes = [(len(m), r, w) for side in range(2) for m in (sends[side], keeps[side])]
-    return on_chip(kernel, [even, got], tokens, shapes)
+            for k, j in enumerate(picks[side]):
+                outs[side][k] = even_ref[j, :, at] + got_ref[j, :, at]
+
+    return on_chip(kernel, [even, got], tokens, [(len(pick), r, w) for pick in picks])
 
 
 def add_up(terms, refs):
     total = None
-    for array, at in terms:
-        value = refs[array][at]
+    for array, at, lanes in terms:
+        value = refs[array][at, :, lanes]
         total = value if total is None else total + value
     return total
 
@@ -290,7 +294,7 @@
             arrays.append(array)
         return places[id(array)]
 
-    plan = [[[(place(a), at) for a, at in terms] for terms in group] for group in groups]
+    plan = [[[(place(a), *at) for a, *at in terms] for terms in group] for group in groups]
     return arrays, plan
 
 
@@ -473,48 +477,84 @@
 
     row_groups = chunks_of(rows, wide)
     chunks = [chunk for group in row_groups for chunk in group]
-    x, c, scale, odd, *xts = first_call(x, c, owners, n, rows, chunks[0])
+    x, c, scale, odd, *xts = first_call(x, c, owners, n, rows, chunks[0], sends)
     token = odd
-    kept = {(1, chunks[0][0]): xts[0], (0, chunks[0][0]): xts[1]}
-
-    def product(k, parity):
-        at = parity, chunks[k][0]
-        out, kept[at] = product_call(
-            x, scale, c, owners, n, rows, chunks[k], parity, kept.get(at), [token]
+    turned = {(1, chunks[0][0]): xts[0], (0, chunks[0][0]): xts[1]}
+
+    def product(chunk, parity, masks):
+        at = parity, chunk[0]
+        out, turned[at] = product_call(
+            x, scale, c, owners, n, rows, chunk, parity, masks, turned.get(at), [token]
         )
         return out
 
+    def masks_of(chunk):
+        return sends if chunk[2] < wide else [list(evens)] * 2
+
     got = swap(odd, 1)
-    state = []
+    backs = []
+    whole_of = {}
     for k, chunk in enumerate(chunks):
-        even = product(k, 0)
+        even = product(chunk, 0, masks_of(chunk))
         token = even
         here = got
-        if k + 1 < len(chunks) and k + 1 not in LATE:
-            odd = product(k + 1, 1)
+        if k + 1 < len(chunks):
+            odd = product(chunks[k + 1], 1, masks_of(chunks[k + 1]))
             token = odd
             got = swap(odd, 1)
-        outs = part_call(even, here, sends, keeps, [token])
+        outs = part_call(
+            even, here,
+            [[masks_of(chunk)[side].index(m) for m in sends[side]] for side in range(2)], [token],
+        )
         token = outs[1]
-        if k + 1 < len(chunks) and k + 1 in LATE:
-            odd = product(k + 1, 1)
+        if chunk[2] == wide:
+            whole_of[chunk[0]] = even, here
+        backs.append([swap(outs[side], orders[side][0]) for side in range(2)])
+
+    state = []
+    first = 0
+    for group in row_groups:
+        off = group[0][0]
+        full = (off, 0, wide)
+        for parity in range(2):
+            turned.pop((parity, off), None)
+        held = masks_of(group[0])
+        if off in whole_of:
+            even, got = whole_of[off]
+        else:
+            held = keeps
+            odd = product(full, 1, keeps)
             token = odd
             got = swap(odd, 1)
-        terms = []
-        for side in range(2):
-            back = swap(outs[2 * side], orders[side][0])
-            terms.append({m: [(outs[2 * side + 1], j), (back, j)] for j, m in enumerate(keeps[side])})
-        for stage in range(1, len(bits) - 1):
-            now = [orders[side][stage] for side in range(2)]
-            out = stage_call(
-                [[terms[side][m] for m in sorted(terms[side]) if m & now[side]] for side in range(2)],
-                ROWS, chunk[2], [],
-            )
+            even = product(full, 0, keeps)
+            token = even
+        for k, (_, q, w) in enumerate(group):
+            terms = []
             for side in range(2):
-                back = swap(out[side], now[side])
-                keep = [m for m in sorted(terms[side]) if not m & now[side]]
-                terms[side] = {m: terms[side][m] + [(back, j)] for j, m in enumerate(keep)}
-        state.append(terms)
+                lanes = slice(side * wide + q, side * wide + q + w)
+                back = backs[first + k][side]
+                terms.append({
+                    m: [
+                        (even, held[side].index(m), lanes),
+                        (got, held[side].index(m), lanes),
+                        (back, j, slice(0, w)),
+                    ]
+                    for j, m in enumerate(keeps[side])
+                })
+            for stage in range(1, len(bits) - 1):
+                now = [orders[side][stage] for side in range(2)]
+                out = stage_call(
+                    [[terms[side][m] for m in sorted(terms[side]) if m & now[side]] for side in range(2)],
+                    ROWS, w, [],
+                )
+                for side in range(2):
+                    back = swap(out[side], now[side])
+                    keep = [m for m in sorted(terms[side]) if not m & now[side]]
+                    terms[side] = {
+                        m: terms[side][m] + [(back, j, slice(0, w))] for j, m in enumerate(keep)
+                    }
+            state.append(terms)
+        first += len(group)
 
     ends = [order[-1] for order in orders]
     before = None

time: 124 us -> 128 us (1.032)
  Pallas kernels: 42.6 us -> 51.3 us
  starting transfers between devices: 35.8 us -> 27.4 us
  waiting for transfers between devices: 44.7 us -> 48.6 us
    pallas_call x23 -> x27, Pallas kernels: 28 us -> 37.3 us  [on_chip(): pl.pallas_call(run, out_shape=tuple((pltpu.VMEM(shape, kind) for shape, k...]
    ppermute x31 -> x33, starting transfers between devices: 35.8 us -> 27.4 us  [swap(): return lax.ppermute(value, axis, [(i, i ^ bit) for i in range(size)])]
    ppermute x31 -> x33, waiting for transfers between devices: 44.7 us -> 48.6 us  [swap(): return lax.ppermute(value, axis, [(i, i ^ bit) for i in range(size)])]
  transfers between devices with their start and end apart: 31 -> 33, of which waited for: 8 -> 17; matrix products, arithmetic and copies ran while one was open for 0% -> 0% of each run, Pallas kernels for 20% -> 29%
where the time goes in v4:
time: 128 us
  Pallas kernels  51.3 us (40%)
  waiting for transfers between devices  48.6 us (38%)
  starting transfers between devices  27.4 us (21%)
    ppermute x33, waiting for transfers between devices, swap(): return lax.ppermute(value, axis, [(i, i ^ bit) for i in range(size)])  48.6 us
    pallas_call x27, Pallas kernels, on_chip(): pl.pallas_call(run, out_shape=tuple((pltpu.VMEM(shape, kind) for shape, k...  37.3 us
    ppermute x33, starting transfers between devices, swap(): return lax.ppermute(value, axis, [(i, i ^ bit) for i in range(size)])  27.4 us
    pallas_call x1, Pallas kernels, first_call(): pl.pallas_call(kernel, out_shape=(pltpu.VMEM(x.shape, x.dtype), pltpu.VME...  8.72 us
    pallas_call x5, Pallas kernels, outward(): pl.pallas_call(run, out_shape=jax.ShapeDtypeStruct(shape, F32), in_specs=...  5.27 us
  transfers between devices with their start and end apart: 33, of which 17 were waited for; matrix products, arithmetic and copies ran while one was open for 0% of the time, Pallas kernels for 29%

profile of v4, /device:TPU:0, one launch (start us, length us, event | category | flops | bytes accessed | tf_op | source)
XLA Modules:
  0.0 128.3 jit_solution(10533306816199118111)
XLA Ops:
  0.6 8.7 %first.1 = (bf16[2048,4096]{1,0:T(8,128)(2,1)S(1)}, bf16[2048,1024]{1,0:T(8,128)(2,1)S(1)}, f32[2048,128]{1,0:T(8,128)S(1)}, f32[2,128,512]{2,1,0:T(8,128)S(1)},...) custom-call(s32[8]{0:T(128)S(1)} %iota_xor_fusion.own.refs_0_, bf16[2048,4096]{1,0:T(8,128)(2,1)} %bitcast.2, ...), custom_call_target="tpu_custom_call" | custom-call | flops 1073741824 | bytes 20971520 | tf_op jit(solution)/shard_map/first/pallas_call | solution.py:218
  9.4 0.6 collective-permute-start
  9.9 0.7 shard_map.86.refs_2_.refs_0_
  10.6 0.7 shard_map.87.refs_2_
  11.5 0.7 shard_map.89.refs_4_.refs_0_
  12.2 1.6 %shard_map.90 = (f32[2,128,512]{2,1,0:T(8,128)S(1)}, bf16[512,2048]{1,0:T(8,128)(2,1)S(1)}) custom-call(s32[8]{0:T(128)S(1)} %iota_xor_fusion.own.refs_0_, bf16[2048,4096]{1,0:T(8,128)(2,1)S(1)} %get-tuple-element.56.refs_1_, f32[2048,128]{1,0:T(8,128)S(1)} %get-tuple-element.57.refs_2_, bf16[2048,1024]{1,0:T(8,128)(2,1)S(1)} %get-tuple-element.58.refs_1_.refs_3_, ...), custom_call_target="tpu_custom_call" | custom-call | flops 536870912 | tf_op jit(solution)/shard_map/pallas_call | solution.py:103
  13.8 0.5 collective-permute-start.2
  14.4 1.6 %shard_map.92 = (f32[2,128,512]{2,1,0:T(8,128)S(1)}, bf16[512,2048]{1,0:T(8,128)(2,1)S(1)}) custom-call(s32[8]{0:T(128)S(1)} %iota_xor_fusion.own.refs_0_, bf16[2048,4096]{1,0:T(8,128)(2,1)S(1)} %get-tuple-element.56.refs_1_, f32[2048,128]{1,0:T(8,128)S(1)} %get-tuple-element.57.refs_2_, bf16[2048,1024]{1,0:T(8,128)(2,1)S(1)} %get-tuple-element.58.refs_1_.refs_3_, ...), custom_call_target="tpu_custom_call" | custom-call | flops 536870912 | tf_op jit(solution)/shard_map/pallas_call | solution.py:103
  16.0 0.7 shard_map.93.refs_2_
  16.9 0.7 shard_map.95.refs_4_.refs_0_
  17.6 3.0 %shard_map.96 = (f32[4,128,1024]{2,1,0:T(8,128)S(1)}, bf16[512,2048]{1,0:T(8,128)(2,1)}) custom-call(s32[8]{0:T(128)S(1)} %iota_xor_fusion.own.refs_0_, bf16[2048,4096]{1,0:T(8,128)(2,1)S(1)} %get-tuple-element.56.refs_1_, f32[2048,128]{1,0:T(8,128)S(1)} %get-tuple-element.57.refs_2_, bf16[2048,1024]{1,0:T(8,128)(2,1)S(1)} %get-tuple-element.58.refs_1_.refs_3_, ...), custom_call_target="tpu_custom_call" | custom-call | flops 2147483648 | tf_op jit(solution)/shard_map/pallas_call | solution.py:103
  20.6 0.5 collective-permute-start.4
  21.2 3.0 %shard_map.98 = (f32[4,128,1024]{2,1,0:T(8,128)S(1)}, bf16[512,2048]{1,0:T(8,128)(2,1)}) custom-call(s32[8]{0:T(128)S(1)} %iota_xor_fusion.own.refs_0_, bf16[2048,4096]{1,0:T(8,128)(2,1)S(1)} %get-tuple-element.56.refs_1_, f32[2048,128]{1,0:T(8,128)S(1)} %get-tuple-element.57.refs_2_, bf16[2048,1024]{1,0:T(8,128)(2,1)S(1)} %get-tuple-element.58.refs_1_.refs_3_, ...), custom_call_target="tpu_custom_call" | custom-call | flops 2147483648 | tf_op jit(solution)/shard_map/pallas_call | solution.py:103
  24.3 3.0 %shard_map.99 = (f32[4,128,1024]{2,1,0:T(8,128)S(1)}, bf16[512,2048]{1,0:T(8,128)(2,1)}) custom-call(s32[8]{0:T(128)S(1)} %iota_xor_fusion.own.refs_0_, bf16[2048,4096]{1,0:T(8,128)(2,1)S(1)} %get-tuple-element.56.refs_1_, f32[2048,128]{1,0:T(8,128)S(1)} %get-tuple-element.57.refs_2_, bf16[2048,1024]{1,0:T(8,128)(2,1)S(1)} %get-tuple-element.58.refs_1_.refs_3_, ...), custom_call_target="tpu_custom_call" | custom-call | flops 2147483648 | tf_op jit(solution)/shard_map/pallas_call | solution.py:103
  27.5 3.2 %shard_map.101 = (f32[4,128,1024]{2,1,0:T(8,128)S(1)}, bf16[512,2048]{1,0:T(8,128)(2,1)}) custom-call(s32[8]{0:T(128)S(1)} %iota_xor_fusion.own.refs_0_, bf16[2048,4096]{1,0:T(8,128)(2,1)S(1)} %get-tuple-element.56.refs_1_, f32[2048,128]{1,0:T(8,128)S(1)} %get-tuple-element.57.refs_2_, bf16[2048,1024]{1,0:T(8,128)(2,1)S(1)} %get-tuple-element.58.refs_1_.refs_3_, ...), custom_call_target="tpu_custom_call" | custom-call | flops 2147483648 | tf_op jit(solution)/shard_map/pallas_call | solution.py:103
  30.7 0.8 collective-permute-done.5.refs_1_
  31.6 3.3 %shard_map.103 = (f32[2,128,1024]{2,1,0:T(8,128)S(1)}, bf16[512,2048]{1,0:T(8,128)(2,1)}) custom-call(s32[8]{0:T(128)S(1)} %iota_xor_fusion.own.refs_0_, bf16[2048,4096]{1,0:T(8,128)(2,1)S(1)} %get-tuple-element.56.refs_1_, f32[2048,128]{1,0:T(8,128)S(1)} %get-tuple-element.57.refs_2_, bf16[2048,1024]{1,0:T(8,128)(2,1)S(1)} %get-tuple-element.58.refs_1_.refs_3_, ...), custom_call_target="tpu_custom_call" | custom-call | flops 1073741824 | tf_op jit(solution)/shard_map/pallas_call | solution.py:103
  35.0 2.8 %collective-permute-start.16 = (f32[2,128,256]{2,1,0:T(8,128)S(1)}, f32[2,128,256]{2,1,0:T(8,128)S(1)}, u32[]{:S(2)}, u32[]{:S(2)}) collective-permute-start(f32[2,128,256]{2,1,0:T(8,128)S(1)} %get-tuple-element.84), channel_id=1, source_target_pairs={{0,2},{1,3},{2,0},{3,1},{4,6},{5,7},{6,4},{7,5},{8,10},{9,11},{10,... | collective-permute-start | bytes 786440 | tf_op jit(solution)/shard_map/ppermute | solution.py:476
  37.8 1.5 %collective-permute-start.18 = (f32[2,128,256]{2,1,0:T(8,128)S(1)}, f32[2,128,256]{2,1,0:T(8,128)S(1)}, u32[]{:S(2)}, u32[]{:S(2)}) collective-permute-start(f32[2,128,256]{2,1,0:T(8,128)S(1)} %get-tuple-element.62.refs_2_), channel_id=1, source_target_pairs={{0,4},{1,5},{2,6},{3,7},{4,0},{5,1},{6,2},{7,3},{8,12},{9,13},{10,... | collective-permute-start | bytes 786440 | tf_op jit(solution)/shard_map/ppermute | solution.py:476
  39.4 3.3 %shard_map.104 = (f32[2,128,1024]{2,1,0:T(8,128)S(1)}, bf16[512,2048]{1,0:T(8,128)(2,1)}) custom-call(s32[8]{0:T(128)S(1)} %iota_xor_fusion.own.refs_0_, bf16[2048,4096]{1,0:T(8,128)(2,1)S(1)} %get-tuple-element.56.refs_1_, f32[2048,128]{1,0:T(8,128)S(1)} %get-tuple-element.57.refs_2_, bf16[2048,1024]{1,0:T(8,128)(2,1)S(1)} %get-tuple-element.58.refs_1_.refs_3_, ...), custom_call_target="tpu_custom_call" | custom-call | flops 1073741824 | tf_op jit(solution)/shard_map/pallas_call | solution.py:103
  42.7 3.3 %shard_map.105 = (f32[2,128,1024]{2,1,0:T(8,128)S(1)}, bf16[512,2048]{1,0:T(8,128)(2,1)}) custom-call(s32[8]{0:T(128)S(1)} %iota_xor_fusion.own.refs_0_, bf16[2048,4096]{1,0:T(8,128)(2,1)S(1)} %get-tuple-element.56.refs_1_, f32[2048,128]{1,0:T(8,128)S(1)} %get-tuple-element.57.refs_2_, bf16[2048,1024]{1,0:T(8,128)(2,1)S(1)} %get-tuple-element.58.refs_1_.refs_3_, ...), custom_call_target="tpu_custom_call" | custom-call | flops 1073741824 | tf_op jit(solution)/shard_map/pallas_call | solution.py:103
  45.9 0.5 collective-permute-start.17
  46.5 2.0 %collective-permute-start.11 = (f32[2,128,256]{2,1,0:T(8,128)S(1)}, f32[2,128,256]{2,1,0:T(8,128)S(1)}, u32[]{:S(2)}, u32[]{:S(2)}) collective-permute-start(f32[2,128,256]{2,1,0:T(8,128)S(1)} %get-tuple-element.82), channel_id=1, source_target_pairs={{0,2},{1,3},{2,0},{3,1},{4,6},{5,7},{6,4},{7,5},{8,10},{9,11},{10,... | collective-permute-start | bytes 786440 | tf_op jit(solution)/shard_map/ppermute | solution.py:476
  48.5 6.7 %collective-permute-done.17.refs_3_ = f32[2,128,256]{2,1,0:T(8,128)S(1)} collective-permute-done((f32[2,128,256]{2,1,0:T(8,128)S(1)}, f32[2,128,256]{2,1,0:T(8,128)S(1)}, u32[]{:S(2)}, u32[]{:S(2)}) %collective-permute-start.17) | collective-permute-done | bytes 262176 | tf_op jit(solution)/shard_map/ppermute | solution.py:476
  55.1 0.5 collective-permute-start.13
  55.6 0.8 collective-permute-start.12
  56.4 4.3 %collective-permute-done.11.refs_2_ = f32[2,128,256]{2,1,0:T(8,128)S(1)} collective-permute-done((f32[2,128,256]{2,1,0:T(8,128)S(1)}, f32[2,128,256]{2,1,0:T(8,128)S(1)}, u32[]{:S(2)}, u32[]{:S(2)}) %collective-permute-start.11) | collective-permute-done | bytes 262176 | tf_op jit(solution)/shard_map/ppermute | solution.py:476
  61.2 1.3 %collective-permute-done.13.refs_4_ = f32[2,128,256]{2,1,0:T(8,128)S(1)} collective-permute-done((f32[2,128,256]{2,1,0:T(8,128)S(1)}, f32[2,128,256]{2,1,0:T(8,128)S(1)}, u32[]{:S(2)}, u32[]{:S(2)}) %collective-permute-start.13) | collective-permute-done | bytes 262176 | tf_op jit(solution)/shard_map/ppermute | solution.py:476
  62.5 0.5 collective-permute-start.8
  63.1 3.3 %collective-permute-done.12.refs_3_ = f32[2,128,256]{2,1,0:T(8,128)S(1)} collective-permute-done((f32[2,128,256]{2,1,0:T(8,128)S(1)}, f32[2,128,256]{2,1,0:T(8,128)S(1)}, u32[]{:S(2)}, u32[]{:S(2)}) %collective-permute-start.12) | collective-permute-done | bytes 262176 | tf_op jit(solution)/shard_map/ppermute | solution.py:476
  66.4 0.5 collective-permute-start.9
  66.8 1.3 %collective-permute-done.14.refs_5_ = f32[2,128,256]{2,1,0:T(8,128)S(1)} collective-permute-done((f32[2,128,256]{2,1,0:T(8,128)S(1)}, f32[2,128,256]{2,1,0:T(8,128)S(1)}, u32[]{:S(2)}, u32[]{:S(2)}) %collective-permute-start.14) | collective-permute-done | bytes 262176 | tf_op jit(solution)/shard_map/ppermute | solution.py:476
  68.1 0.5 collective-permute-start.6
  69.1 3.3 %shard_map.106 = (f32[2,128,1024]{2,1,0:T(8,128)S(1)}, bf16[512,2048]{1,0:T(8,128)(2,1)}) custom-call(s32[8]{0:T(128)S(1)} %iota_xor_fusion.own.refs_0_, bf16[2048,4096]{1,0:T(8,128)(2,1)S(1)} %get-tuple-element.56.refs_1_, f32[2048,128]{1,0:T(8,128)S(1)} %get-tuple-element.57.refs_2_, bf16[2048,1024]{1,0:T(8,128)(2,1)S(1)} %get-tuple-element.58.refs_1_.refs_3_, ...), custom_call_target="tpu_custom_call" | custom-call | flops 1073741824 | tf_op jit(solution)/shard_map/pallas_call | solution.py:103
  72.4 0.9 shard_map.107
  73.4 0.9 shard_map.108
  74.3 3.3 %collective-permute-done.8.refs_2_ = f32[2,128,512]{2,1,0:T(8,128)S(1)} collective-permute-done((f32[2,128,512]{2,1,0:T(8,128)S(1)}, f32[2,128,512]{2,1,0:T(8,128)S(1)}, u32[]{:S(2)}, u32[]{:S(2)}) %collective-permute-start.8) | collective-permute-done | bytes 524320 | tf_op jit(solution)/shard_map/ppermute | solution.py:476
  77.6 3.6 %collective-permute-done.9.refs_3_ = f32[2,128,512]{2,1,0:T(8,128)S(1)} collective-permute-done((f32[2,128,512]{2,1,0:T(8,128)S(1)}, f32[2,128,512]{2,1,0:T(8,128)S(1)}, u32[]{:S(2)}, u32[]{:S(2)}) %collective-permute-start.9) | collective-permute-done | bytes 524320 | tf_op jit(solution)/shard_map/ppermute | solution.py:476
  81.1 1.0 shard_map.109
  82.1 6.3 %collective-permute-done.6.refs_2_ = f32[2,128,512]{2,1,0:T(8,128)S(1)} collective-permute-done((f32[2,128,512]{2,1,0:T(8,128)S(1)}, f32[2,128,512]{2,1,0:T(8,128)S(1)}, u32[]{:S(2)}, u32[]{:S(2)}) %collective-permute-start.6) | collective-permute-done | bytes 524320 | tf_op jit(solution)/shard_map/ppermute | solution.py:476
  88.4 2.2 %collective-permute-done.7.refs_3_ = f32[2,128,512]{2,1,0:T(8,128)S(1)} collective-permute-done((f32[2,128,512]{2,1,0:T(8,128)S(1)}, f32[2,128,512]{2,1,0:T(8,128)S(1)}, u32[]{:S(2)}, u32[]{:S(2)}) %collective-permute-start.7) | collective-permute-done | bytes 524320 | tf_op jit(solution)/shard_map/ppermute | solution.py:476
  90.6 0.9 shard_map.110
  91.5 0.5 collective-permute-start.20
  92.0 0.5 collective-permute-start.21
  92.5 3.3 %collective-permute-done.20.refs_1_ = f32[128,128]{1,0:T(8,128)S(1)} collective-permute-done((f32[128,128]{1,0:T(8,128)S(1)}, f32[128,128]{1,0:T(8,128)S(1)}, u32[]{:S(2)}, u32[]{:S(2)}) %collective-permute-start.20) | collective-permute-done | bytes 65568 | tf_op jit(solution)/shard_map/ppermute | solution.py:476
  95.8 0.5 collective-permute-done.21.refs_2_
  96.3 4.0 %collective-permute-start.32 = (f32[128,256]{1,0:T(8,128)S(1)}, f32[128,256]{1,0:T(8,128)S(1)}, u32[]{:S(2)}, u32[]{:S(2)}) collective-permute-start(f32[128,256]{1,0:T(8,128)S(1)} %shard_map.111.refs_1_.refs_0_), channel_id=1, source_target_pairs={{0,24},{8,16},{16,8},{24,0},{1,25},{9,17},{17,9},{25,1},{2,26},{10... | collective-permute-start | bytes 393224 | tf_op jit(solution)/shard_map/ppermute | solution.py:476
  100.7 1.7 %collective-permute-start.28 = (f32[2,128,256]{2,1,0:T(8,128)S(1)}, f32[2,128,256]{2,1,0:T(8,128)S(1)}, u32[]{:S(2)}, u32[]{:S(2)}) collective-permute-start(f32[2,128,256]{2,1,0:T(8,128)S(1)} %get-tuple-element.90.refs_13_), channel_id=1, source_target_pairs={{0,4},{1,5},{2,6},{3,7},{4,0},{5,1},{6,2},{7,3},{8,12},{9,13},{10,... | collective-permute-start | bytes 786440 | tf_op jit(solution)/shard_map/ppermute | solution.py:476
  102.4 1.5 %collective-permute-start.27 = (f32[2,128,256]{2,1,0:T(8,128)S(1)}, f32[2,128,256]{2,1,0:T(8,128)S(1)}, u32[]{:S(2)}, u32[]{:S(2)}) collective-permute-start(f32[2,128,256]{2,1,0:T(8,128)S(1)} %get-tuple-element.108), channel_id=1, source_target_pairs={{0,2},{1,3},{2,0},{3,1},{4,6},{5,7},{6,4},{7,5},{8,10},{9,11},{10,... | collective-permute-start | bytes 786440 | tf_op jit(solution)/shard_map/ppermute | solution.py:476
  103.9 0.8 collective-permute-done.32.refs_3_
  104.7 1.5 %collective-permute-start.30 = (f32[128,256]{1,0:T(8,128)S(1)}, f32[128,256]{1,0:T(8,128)S(1)}, u32[]{:S(2)}, u32[]{:S(2)}) collective-permute-start(f32[128,256]{1,0:T(8,128)S(1)} %shard_map.111.refs_1_.refs_0_), channel_id=1, source_target_pairs={{0,8},{8,0},{16,24},{24,16},{1,9},{9,1},{17,25},{25,17},{2,10},{10... | collective-permute-start | bytes 393224 | tf_op jit(solution)/shard_map/ppermute | solution.py:476
  106.2 4.0 %collective-permute-done.31.refs_2_ = f32[128,256]{1,0:T(8,128)S(1)} collective-permute-done((f32[128,256]{1,0:T(8,128)S(1)}, f32[128,256]{1,0:T(8,128)S(1)}, u32[]{:S(2)}, u32[]{:S(2)}) %collective-permute-start.31) | collective-permute-done | bytes 131104 | tf_op jit(solution)/shard_map/ppermute | solution.py:476
  110.2 0.6 collective-permute-start.24
  111.1 1.7 %collective-permute-start.26 = (f32[2,128,256]{2,1,0:T(8,128)S(1)}, f32[2,128,256]{2,1,0:T(8,128)S(1)}, u32[]{:S(2)}, u32[]{:S(2)}) collective-permute-start(f32[2,128,256]{2,1,0:T(8,128)S(1)} %get-tuple-element.95.refs_11_), channel_id=1, source_target_pairs={{0,4},{1,5},{2,6},{3,7},{4,0},{5,1},{6,2},{7,3},{8,12},{9,13},{10,... | collective-permute-start | bytes 786440 | tf_op jit(solution)/shard_map/ppermute | solution.py:476
  112.8 0.5 collective-permute-start.25
  113.4 1.7 %collective-permute-start.23 = (f32[1,128,512]{2,1,0:T(8,128)S(1)}, f32[1,128,512]{2,1,0:T(8,128)S(1)}, u32[]{:S(2)}, u32[]{:S(2)}) collective-permute-start(f32[1,128,512]{2,1,0:T(8,128)S(1)} %get-tuple-element.106), channel_id=1, source_target_pairs={{0,2},{1,3},{2,0},{3,1},{4,6},{5,7},{6,4},{7,5},{8,10},{9,11},{10,... | collective-permute-start | bytes 786440 | tf_op jit(solution)/shard_map/ppermute | solution.py:476
  115.2 0.9 shard_map.112.refs_0_.refs_6_
  116.1 1.9 %shard_map.117 = f32[512,1024]{1,0:T(8,128)} custom-call(f32[128,256]{1,0:T(8,128)S(1)} %shard_map.111.refs_1_.refs_0_, f32[128,256]{1,0:T(8,128)S(1)} %collective-permute-done.30.refs_1_, f32[128,256]{1,0:T(8,128)S(1)} %collective-permute-done.31.refs_2_, f32[128,256]{1,0:T(8,128)S(1)} %collective-permute-done.32.refs_3_, bf16[128,96]{1,0:T(8,128)(2,1)S(1)} %copy-done.4, ...), custom_call_target="tpu_custom_call" | custom-call | flops 402653184 | bytes 2097152 | tf_op jit(solution)/shard_map/pallas_call | solution.py:388
  118.0 0.9 shard_map.113.refs_3_
  118.8 5.6 %collective-permute-done.26.refs_1_ = f32[2,128,256]{2,1,0:T(8,128)S(1)} collective-permute-done((f32[2,128,256]{2,1,0:T(8,128)S(1)}, f32[2,128,256]{2,1,0:T(8,128)S(1)}, u32[]{:S(2)}, u32[]{:S(2)}) %collective-permute-start.26) | collective-permute-done | bytes 262176 | tf_op jit(solution)/shard_map/ppermute | solution.py:476
  124.4 0.8 shard_map.114.refs_3_
  125.3 0.8 shard_map.115.refs_3_
  126.2 1.1 collective-permute-done.22.refs_1_
  127.3 0.8 shard_map.116
  (46 shorter events, 2.7 us)
Async XLA Ops:
  9.4 2.1 %collective-permute-start = (f32[2,128,512]{2,1,0:T(8,128)S(1)}, f32[2,128,512]{2,1,0:T(8,128)S(1)}, u32[]{:S(2)}, u32[]{:S(2)}) collective-permute-start(f32[2,128,512]{2,1,0:T(8,128)S(1)} %get-tuple-element.60.refs_2_), channel_id=1, source_target_pairs={{0,1},{1,0},{2,3},{3,2},{4,5},{5,4},{6,7},{7,6},{8,9},{9,8},{10,11... | collective-permute-start | bytes 1572872 | tf_op jit(solution)/shard_map/ppermute | solution.py:476
  11.4 3.0 %collective-permute-start.1 = (f32[2,128,512]{2,1,0:T(8,128)S(1)}, f32[2,128,512]{2,1,0:T(8,128)S(1)}, u32[]{:S(2)}, u32[]{:S(2)}) collective-permute-start(f32[2,128,512]{2,1,0:T(8,128)S(1)} %shard_map.87.refs_2_), channel_id=1, source_target_pairs={{0,1},{1,0},{2,3},{3,2},{4,5},{5,4},{6,7},{7,6},{8,9},{9,8},{10,11... | collective-permute-start | bytes 1572872 | tf_op jit(solution)/shard_map/ppermute | solution.py:476
  13.8 3.0 %collective-permute-start.2 = (f32[2,128,512]{2,1,0:T(8,128)S(1)}, f32[2,128,512]{2,1,0:T(8,128)S(1)}, u32[]{:S(2)}, u32[]{:S(2)}) collective-permute-start(f32[2,128,512]{2,1,0:T(8,128)S(1)} %get-tuple-element.63.refs_2_), channel_id=1, source_target_pairs={{0,1},{1,0},{2,3},{3,2},{4,5},{5,4},{6,7},{7,6},{8,9},{9,8},{10,11... | collective-permute-start | bytes 1572872 | tf_op jit(solution)/shard_map/ppermute | solution.py:476
  16.7 4.4 %collective-permute-start.3 = (f32[2,128,512]{2,1,0:T(8,128)S(1)}, f32[2,128,512]{2,1,0:T(8,128)S(1)}, u32[]{:S(2)}, u32[]{:S(2)}) collective-permute-start(f32[2,128,512]{2,1,0:T(8,128)S(1)} %shard_map.93.refs_2_), channel_id=1, source_target_pairs={{0,1},{1,0},{2,3},{3,2},{4,5},{5,4},{6,7},{7,6},{8,9},{9,8},{10,11... | collective-permute-start | bytes 1572872 | tf_op jit(solution)/shard_map/ppermute | solution.py:476
  20.6 6.7 %collective-permute-start.4 = (f32[4,128,1024]{2,1,0:T(8,128)S(1)}, f32[4,128,1024]{2,1,0:T(8,128)S(1)}, u32[]{:S(2)}, u32[]{:S(2)}) collective-permute-start(f32[4,128,1024]{2,1,0:T(8,128)S(1)} %get-tuple-element.69.refs_2_), channel_id=1, source_target_pairs={{0,1},{1,0},{2,3},{3,2},{4,5},{5,4},{6,7},{7,6},{8,9},{9,8},{10,11... | collective-permute-start | bytes 6291464 | tf_op jit(solution)/shard_map/ppermute | solution.py:476
  27.3 4.2 %collective-permute-start.5 = (f32[4,128,1024]{2,1,0:T(8,128)S(1)}, f32[4,128,1024]{2,1,0:T(8,128)S(1)}, u32[]{:S(2)}, u32[]{:S(2)}) collective-permute-start(f32[4,128,1024]{2,1,0:T(8,128)S(1)} %get-tuple-element.72.refs_2_), channel_id=1, source_target_pairs={{0,1},{1,0},{2,3},{3,2},{4,5},{5,4},{6,7},{7,6},{8,9},{9,8},{10,11... | collective-permute-start | bytes 6291464 | tf_op jit(solution)/shard_map/ppermute | solution.py:476
  34.9 33.8 %collective-permute-start.15 = (f32[2,128,1024]{2,1,0:T(8,128)S(1)}, f32[2,128,1024]{2,1,0:T(8,128)S(1)}, u32[]{:S(2)}, u32[]{:S(2)}) collective-permute-start(f32[2,128,1024]{2,1,0:T(8,128)S(1)} %get-tuple-element.78.refs_4_), channel_id=1, source_target_pairs={{0,1},{1,0},{2,3},{3,2},{4,5},{5,4},{6,7},{7,6},{8,9},{9,8},{10,11... | collective-permute-start | bytes 3145736 | tf_op jit(solution)/shard_map/ppermute | solution.py:476
  35.0 11.5 %collective-permute-start.16 = (f32[2,128,256]{2,1,0:T(8,128)S(1)}, f32[2,128,256]{2,1,0:T(8,128)S(1)}, u32[]{:S(2)}, u32[]{:S(2)}) collective-permute-start(f32[2,128,256]{2,1,0:T(8,128)S(1)} %get-tuple-element.84), channel_id=1, source_target_pairs={{0,2},{1,3},{2,0},{3,1},{4,6},{5,7},{6,4},{7,5},{8,10},{9,11},{10,... | collective-permute-start | bytes 786440 | tf_op jit(solution)/shard_map/ppermute | solution.py:476
  37.8 8.7 %collective-permute-start.18 = (f32[2,128,256]{2,1,0:T(8,128)S(1)}, f32[2,128,256]{2,1,0:T(8,128)S(1)}, u32[]{:S(2)}, u32[]{:S(2)}) collective-permute-start(f32[2,128,256]{2,1,0:T(8,128)S(1)} %get-tuple-element.62.refs_2_), channel_id=1, source_target_pairs={{0,4},{1,5},{2,6},{3,7},{4,0},{5,1},{6,2},{7,3},{8,12},{9,13},{10,... | collective-permute-start | bytes 786440 | tf_op jit(solution)/shard_map/ppermute | solution.py:476
  45.9 27.4 %collective-permute-start.10 = (f32[2,128,1024]{2,1,0:T(8,128)S(1)}, f32[2,128,1024]{2,1,0:T(8,128)S(1)}, u32[]{:S(2)}, u32[]{:S(2)}) collective-permute-start(f32[2,128,1024]{2,1,0:T(8,128)S(1)} %get-tuple-element.80.refs_4_), channel_id=1, source_target_pairs={{0,1},{1,0},{2,3},{3,2},{4,5},{5,4},{6,7},{7,6},{8,9},{9,8},{10,11... | collective-permute-start | bytes 3145736 | tf_op jit(solution)/shard_map/ppermute | solution.py:476
  45.9 9.2 %collective-permute-start.17 = (f32[2,128,256]{2,1,0:T(8,128)S(1)}, f32[2,128,256]{2,1,0:T(8,128)S(1)}, u32[]{:S(2)}, u32[]{:S(2)}) collective-permute-start(f32[2,128,256]{2,1,0:T(8,128)S(1)} %get-tuple-element.85), channel_id=1, source_target_pairs={{0,2},{1,3},{2,0},{3,1},{4,6},{5,7},{6,4},{7,5},{8,10},{9,11},{10,... | collective-permute-start | bytes 786440 | tf_op jit(solution)/shard_map/ppermute | solution.py:476
  46.5 9.1 %collective-permute-start.19 = (f32[2,128,256]{2,1,0:T(8,128)S(1)}, f32[2,128,256]{2,1,0:T(8,128)S(1)}, u32[]{:S(2)}, u32[]{:S(2)}) collective-permute-start(f32[2,128,256]{2,1,0:T(8,128)S(1)} %get-tuple-element.64.refs_4_), channel_id=1, source_target_pairs={{0,4},{1,5},{2,6},{3,7},{4,0},{5,1},{6,2},{7,3},{8,12},{9,13},{10,... | collective-permute-start | bytes 786440 | tf_op jit(solution)/shard_map/ppermute | solution.py:476
  46.5 14.2 %collective-permute-start.11 = (f32[2,128,256]{2,1,0:T(8,128)S(1)}, f32[2,128,256]{2,1,0:T(8,128)S(1)}, u32[]{:S(2)}, u32[]{:S(2)}) collective-permute-start(f32[2,128,256]{2,1,0:T(8,128)S(1)} %get-tuple-element.82), channel_id=1, source_target_pairs={{0,2},{1,3},{2,0},{3,1},{4,6},{5,7},{6,4},{7,5},{8,10},{9,11},{10,... | collective-permute-start | bytes 786440 | tf_op jit(solution)/shard_map/ppermute | solution.py:476
  55.1 7.4 %collective-permute-start.13 = (f32[2,128,256]{2,1,0:T(8,128)S(1)}, f32[2,128,256]{2,1,0:T(8,128)S(1)}, u32[]{:S(2)}, u32[]{:S(2)}) collective-permute-start(f32[2,128,256]{2,1,0:T(8,128)S(1)} %get-tuple-element.68.refs_2_), channel_id=1, source_target_pairs={{0,4},{1,5},{2,6},{3,7},{4,0},{5,1},{6,2},{7,3},{8,12},{9,13},{10,... | collective-permute-start | bytes 786440 | tf_op jit(solution)/shard_map/ppermute | solution.py:476
  55.6 10.7 %collective-permute-start.12 = (f32[2,128,256]{2,1,0:T(8,128)S(1)}, f32[2,128,256]{2,1,0:T(8,128)S(1)}, u32[]{:S(2)}, u32[]{:S(2)}) collective-permute-start(f32[2,128,256]{2,1,0:T(8,128)S(1)} %get-tuple-element.83), channel_id=1, source_target_pairs={{0,2},{1,3},{2,0},{3,1},{4,6},{5,7},{6,4},{7,5},{8,10},{9,11},{10,... | collective-permute-start | bytes 786440 | tf_op jit(solution)/shard_map/ppermute | solution.py:476
  60.7 7.4 %collective-permute-start.14 = (f32[2,128,256]{2,1,0:T(8,128)S(1)}, f32[2,128,256]{2,1,0:T(8,128)S(1)}, u32[]{:S(2)}, u32[]{:S(2)}) collective-permute-start(f32[2,128,256]{2,1,0:T(8,128)S(1)} %get-tuple-element.70.refs_4_), channel_id=1, source_target_pairs={{0,4},{1,5},{2,6},{3,7},{4,0},{5,1},{6,2},{7,3},{8,12},{9,13},{10,... | collective-permute-start | bytes 786440 | tf_op jit(solution)/shard_map/ppermute | solution.py:476
  62.5 15.1 %collective-permute-start.8 = (f32[2,128,512]{2,1,0:T(8,128)S(1)}, f32[2,128,512]{2,1,0:T(8,128)S(1)}, u32[]{:S(2)}, u32[]{:S(2)}) collective-permute-start(f32[2,128,512]{2,1,0:T(8,128)S(1)} %get-tuple-element.77), channel_id=1, source_target_pairs={{0,2},{1,3},{2,0},{3,1},{4,6},{5,7},{6,4},{7,5},{8,10},{9,11},{10,... | collective-permute-start | bytes 1572872 | tf_op jit(solution)/shard_map/ppermute | solution.py:476
  66.4 14.8 %collective-permute-start.9 = (f32[2,128,512]{2,1,0:T(8,128)S(1)}, f32[2,128,512]{2,1,0:T(8,128)S(1)}, u32[]{:S(2)}, u32[]{:S(2)}) collective-permute-start(f32[2,128,512]{2,1,0:T(8,128)S(1)} %get-tuple-element.73.refs_4_), channel_id=1, source_target_pairs={{0,4},{1,5},{2,6},{3,7},{4,0},{5,1},{6,2},{7,3},{8,12},{9,13},{10,... | collective-permute-start | bytes 1572872 | tf_op jit(solution)/shard_map/ppermute | solution.py:476
  68.1 4.3 %copy-start = (f32[1,512,1024]{2,1,0:T(8,128)S(1)}, f32[1,512,1024]{2,1,0:T(8,128)}, u32[]{:S(2)}) copy-start(f32[1,512,1024]{2,1,0:T(8,128)} %refs_4_.3) | copy-start | bytes 6291460
  68.1 4.3 %copy-start.1 = (bf16[768,64]{1,0:T(8,128)(2,1)S(1)}, bf16[768,64]{1,0:T(8,128)(2,1)}, u32[]{:S(2)}) copy-start(bf16[768,64]{1,0:T(8,128)(2,1)} %constant.28.refs_8_.refs_6_) | copy-start | bytes 294916
  68.1 4.3 %copy-start.3 = (bf16[32,384]{1,0:T(8,128)(2,1)S(1)}, bf16[32,384]{1,0:T(8,128)(2,1)}, u32[]{:S(2)}) copy-start(bf16[32,384]{1,0:T(8,128)(2,1)} %constant.23.refs_7_.refs_5_) | copy-start | bytes 73732
  68.1 20.2 %collective-permute-start.6 = (f32[2,128,512]{2,1,0:T(8,128)S(1)}, f32[2,128,512]{2,1,0:T(8,128)S(1)}, u32[]{:S(2)}, u32[]{:S(2)}) collective-permute-start(f32[2,128,512]{2,1,0:T(8,128)S(1)} %get-tuple-element.75), channel_id=1, source_target_pairs={{0,2},{1,3},{2,0},{3,1},{4,6},{5,7},{6,4},{7,5},{8,10},{9,11},{10,... | collective-permute-start | bytes 1572872 | tf_op jit(solution)/shard_map/ppermute | solution.py:476
  68.7 21.9 %collective-permute-start.7 = (f32[2,128,512]{2,1,0:T(8,128)S(1)}, f32[2,128,512]{2,1,0:T(8,128)S(1)}, u32[]{:S(2)}, u32[]{:S(2)}) collective-permute-start(f32[2,128,512]{2,1,0:T(8,128)S(1)} %get-tuple-element.76.refs_4_), channel_id=1, source_target_pairs={{0,4},{1,5},{2,6},{3,7},{4,0},{5,1},{6,2},{7,3},{8,12},{9,13},{10,... | collective-permute-start | bytes 1572872 | tf_op jit(solution)/shard_map/ppermute | solution.py:476
  90.6 24.6 %copy-start.2 = (bf16[192,256]{1,0:T(8,128)(2,1)S(1)}, bf16[192,256]{1,0:T(8,128)(2,1)}, u32[]{:S(2)}) copy-start(bf16[192,256]{1,0:T(8,128)(2,1)} %constant.38.refs_3_.refs_5_) | copy-start | bytes 294916
  90.6 24.6 %copy-start.4 = (bf16[128,96]{1,0:T(8,128)(2,1)S(1)}, bf16[128,96]{1,0:T(8,128)(2,1)}, u32[]{:S(2)}) copy-start(bf16[128,96]{1,0:T(8,128)(2,1)} %constant.33.refs_2_.refs_4_) | copy-start | bytes 73732
  91.5 4.3 %collective-permute-start.20 = (f32[128,128]{1,0:T(8,128)S(1)}, f32[128,128]{1,0:T(8,128)S(1)}, u32[]{:S(2)}, u32[]{:S(2)}) collective-permute-start(f32[128,128]{1,0:T(8,128)S(1)} %get-tuple-element.103), channel_id=1, source_target_pairs={{0,4},{1,5},{2,6},{3,7},{4,0},{5,1},{6,2},{7,3},{8,12},{9,13},{10,... | collective-permute-start | bytes 196616 | tf_op jit(solution)/shard_map/ppermute | solution.py:476
  92.0 4.3 %collective-permute-start.21 = (f32[128,128]{1,0:T(8,128)S(1)}, f32[128,128]{1,0:T(8,128)S(1)}, u32[]{:S(2)}, u32[]{:S(2)}) collective-permute-start(f32[128,128]{1,0:T(8,128)S(1)} %get-tuple-element.104), channel_id=1, source_target_pairs={{0,2},{1,3},{2,0},{3,1},{4,6},{5,7},{6,4},{7,5},{8,10},{9,11},{10,... | collective-permute-start | bytes 196616 | tf_op jit(solution)/shard_map/ppermute | solution.py:476
  96.3 8.4 %collective-permute-start.32 = (f32[128,256]{1,0:T(8,128)S(1)}, f32[128,256]{1,0:T(8,128)S(1)}, u32[]{:S(2)}, u32[]{:S(2)}) collective-permute-start(f32[128,256]{1,0:T(8,128)S(1)} %shard_map.111.refs_1_.refs_0_), channel_id=1, source_target_pairs={{0,24},{8,16},{16,8},{24,0},{1,25},{9,17},{17,9},{25,1},{2,26},{10... | collective-permute-start | bytes 393224 | tf_op jit(solution)/shard_map/ppermute | solution.py:476
  100.3 12.5 %collective-permute-start.29 = (f32[2,128,256]{2,1,0:T(8,128)S(1)}, f32[2,128,256]{2,1,0:T(8,128)S(1)}, u32[]{:S(2)}, u32[]{:S(2)}) collective-permute-start(f32[2,128,256]{2,1,0:T(8,128)S(1)} %get-tuple-element.109), channel_id=1, source_target_pairs={{0,2},{1,3},{2,0},{3,1},{4,6},{5,7},{6,4},{7,5},{8,10},{9,11},{10,... | collective-permute-start | bytes 786440 | tf_op jit(solution)/shard_map/ppermute | solution.py:476
  100.7 12.7 %collective-permute-start.28 = (f32[2,128,256]{2,1,0:T(8,128)S(1)}, f32[2,128,256]{2,1,0:T(8,128)S(1)}, u32[]{:S(2)}, u32[]{:S(2)}) collective-permute-start(f32[2,128,256]{2,1,0:T(8,128)S(1)} %get-tuple-element.90.refs_13_), channel_id=1, source_target_pairs={{0,4},{1,5},{2,6},{3,7},{4,0},{5,1},{6,2},{7,3},{8,12},{9,13},{10,... | collective-permute-start | bytes 786440 | tf_op jit(solution)/shard_map/ppermute | solution.py:476
  102.4 11.0 %collective-permute-start.27 = (f32[2,128,256]{2,1,0:T(8,128)S(1)}, f32[2,128,256]{2,1,0:T(8,128)S(1)}, u32[]{:S(2)}, u32[]{:S(2)}) collective-permute-start(f32[2,128,256]{2,1,0:T(8,128)S(1)} %get-tuple-element.108), channel_id=1, source_target_pairs={{0,2},{1,3},{2,0},{3,1},{4,6},{5,7},{6,4},{7,5},{8,10},{9,11},{10,... | collective-permute-start | bytes 786440 | tf_op jit(solution)/shard_map/ppermute | solution.py:476
  103.9 6.3 %collective-permute-start.31 = (f32[128,256]{1,0:T(8,128)S(1)}, f32[128,256]{1,0:T(8,128)S(1)}, u32[]{:S(2)}, u32[]{:S(2)}) collective-permute-start(f32[128,256]{1,0:T(8,128)S(1)} %shard_map.111.refs_1_.refs_0_), channel_id=1, source_target_pairs={{0,16},{8,24},{16,0},{24,8},{1,17},{9,25},{17,1},{25,9},{2,18},{10... | collective-permute-start | bytes 393224 | tf_op jit(solution)/shard_map/ppermute | solution.py:476
  104.7 6.4 %collective-permute-start.30 = (f32[128,256]{1,0:T(8,128)S(1)}, f32[128,256]{1,0:T(8,128)S(1)}, u32[]{:S(2)}, u32[]{:S(2)}) collective-permute-start(f32[128,256]{1,0:T(8,128)S(1)} %shard_map.111.refs_1_.refs_0_), channel_id=1, source_target_pairs={{0,8},{8,0},{16,24},{24,16},{1,9},{9,1},{17,25},{25,17},{2,10},{10... | collective-permute-start | bytes 393224 | tf_op jit(solution)/shard_map/ppermute | solution.py:476
  110.2 15.1 %collective-permute-start.24 = (f32[1,128,512]{2,1,0:T(8,128)S(1)}, f32[1,128,512]{2,1,0:T(8,128)S(1)}, u32[]{:S(2)}, u32[]{:S(2)}) collective-permute-start(f32[1,128,512]{2,1,0:T(8,128)S(1)} %get-tuple-element.100.refs_11_), channel_id=1, source_target_pairs={{0,4},{1,5},{2,6},{3,7},{4,0},{5,1},{6,2},{7,3},{8,12},{9,13},{10,... | collective-permute-start | bytes 786440 | tf_op jit(solution)/shard_map/ppermute | solution.py:476
  111.1 13.3 %collective-permute-start.26 = (f32[2,128,256]{2,1,0:T(8,128)S(1)}, f32[2,128,256]{2,1,0:T(8,128)S(1)}, u32[]{:S(2)}, u32[]{:S(2)}) collective-permute-start(f32[2,128,256]{2,1,0:T(8,128)S(1)} %get-tuple-element.95.refs_11_), channel_id=1, source_target_pairs={{0,4},{1,5},{2,6},{3,7},{4,0},{5,1},{6,2},{7,3},{8,12},{9,13},{10,... | collective-permute-start | bytes 786440 | tf_op jit(solution)/shard_map/ppermute | solution.py:476
  112.8 12.5 %collective-permute-start.25 = (f32[1,128,512]{2,1,0:T(8,128)S(1)}, f32[1,128,512]{2,1,0:T(8,128)S(1)}, u32[]{:S(2)}, u32[]{:S(2)}) collective-permute-start(f32[1,128,512]{2,1,0:T(8,128)S(1)} %get-tuple-element.107), channel_id=1, source_target_pairs={{0,2},{1,3},{2,0},{3,1},{4,6},{5,7},{6,4},{7,5},{8,10},{9,11},{10,... | collective-permute-start | bytes 786440 | tf_op jit(solution)/shard_map/ppermute | solution.py:476
  113.3 13.9 %collective-permute-start.22 = (f32[1,128,512]{2,1,0:T(8,128)S(1)}, f32[1,128,512]{2,1,0:T(8,128)S(1)}, u32[]{:S(2)}, u32[]{:S(2)}) collective-permute-start(f32[1,128,512]{2,1,0:T(8,128)S(1)} %get-tuple-element.105), channel_id=1, source_target_pairs={{0,4},{1,5},{2,6},{3,7},{4,0},{5,1},{6,2},{7,3},{8,12},{9,13},{10,... | collective-permute-start | bytes 786440 | tf_op jit(solution)/shard_map/ppermute | solution.py:476
  113.4 13.8 %collective-permute-start.23 = (f32[1,128,512]{2,1,0:T(8,128)S(1)}, f32[1,128,512]{2,1,0:T(8,128)S(1)}, u32[]{:S(2)}, u32[]{:S(2)}) collective-permute-start(f32[1,128,512]{2,1,0:T(8,128)S(1)} %get-tuple-element.106), channel_id=1, source_target_pairs={{0,2},{1,3},{2,0},{3,1},{4,6},{5,7},{6,4},{7,5},{8,10},{9,11},{10,... | collective-permute-start | bytes 786440 | tf_op jit(solution)/shard_map/ppermute | solution.py:476
